TPU v7x, 32 devices: a whole 2x2x4 slice. The times are simulated.
32 devices in a mesh: band: 8 (over y, x, core), slab: 4 (over z).
Axes of the slice: x: 2, y: 2, z: 4, core: 2. Of those that a mesh axis runs over, the one named last changes fastest.
Arguments:
- orbitals: float32 [16, 144, 5184], P('band', 'slab'), may hold values from -6 to 6
Outputs:
- exchange: float32 [16, 144, 5184], P('band', 'slab')
All inputs are finite; a program needn't handle non-finite values.
Results may differ from a plain program's by a relative error of at most 0.0001.
Values sent between devices are 32-bit elements; how exact they have to be, the bound alone decides.
No kernel may reach another device: no remote copies, remote signals or barrier semaphores. Data moves between devices by JAX's collectives and lax.ppermute only.
A program may use at most 384 MiB of HBM per device.

v0:
```python
import jax
import jax.numpy as jnp
from jax import lax
from jax.sharding import PartitionSpec as P

NY = 72
SWEEPS = 3
CYCLE = 2


centre_weight = 8.5


def from_behind(value, axis, steps):
    count = lax.axis_size(axis)
    pairs = [(source, (source + steps) % count) for source in range(count)]
    return lax.ppermute(value, axis, pairs)


def extended(cells, sides, width):
    for axis, dim in sides:
        count = lax.axis_size(axis)
        head = lax.slice_in_dim(cells, 0, width, axis=dim)
        tail = lax.slice_in_dim(cells, cells.shape[dim] - width, cells.shape[dim], axis=dim)
        cells = jnp.concatenate(
            [
                lax.ppermute(tail, axis, [(i, (i + 1) % count) for i in range(count)]),
                cells,
                lax.ppermute(head, axis, [((i + 1) % count, i) for i in range(count)]),
            ],
            axis=dim,
        )
    return cells


def along_x(field, step):
    return jnp.roll(field, -step * NY, axis=-1)


def along_y(field, step):
    column = jnp.arange(field.shape[-1]) % NY
    inside = jnp.roll(field, -step, axis=-1)
    if step > 0:
        wrapped = jnp.roll(field, NY - step, axis=-1)
        keep = column + step < NY
    else:
        wrapped = jnp.roll(field, -step - NY, axis=-1)
        keep = column + step >= 0
    return jnp.where(keep, inside, wrapped)


def plane_off(field):
    xpart = 16.0 * (along_x(field, -1) + along_x(field, 1)) - (
        along_x(field, -2) + along_x(field, 2)
    )
    ypart = 16.0 * (along_y(field, -1) + along_y(field, 1)) - (
        along_y(field, -2) + along_y(field, 2)
    )
    return xpart + ypart


def trim_off(field):
    depth = field.shape[-2]
    centre = field[..., 2 : depth - 2, :]
    zpart = 16.0 * (field[..., 1 : depth - 3, :] + field[..., 3 : depth - 1, :]) - (
        field[..., 0 : depth - 4, :] + field[..., 4:depth, :]
    )
    return (plane_off(centre) + zpart) / 12.0


def fetch(own, sign):
    blocks = []
    block = own
    for step in range(CYCLE):
        block = from_behind(block, "band", sign)
        blocks.append(block)
    return blocks


def per_device(orbitals):
    exchange = jnp.zeros(orbitals.shape, jnp.float32)
    received = fetch(orbitals, 1)
    for step in range(CYCLE):
        block_ext = received[step]
        firsts = orbitals[:, None]
        density = firsts * block_ext[None]
        field = density / centre_weight
        for sweep in range(1, SWEEPS):
            padded = extended(field, (("slab", 2),), 2)
            field = (density + trim_off(padded)) / centre_weight
        total = -jnp.sum(field * block_ext[None], axis=1)
        travel = -jnp.sum(field * firsts, axis=0)
        own_part, travel = (total, travel)
        exchange = exchange + own_part + from_behind(travel, "band", -(step + 1))
    return exchange


def solution(mesh):
    return jax.shard_map(
        per_device,
        mesh=mesh,
        in_specs=(P("band", "slab", None),),
        out_specs=P("band", "slab", None),
        check_vma=False,
    )
```

profile of v0, /device:TPU:0, one launch (start us, length us, event | category | flops | bytes accessed | tf_op | source)
XLA Modules:
  0.0 584.5 jit_solution(5995956760921183858)
XLA Ops:
  4.2 16.9 %collective-permute-done = f32[2,36,5184]{2,0,1:T(2,128)S(1)} collective-permute-done((f32[2,36,5184]{2,0,1:T(2,128)}, f32[2,36,5184]{2,0,1:T(2,128)S(1)}, u32[]{:S(2)}, u32[]{:S(2)}) %collective-permute-start) | collective-permute-done | bytes 1493024 | tf_op jit(solution)/shard_map/ppermute | solution.py:17
  23.7 17.5 %collective-permute-done.6 = f32[2,36,5184]{2,0,1:T(2,128)S(1)} collective-permute-done((f32[2,36,5184]{2,0,1:T(2,128)S(1)}, f32[2,36,5184]{2,0,1:T(2,128)S(1)}, u32[]{:S(2)}, u32[]{:S(2)}) %collective-permute-start.6) | collective-permute-done | bytes 1493024 | tf_op jit(solution)/shard_map/ppermute | solution.py:17
  41.2 3.2 multiply_multiply_fusion.1
  49.0 10.5 %fusion.85 = (f32[2,2,36,5114]{3,1,2,0:T(2,128)}, f32[2,2,36,5114]{3,1,2,0:T(2,128)}, f32[2,2,36,5114]{3,1,2,0:T(2,128)}, f32[2,2,36,5114]{3,1,2,0:T(2,128)}) fusion(f32[2,2,36,5184]{3,1,2,0:T(2,128)S(1)} %get-tuple-element.115, f32[2,2,36,5184]{3,1,2,0:T(2,128)S(1)} %get-tuple-element.116), kind=kLoop, calls=%fused_computation.154 | loop fusion | bytes 23565312 | tf_op jit(solution)/shard_map/jit(_roll_static)/slice | solution.py:47
  59.5 10.4 %fusion.81 = (f32[2,2,36,5113]{3,1,2,0:T(2,128)}, f32[2,2,36,5113]{3,1,2,0:T(2,128)}, f32[2,2,36,5113]{3,1,2,0:T(2,128)}, f32[2,2,36,5113]{3,1,2,0:T(2,128)}) fusion(f32[2,2,36,5184]{3,1,2,0:T(2,128)S(1)} %get-tuple-element.115, f32[2,2,36,5184]{3,1,2,0:T(2,128)S(1)} %get-tuple-element.116), kind=kLoop, calls=%fused_computation.150 | loop fusion | bytes 23560704 | tf_op jit(solution)/shard_map/jit(_roll_static)/slice | solution.py:47
  69.9 10.2 %fusion.78 = (f32[2,2,36,5040]{3,1,2,0:T(2,128)}, f32[2,2,36,5040]{3,1,2,0:T(2,128)}, f32[2,2,36,5040]{3,1,2,0:T(2,128)}, f32[2,2,36,5040]{3,1,2,0:T(2,128)}) fusion(f32[2,2,36,5184]{3,1,2,0:T(2,128)S(1)} %get-tuple-element.115, f32[2,2,36,5184]{3,1,2,0:T(2,128)S(1)} %get-tuple-element.116), kind=kLoop, calls=%fused_computation.147 | loop fusion | bytes 23224320 | tf_op jit(solution)/shard_map/jit(_roll_static)/slice | solution.py:37
  80.1 10.6 %fusion.76 = (f32[2,2,36,5112]{3,1,2,0:T(2,128)}, f32[2,2,36,5112]{3,1,2,0:T(2,128)}, f32[2,2,36,5112]{3,1,2,0:T(2,128)}, f32[2,2,36,5112]{3,1,2,0:T(2,128)}) fusion(f32[2,2,36,5184]{3,1,2,0:T(2,128)S(1)} %get-tuple-element.115, f32[2,2,36,5184]{3,1,2,0:T(2,128)S(1)} %get-tuple-element.116), kind=kLoop, calls=%fused_computation.145 | loop fusion | bytes 23556096 | tf_op jit(solution)/shard_map/jit(_roll_static)/slice | solution.py:37
  90.7 10.1 %fusion.80 = (f32[2,2,36,5183]{3,1,2,0:T(2,128)}, f32[2,2,36,5183]{3,1,2,0:T(2,128)}, f32[2,2,36,5183]{3,1,2,0:T(2,128)S(1)}, f32[2,2,36,5183]{3,1,2,0:T(2,128)S(1)}) fusion(f32[2,2,36,5184]{3,1,2,0:T(2,128)S(1)} %get-tuple-element.115, f32[2,2,36,5184]{3,1,2,0:T(2,128)S(1)} %get-tuple-element.116), kind=kLoop, calls=%fused_computation.149 | loop fusion | bytes 23883264 | tf_op jit(solution)/shard_map/jit(_roll_static)/slice | solution.py:42
  100.8 10.0 %fusion.84 = (f32[2,2,36,5182]{3,1,2,0:T(2,128)}, f32[2,2,36,5182]{3,1,2,0:T(2,128)}, f32[2,2,36,5182]{3,1,2,0:T(2,128)S(1)}, f32[2,2,36,5182]{3,1,2,0:T(2,128)}) fusion(f32[2,2,36,5184]{3,1,2,0:T(2,128)S(1)} %get-tuple-element.115, f32[2,2,36,5184]{3,1,2,0:T(2,128)S(1)} %get-tuple-element.116), kind=kLoop, calls=%fused_computation.153 | loop fusion | bytes 23878656 | tf_op jit(solution)/shard_map/jit(_roll_static)/slice | solution.py:42
  110.8 2.3 collective-permute-start.1
  115.0 3.8 collective-permute-start.8
  124.1 100.7 %fusion.24 = f32[2,2,36,5184]{3,1,2,0:T(2,128)S(1)} fusion(f32[2,2,2,5184]{3,1,2,0:T(2,128)} %copy-done.9, f32[2,2,36,5184]{3,1,2,0:T(2,128)S(1)} %get-tuple-element.115, f32[2,2,2,5184]{3,1,2,0:T(2,128)} %copy-done.8, f32[2,2,36,5114]{3,1,2,0:T(2,128)} %get-tuple-element.56, f32[2,2,36,70]{3,1,2,0:T(2,128)} %get-tuple-element.58, ...), kind=kLoop, calls=%fused_computation.46 | loop fusion | flops 28366848 | bytes 45142272 | tf_op jit(solution)/shard_map/div | solution.py:90
  228.7 99.6 %fusion.25 = f32[2,2,36,5184]{3,1,2,0:T(2,128)S(1)} fusion(f32[2,2,2,5184]{3,1,2,0:T(2,128)} %collective-permute-done.8, f32[2,2,36,5184]{3,1,2,0:T(2,128)S(1)} %get-tuple-element.116, f32[2,2,2,5184]{3,1,2,0:T(2,128)} %collective-permute-done.7, f32[2,2,36,5114]{3,1,2,0:T(2,128)} %get-tuple-element.137, f32[2,2,36,70]{3,1,2,0:T(2,128)S(1)} %get-tuple-element.139, ...), kind=kLoop, calls=%fused_computation.47 | loop fusion | flops 28366848 | bytes 45142272 | tf_op jit(solution)/shard_map/div | solution.py:90
  332.7 5.7 fusion.72
  338.4 5.7 fusion.68
  344.1 5.7 fusion.65
  349.8 6.0 %fusion.63 = (f32[2,2,36,5112]{3,1,2,0:T(2,128)}, f32[2,2,36,5112]{3,1,2,0:T(2,128)}) fusion(f32[2,2,36,5184]{3,1,2,0:T(2,128)S(1)} %fusion.24), kind=kLoop, calls=%fused_computation.132 | loop fusion | bytes 11778048 | tf_op jit(solution)/shard_map/jit(_roll_static)/slice | solution.py:37
  355.8 5.7 fusion.98
  361.5 5.7 fusion.94
  367.2 6.0 %fusion.91 = (f32[2,2,36,5040]{3,1,2,0:T(2,128)}, f32[2,2,36,5040]{3,1,2,0:T(2,128)}) fusion(f32[2,2,36,5184]{3,1,2,0:T(2,128)S(1)} %fusion.25), kind=kLoop, calls=%fused_computation.160 | loop fusion | bytes 11612160 | tf_op jit(solution)/shard_map/jit(_roll_static)/slice | solution.py:37
  373.1 5.7 fusion.89
  378.9 5.9 %fusion.67 = (f32[2,2,36,5183]{3,1,2,0:T(2,128)}, f32[2,2,36,5183]{3,1,2,0:T(2,128)}) fusion(f32[2,2,36,5184]{3,1,2,0:T(2,128)S(1)} %fusion.24), kind=kLoop, calls=%fused_computation.136 | loop fusion | bytes 11941632 | tf_op jit(solution)/shard_map/jit(_roll_static)/slice | solution.py:42
  384.7 5.8 fusion.71
  390.5 6.3 %fusion.93 = (f32[2,2,36,5183]{3,1,2,0:T(2,128)}, f32[2,2,36,5183]{3,1,2,0:T(2,128)}) fusion(f32[2,2,36,5184]{3,1,2,0:T(2,128)S(1)} %fusion.25), kind=kLoop, calls=%fused_computation.162 | loop fusion | bytes 11941632 | tf_op jit(solution)/shard_map/jit(_roll_static)/slice | solution.py:42
  396.8 5.8 fusion.97
  403.9 2.5 collective-permute-start.4
  406.4 3.8 collective-permute-start.10
  411.2 3.4 collective-permute-done.9
  414.8 111.0 %multiply_reduce_fusion.3 = (f32[2,36,5184]{2,1,0:T(8,128)}, f32[2,36,5184]{2,0,1:T(2,128)}, f32[2,36,5184]{2,0,1:T(2,128)}, f32[2,36,5184]{2,1,0:T(8,128)}) fusion(f32[2,36,5184]{2,0,1:T(2,128)} %broadcast_multiply_fusion.2, f32[2,36,5184]{2,1,0:T(8,128)} %copy.14, f32[2,36,5184]{2,0,1:T(2,128)} %broadcast_multiply_fusion, ...), kind=kLoop, calls=%fused_computation.115 | loop fusion | flops 59719680 | bytes 93249792 | tf_op jit(solution)/shard_map/reduce_sum | solution.py:91
  528.7 5.6 collective-permute-start.11
  534.3 32.7 %collective-permute-done.11 = f32[2,36,5184]{2,0,1:T(2,128)S(1)} collective-permute-done((f32[2,36,5184]{2,0,1:T(2,128)S(1)}, f32[2,36,5184]{2,0,1:T(2,128)S(1)}, u32[]{:S(2)}, u32[]{:S(2)}) %collective-permute-start.11) | collective-permute-done | bytes 1493024 | tf_op jit(solution)/shard_map/ppermute | solution.py:17
  567.0 15.0 %collective-permute-done.5 = f32[2,36,5184]{2,0,1:T(2,128)S(1)} collective-permute-done((f32[2,36,5184]{2,0,1:T(2,128)S(1)}, f32[2,36,5184]{2,0,1:T(2,128)S(1)}, u32[]{:S(2)}, u32[]{:S(2)}) %collective-permute-start.5) | collective-permute-done | bytes 1493024 | tf_op jit(solution)/shard_map/ppermute | solution.py:17
  (67 shorter events, 34.5 us)
Async XLA Ops:
  0.0 2.0 copy-start.7
  0.0 21.1 %collective-permute-start = (f32[2,36,5184]{2,0,1:T(2,128)}, f32[2,36,5184]{2,0,1:T(2,128)S(1)}, u32[]{:S(2)}, u32[]{:S(2)}) collective-permute-start(f32[2,36,5184]{2,0,1:T(2,128)} %param.1), channel_id=1, source_target_pairs={{0,4},{4,8},{8,12},{12,16},{16,20},{20,24},{24,28},{28,0},{1,5},{5... | collective-permute-start | bytes 4478984 | tf_op jit(solution)/shard_map/ppermute | solution.py:17
  2.0 226.7 %copy-start.1 = (f32[2,36,5184]{2,1,0:T(8,128)}, f32[2,36,5184]{2,1,0:T(8,128)S(1)}, u32[]{:S(2)}) copy-start(f32[2,36,5184]{2,1,0:T(8,128)S(1)} %copy.13) | copy-start | bytes 4478980
  21.1 103.0 %copy-start.2 = (f32[2,36,5184]{2,0,1:T(2,128)}, f32[2,36,5184]{2,0,1:T(2,128)S(1)}, u32[]{:S(2)}) copy-start(f32[2,36,5184]{2,0,1:T(2,128)S(1)} %collective-permute-done) | copy-start | bytes 4478980
  21.1 20.1 %collective-permute-start.6 = (f32[2,36,5184]{2,0,1:T(2,128)S(1)}, f32[2,36,5184]{2,0,1:T(2,128)S(1)}, u32[]{:S(2)}, u32[]{:S(2)}) collective-permute-start(f32[2,36,5184]{2,0,1:T(2,128)S(1)} %collective-permute-done), channel_id=1, source_target_pairs={{0,4},{4,8},{8,12},{12,16},{16,20},{20,24},{24,28},{28,0},{1,5},{5... | collective-permute-start | bytes 4478984 | tf_op jit(solution)/shard_map/ppermute | solution.py:17
  41.2 187.5 %copy-start.3 = (f32[2,36,5184]{2,0,1:T(2,128)}, f32[2,36,5184]{2,0,1:T(2,128)S(1)}, u32[]{:S(2)}) copy-start(f32[2,36,5184]{2,0,1:T(2,128)S(1)} %collective-permute-done.6) | copy-start | bytes 4478980
  110.8 11.0 %collective-permute-start.1 = (f32[2,2,2,5184]{3,1,2,0:T(2,128)S(1)}, f32[2,2,2,5184]{3,1,2,0:T(2,128)S(1)}, u32[]{:S(2)}, u32[]{:S(2)}) collective-permute-start(f32[2,2,2,5184]{3,1,2,0:T(2,128)S(1)} %get-tuple-element.59), channel_id=1, source_target_pairs={{0,1},{1,2},{2,3},{3,0},{4,5},{5,6},{6,7},{7,4},{8,9},{9,10},{10,1... | collective-permute-start | bytes 497672 | tf_op jit(solution)/shard_map/ppermute | solution.py:27
  113.0 10.4 %collective-permute-start.2 = (f32[2,2,2,5184]{3,1,2,0:T(2,128)S(1)}, f32[2,2,2,5184]{3,1,2,0:T(2,128)S(1)}, u32[]{:S(2)}, u32[]{:S(2)}) collective-permute-start(f32[2,2,2,5184]{3,1,2,0:T(2,128)S(1)} %get-tuple-element.60), channel_id=1, source_target_pairs={{1,0},{2,1},{3,2},{0,3},{5,4},{6,5},{7,6},{4,7},{9,8},{10,9},{11,1... | collective-permute-start | bytes 497672 | tf_op jit(solution)/shard_map/ppermute | solution.py:29
  115.0 113.7 %collective-permute-start.7 = (f32[2,2,2,5184]{3,1,2,0:T(2,128)}, f32[2,2,2,5184]{3,1,2,0:T(2,128)}, u32[]{:S(2)}, u32[]{:S(2)}) collective-permute-start(f32[2,2,2,5184]{3,1,2,0:T(2,128)} %get-tuple-element.111), channel_id=1, source_target_pairs={{0,1},{1,2},{2,3},{3,0},{4,5},{5,6},{6,7},{7,4},{8,9},{9,10},{10,1... | collective-permute-start | bytes 497672 | tf_op jit(solution)/shard_map/ppermute | solution.py:27
  115.0 113.7 %collective-permute-start.8 = (f32[2,2,2,5184]{3,1,2,0:T(2,128)}, f32[2,2,2,5184]{3,1,2,0:T(2,128)}, u32[]{:S(2)}, u32[]{:S(2)}) collective-permute-start(f32[2,2,2,5184]{3,1,2,0:T(2,128)} %get-tuple-element.112), channel_id=1, source_target_pairs={{1,0},{2,1},{3,2},{0,3},{5,4},{6,5},{7,6},{4,7},{9,8},{10,9},{11,1... | collective-permute-start | bytes 497672 | tf_op jit(solution)/shard_map/ppermute | solution.py:29
  121.7 1.7 copy-start.8
  123.5 0.7 copy-start.9
  328.3 82.0 %copy-start = (f32[2,2,36,5184]{3,1,2,0:T(2,128)}, f32[2,2,36,5184]{3,1,2,0:T(2,128)S(1)}, u32[]{:S(2)}) copy-start(f32[2,2,36,5184]{3,1,2,0:T(2,128)S(1)} %fusion.25) | copy-start | bytes 8957956
  402.6 8.4 %collective-permute-start.3 = (f32[2,2,2,5184]{3,1,2,0:T(2,128)S(1)}, f32[2,2,2,5184]{3,1,2,0:T(2,128)}, u32[]{:S(2)}, u32[]{:S(2)}) collective-permute-start(f32[2,2,2,5184]{3,1,2,0:T(2,128)S(1)} %get-tuple-element.33), channel_id=1, source_target_pairs={{0,1},{1,2},{2,3},{3,0},{4,5},{5,6},{6,7},{7,4},{8,9},{9,10},{10,1... | collective-permute-start | bytes 497672 | tf_op jit(solution)/shard_map/ppermute | solution.py:27
  403.9 7.3 %collective-permute-start.4 = (f32[2,2,2,5184]{3,1,2,0:T(2,128)S(1)}, f32[2,2,2,5184]{3,1,2,0:T(2,128)}, u32[]{:S(2)}, u32[]{:S(2)}) collective-permute-start(f32[2,2,2,5184]{3,1,2,0:T(2,128)S(1)} %get-tuple-element.34), channel_id=1, source_target_pairs={{1,0},{2,1},{3,2},{0,3},{5,4},{6,5},{7,6},{4,7},{9,8},{10,9},{11,1... | collective-permute-start | bytes 497672 | tf_op jit(solution)/shard_map/ppermute | solution.py:29
  406.4 8.2 %collective-permute-start.9 = (f32[2,2,2,5184]{3,1,2,0:T(2,128)S(1)}, f32[2,2,2,5184]{3,1,2,0:T(2,128)}, u32[]{:S(2)}, u32[]{:S(2)}) collective-permute-start(f32[2,2,2,5184]{3,1,2,0:T(2,128)S(1)} %get-tuple-element.85), channel_id=1, source_target_pairs={{0,1},{1,2},{2,3},{3,0},{4,5},{5,6},{6,7},{7,4},{8,9},{9,10},{10,1... | collective-permute-start | bytes 497672 | tf_op jit(solution)/shard_map/ppermute | solution.py:27
  406.4 8.4 %collective-permute-start.10 = (f32[2,2,2,5184]{3,1,2,0:T(2,128)S(1)}, f32[2,2,2,5184]{3,1,2,0:T(2,128)}, u32[]{:S(2)}, u32[]{:S(2)}) collective-permute-start(f32[2,2,2,5184]{3,1,2,0:T(2,128)S(1)} %get-tuple-element.86), channel_id=1, source_target_pairs={{1,0},{2,1},{3,2},{0,3},{5,4},{6,5},{7,6},{4,7},{9,8},{10,9},{11,1... | collective-permute-start | bytes 497672 | tf_op jit(solution)/shard_map/ppermute | solution.py:29
  525.8 2.2 copy-start.6
  525.8 56.1 %copy-start.4 = (f32[2,36,5184]{2,1,0:T(8,128)S(1)}, f32[2,36,5184]{2,1,0:T(8,128)}, u32[]{:S(2)}) copy-start(f32[2,36,5184]{2,1,0:T(8,128)} %get-tuple-element.5) | copy-start | bytes 4478980
  525.8 56.1 %copy-start.5 = (f32[2,36,5184]{2,1,0:T(8,128)S(1)}, f32[2,36,5184]{2,1,0:T(8,128)}, u32[]{:S(2)}) copy-start(f32[2,36,5184]{2,1,0:T(8,128)} %get-tuple-element.114) | copy-start | bytes 4478980
  528.7 38.3 %collective-permute-start.11 = (f32[2,36,5184]{2,0,1:T(2,128)S(1)}, f32[2,36,5184]{2,0,1:T(2,128)S(1)}, u32[]{:S(2)}, u32[]{:S(2)}) collective-permute-start(f32[2,36,5184]{2,0,1:T(2,128)S(1)} %neg.15), channel_id=1, source_target_pairs={{0,24},{4,28},{8,0},{12,4},{16,8},{20,12},{24,16},{28,20},{1,25},{... | collective-permute-start | bytes 4478984 | tf_op jit(solution)/shard_map/ppermute | solution.py:17
  534.3 47.7 %collective-permute-start.5 = (f32[2,36,5184]{2,0,1:T(2,128)S(1)}, f32[2,36,5184]{2,0,1:T(2,128)S(1)}, u32[]{:S(2)}, u32[]{:S(2)}) collective-permute-start(f32[2,36,5184]{2,0,1:T(2,128)S(1)} %neg.13), channel_id=1, source_target_pairs={{0,28},{4,0},{8,4},{12,8},{16,12},{20,16},{24,20},{28,24},{1,29},{... | collective-permute-start | bytes 4478984 | tf_op jit(solution)/shard_map/ppermute | solution.py:17
where the time goes:
time: 595 us; the launch traced here: 585 us
  other arithmetic  323 us (54%)
  local copies, waits for them, and re-layouts  152 us (26%)
  waiting for transfers between devices  87.6 us (15%)
  starting transfers between devices  21.8 us (4%)
    div x2, other arithmetic, per_device(): field = (density + trim_off(padded)) / centre_weight  200 us
    reduce_sum x1, other arithmetic, per_device(): total = -jnp.sum(field * block_ext[None], axis=1)  111 us
    ppermute x4, waiting for transfers between devices, from_behind(): return lax.ppermute(value, axis, pairs)  82.1 us
    slice x12, local copies, waits for them, and re-layouts, along_y(): wrapped = jnp.roll(field, -step - NY, axis=-1)  48.7 us
    slice x12, local copies, waits for them, and re-layouts, along_y(): inside = jnp.roll(field, -step, axis=-1)  48.5 us
    slice x12, local copies, waits for them, and re-layouts, along_x(): return jnp.roll(field, -step * NY, axis=-1)  48.1 us
    ppermute x4, starting transfers between devices, extended(): lax.ppermute(head, axis, [((i + 1) % count, i) for i in range(count)])  12.2 us
  transfers between devices with their start and end apart: 12, of which 8 were waited for; matrix products, arithmetic and copies ran while one was open for 20% of the time, Pallas kernels for 0%

commit v1 on v0

v1 whole, which is shorter than its diff:
```python
import functools

import jax
import jax.numpy as jnp
from jax import lax
from jax.experimental import pallas as pl
from jax.experimental.pallas import tpu as pltpu
from jax.sharding import PartitionSpec as P

NY = 72
LANES = 128
REACH = 2
HALO = 4
CENTRE = 8.5
ALPHA = 1.0 / (12.0 * CENTRE)
VMEM = pl.BlockSpec(memory_space=pltpu.VMEM)
SMEM = pl.BlockSpec(memory_space=pltpu.SMEM)


def params(limit=None):
    return pltpu.CompilerParams(vmem_limit_bytes=limit)


def sds(*shape):
    return jax.ShapeDtypeStruct(shape, jnp.float32)


def call(body, out, inputs, scratch=(), flops=0, smem=False, limit=None, name=None):
    nbytes = sum(4 * x.size for x in inputs) + sum(4 * o.size for o in out)
    specs = [VMEM] * len(inputs)
    if smem:
        specs[0] = SMEM
    return pl.pallas_call(
        body,
        out_shape=out,
        in_specs=specs,
        out_specs=[VMEM] * len(out),
        scratch_shapes=scratch,
        compiler_params=params(limit),
        cost_estimate=pl.CostEstimate(flops=flops, bytes_accessed=nbytes, transcendentals=0),
        name=name,
    )(*inputs)


def pack_body(chips, width, n_in, *refs):
    chip_ref, ins, outs = refs[0], refs[1 : 1 + n_in], refs[1 + n_in :]
    chip = chip_ref[0]
    total = ins[0].shape[2]
    span = (width + 2 * HALO) * NY
    for ahead in range(chips):
        for target in range(chips):

            @pl.when(lax.rem(chip + ahead, chips) == target)
            def _(ahead=ahead, target=target):
                start = (target * width - HALO) * NY
                row = 0
                for ref in ins:
                    rows = ref.shape[1]
                    for orb in range(ref.shape[0]):
                        lo, hi = start, start + span
                        if lo < 0:
                            value = jnp.concatenate(
                                [ref[orb, :, lo + total : total], ref[orb, :, 0:hi]], axis=-1
                            )
                        elif hi > total:
                            value = jnp.concatenate(
                                [ref[orb, :, lo:total], ref[orb, :, 0 : hi - total]], axis=-1
                            )
                        else:
                            value = ref[orb, :, lo:hi]
                        outs[ahead][orb, row : row + rows, :] = value
                    row += rows


def pack(chip, pieces, chips, width):
    orbs = pieces[0].shape[0]
    rows = sum(p.shape[1] for p in pieces)
    span = (width + 2 * HALO) * NY
    return call(
        functools.partial(pack_body, chips, width, len(pieces)),
        [sds(orbs, rows, span)] * chips,
        [chip, *pieces],
        smem=True,
        name="pack",
    )


def gather_body(chips, *refs):
    main, edge, out = refs[:chips], refs[chips : 2 * chips], refs[2 * chips]
    orbs, depth, span = main[0].shape

    def move(sources, lo, hi, at):
        for a in range(0, span, LANES):
            b = min(a + LANES, span)
            value = jnp.concatenate([ref[:, lo:hi, a:b] for ref in sources], axis=0)
            out[at : at + hi - lo, :, a:b] = jnp.swapaxes(value, 0, 1)

    move(edge, 0, HALO, 0)
    for z in range(0, depth, 8):
        move(main, z, min(z + 8, depth), HALO + z)
    move(edge, HALO, 2 * HALO, HALO + depth)


def gather(main, edge):
    orbs, depth, span = main[0].shape
    chips = len(main)
    return call(
        functools.partial(gather_body, chips),
        [sds(depth + 2 * HALO, orbs * chips, span)],
        [*main, *edge],
        name="gather",
    )[0]


def lane_iota(rows):
    return lax.broadcasted_iota(jnp.int32, (rows, LANES), 1)


def row_iota(rows):
    return lax.broadcasted_iota(jnp.int32, (rows, LANES), 0)


def roll_rows(value, shift):
    return pltpu.roll(value, shift % value.shape[0], 0)


def roll_lanes(value, shift):
    return pltpu.roll(value, shift % LANES, 1)


def unpack(flat_ref, out_ref, change=None):
    depth, rows, span = flat_ref.shape
    lane = lane_iota(rows)

    def plane(z, _):
        for col in range(span // NY):
            tile, offset = divmod(col * NY, LANES)
            tile *= LANES
            end = min(tile + LANES, span)
            head = flat_ref[z, :, tile:end]
            if end - tile < LANES:
                head = jnp.concatenate(
                    [head, jnp.zeros((rows, LANES - (end - tile)), jnp.float32)], axis=-1
                )
            value = roll_lanes(head, -offset) if offset else head
            if offset + NY > LANES:
                stop = min(tile + 2 * LANES, span)
                tail = flat_ref[z, :, tile + LANES : stop]
                if stop - tile - LANES < LANES:
                    pad = 2 * LANES - (stop - tile)
                    tail = jnp.concatenate(
                        [tail, jnp.zeros((rows, pad), jnp.float32)], axis=-1
                    )
                value = jnp.where(lane < LANES - offset, value, roll_lanes(tail, -offset))
            if change is not None:
                value = change(value)
            after = roll_lanes(value, NY)
            before = roll_lanes(value, LANES - NY)
            value = jnp.where(
                lane < NY,
                value,
                jnp.where(
                    lane < NY + HALO, after, jnp.where(lane >= LANES - HALO, before, 0.0)
                ),
            )
            out_ref[z, col] = value
        return 0

    lax.fori_loop(0, depth, plane, 0)


def repack(tiles, out_ref, z):
    rows = tiles[0].shape[0]
    lane = lane_iota(rows)
    span = len(tiles) * NY
    for start in range(0, span, LANES):
        stop = min(start + LANES, span)
        value = None
        for col in range(start // NY, (stop - 1) // NY + 1):
            shift = col * NY - start
            part = roll_lanes(tiles[col], shift)
            if value is None:
                value = part
            else:
                value = jnp.where(lane < shift, value, part)
        out_ref[z, :, start:stop] = value[:, : stop - start]


def stencil(source, z, col, centre):
    c = col + REACH
    near = (centre[c - 1] + centre[c + 1]) + (source[z + 1, c] + source[z + 3, c])
    near = near + (roll_lanes(centre[c], 1) + roll_lanes(centre[c], -1))
    far = (centre[c - 2] + centre[c + 2]) + (source[z, c] + source[z + 4, c])
    far = far + (roll_lanes(centre[c], 2) + roll_lanes(centre[c], -2))
    return 16.0 * near - far


def potentials(first, partner, rho, field, finish):
    depth, cols = rho.shape[:2]

    def density(z, _):
        for col in range(cols):
            rho[z, col] = first[z, col] * partner[z, col]
        return 0

    lax.fori_loop(0, depth, density, 0)

    def sweep(z, _):
        centre = [rho[z + REACH, col] for col in range(cols)]
        for col in range(cols - 2 * REACH):
            field[z, col] = centre[col + REACH] + ALPHA * stencil(rho, z, col, centre)
        return 0

    lax.fori_loop(0, depth - 2 * REACH, sweep, 0)

    def last(z, _):
        centre = [field[z + REACH, col] for col in range(cols - 2 * REACH)]
        finish(
            z,
            [
                rho[z + HALO, col + HALO] + ALPHA * stencil(field, z, col, centre)
                for col in range(cols - 2 * HALO)
            ],
        )
        return 0

    lax.fori_loop(0, depth - 2 * HALO, last, 0)


def mixed(value, even, odd):
    rows = value.shape[0]
    return jnp.where(row_iota(rows) % 2 == 0, roll_rows(value, even), roll_rows(value, odd))


def same_body(swapped, final, *refs):
    if final:
        planes, acc_in, acc, partner, rho, field = refs
    else:
        flat, planes, acc, partner, rho, field = refs
        unpack(flat, planes)
    depth, cols, rows, _ = planes.shape

    def to_partner(value):
        return mixed(value, 1, 3) if swapped else roll_rows(value, 2)

    def from_partner(value):
        return mixed(value, -3, -1) if swapped else roll_rows(value, -2)

    def shift(z, _):
        for col in range(cols):
            partner[z, col] = to_partner(planes[z, col])
        return 0

    lax.fori_loop(0, depth, shift, 0)

    def finish(z, values):
        tiles = []
        for col, value in enumerate(values):
            own = value * partner[z + HALO, col + HALO]
            other = value * planes[z + HALO, col + HALO]
            total = own + from_partner(other)
            if final:
                tiles.append((total + acc_in[z, col]) * (-1.0 / CENTRE))
            else:
                acc[z, col] = total
        if final:
            repack(tiles, acc, z)

    potentials(planes, partner, rho, field, finish)


def cross_kernel(core_ref, planes, acc_in, flat, acc, travel, partner, rho, field, kept):
    depth, cols, rows, _ = planes.shape
    odd = core_ref[0] == 1
    unpack(flat, partner, lambda value: jnp.where(odd, value, roll_rows(value, 2)))

    def straight(z, values):
        for col, value in enumerate(values):
            acc[z, col] = acc_in[z, col] + value * partner[z + HALO, col + HALO]
            kept[z, col] = value * planes[z + HALO, col + HALO]

    potentials(planes, partner, rho, field, straight)

    def shift(z, _):
        for col in range(cols):
            partner[z, col] = mixed(partner[z, col], -1, 1)
        return 0

    lax.fori_loop(0, depth, shift, 0)

    def swapped(z, values):
        tiles = []
        for col, value in enumerate(values):
            acc[z, col] = acc[z, col] + value * partner[z + HALO, col + HALO]
            total = kept[z, col] + mixed(value * planes[z + HALO, col + HALO], -1, 1)
            total = jnp.where(odd, total, roll_rows(total, -2))
            tiles.append(total * (-1.0 / CENTRE))
        repack(tiles, travel, z)

    potentials(planes, partner, rho, field, swapped)


def split_body(*refs):
    mine, theirs, outs = refs[0], refs[1], refs[2:]
    depth, rows, span = mine.shape
    orbs = outs[0].shape[0]
    for z in range(0, depth, 8):
        top = min(z + 8, depth)
        for a in range(0, span, LANES):
            b = min(a + LANES, span)
            value = mine[z:top, :, a:b] + theirs[z:top, :, a:b]
            value = jnp.swapaxes(value, 0, 1)
            for slot, out in enumerate(outs):
                out[:, z:top, a:b] = value[slot * orbs : (slot + 1) * orbs]


def place_body(chips, chip_ref, *refs):
    ins, out = refs[:chips], refs[chips]
    chip = chip_ref[0]
    span = ins[0].shape[2]
    for behind in range(chips):
        for source in range(chips):

            @pl.when(lax.rem(chip + chips - behind, chips) == source)
            def _(behind=behind, source=source):
                out[:, :, source * span : (source + 1) * span] = ins[behind][...]


def per_device(n_band, orbitals):
    orbs, depth, total = orbitals.shape
    chips = n_band // 2
    width = total // NY // chips
    index = lax.axis_index("band")
    chip = (index // 2).astype(jnp.int32).reshape(1)
    core = (index % 2).astype(jnp.int32).reshape(1)

    def along(value, steps):
        pairs = [(i, (i + 2 * steps) % n_band) for i in range(n_band)]
        return lax.ppermute(value, "band", pairs)

    def partner_core(value):
        return lax.ppermute(value, "band", [(i, i ^ 1) for i in range(n_band)])

    n_slab = lax.axis_size("slab")
    up = [(i, (i + 1) % n_slab) for i in range(n_slab)]
    down = [(j, i) for i, j in up]
    below = lax.ppermute(orbitals[:, depth - HALO :], "slab", up)
    above = lax.ppermute(orbitals[:, :HALO], "slab", down)

    main = pack(chip, [orbitals], chips, width)
    main = [main[0]] + [along(main[s], s) for s in range(1, chips)]
    edge = pack(chip, [below, above], chips, width)
    edge = [edge[0]] + [along(edge[s], s) for s in range(1, chips)]
    order = [0] + list(range(chips - 1, 0, -1))
    flat = gather([main[s] for s in order], [edge[s] for s in order])
    other = partner_core(flat)

    rows = orbs * chips
    cols = width + 2 * HALO
    full = (depth + 2 * HALO, cols, rows, LANES)
    swept = (depth + 2 * REACH, cols - 2 * REACH, rows, LANES)
    inner = (depth, width, rows, LANES)
    scratch = [pltpu.VMEM(s, jnp.float32) for s in (full, full, swept)]
    points = rows * LANES * depth * cols
    planes, acc = call(
        functools.partial(same_body, False, False),
        [sds(*full), sds(*inner)],
        [flat],
        scratch=scratch,
        flops=40 * points,
        name="same",
    )
    acc, travel = call(
        cross_kernel,
        [sds(*inner), sds(depth, rows, width * NY)],
        [core, planes, acc, other],
        scratch=scratch + [pltpu.VMEM(inner, jnp.float32)],
        flops=80 * points,
        smem=True,
        name="cross",
    )
    back = partner_core(travel)
    mine = call(
        functools.partial(same_body, True, True),
        [sds(depth, rows, width * NY)],
        [planes, acc],
        scratch=scratch,
        flops=40 * points,
        name="same_swapped",
    )[0]
    parts = call(
        split_body,
        [sds(orbs, depth, width * NY)] * chips,
        [mine, back],
        name="split",
    )
    parts = [parts[0]] + [along(parts[s], s) for s in range(1, chips)]
    return call(
        functools.partial(place_body, chips),
        [sds(orbs, depth, total)],
        [chip, *parts],
        smem=True,
        name="place",
    )[0]


def solution(mesh):
    return jax.shard_map(
        functools.partial(per_device, mesh.shape["band"]),
        mesh=mesh,
        in_specs=(P("band", "slab", None),),
        out_specs=P("band", "slab", None),
        check_vma=False,
    )
```

time: 595 us -> 176 us (0.30); the launches traced: 585 us -> 176 us
  other arithmetic: 323 us -> 0 us
  local copies, waits for them, and re-layouts: 152 us -> 17.1 us
  Pallas kernels: 0 us -> 108 us
  waiting for transfers between devices: 87.6 us -> 32.7 us
    div x3 -> x0, other arithmetic: 203 us -> none  [the longest x2 200 us: per_device(): field = (density + trim_off(padded)) / centre_weight]
    slice x40 -> x1, local copies, waits for them, and re-layouts: 146 us -> 1.12 us  [per_device(): above = lax.ppermute(orbitals[:, :HALO], 'slab', down)]
    reduce_sum x1 -> x0, other arithmetic: 111 us -> none  [per_device(): total = -jnp.sum(field * block_ext[None], axis=1)]
    pallas_call x0 -> x8, Pallas kernels: none -> 108 us  [call(): pl.pallas_call(body, out_shape=out, in_specs=specs, out_specs=[VMEM] * le...]
    ppermute x12 -> x13, waiting for transfers between devices: 87.6 us -> 32.7 us  [the longest x9 25.2 us: along(): return lax.ppermute(value, 'band', pairs)]
    pallas_call x0 -> x4, local copies, waits for them, and re-layouts: none -> 6.41 us  [call(): pl.pallas_call(body, out_shape=out, in_specs=specs, out_specs=[VMEM] * le...]
    ppermute x12 -> x13, starting transfers between devices: 21.8 us -> 18.1 us  [the longest x9 13.9 us: along(): return lax.ppermute(value, 'band', pairs)]
  transfers between devices with their start and end apart: 12 -> 13, of which waited for: 8 -> 9; matrix products, arithmetic and copies ran while one was open for 20% -> 3% of each run, Pallas kernels for 0% -> 28%
where the time goes in v1:
time: 176 us
  Pallas kernels  108 us (61%)
  waiting for transfers between devices  32.7 us (19%)
  starting transfers between devices  18.1 us (10%)
  local copies, waits for them, and re-layouts  17.1 us (10%)
    pallas_call x8, Pallas kernels, call(): pl.pallas_call(body, out_shape=out, in_specs=specs, out_specs=[VMEM] * le...  108 us
    ppermute x9, waiting for transfers between devices, along(): return lax.ppermute(value, 'band', pairs)  25.2 us
    ppermute x9, starting transfers between devices, along(): return lax.ppermute(value, 'band', pairs)  13.9 us
    unnamed x19, local copies, waits for them, and re-layouts  6.91 us
    pallas_call x4, local copies, waits for them, and re-layouts, call(): pl.pallas_call(body, out_shape=out, in_specs=specs, out_specs=[VMEM] * le...  6.41 us
    ppermute x1, waiting for transfers between devices, per_device(): above = lax.ppermute(orbitals[:, :HALO], 'slab', down)  4.54 us
    ppermute x1, starting transfers between devices, per_device(): above = lax.ppermute(orbitals[:, :HALO], 'slab', down)  3.66 us
  transfers between devices with their start and end apart: 13, of which 9 were waited for; matrix products, arithmetic and copies ran while one was open for 3% of the time, Pallas kernels for 28%

profile of v1, /device:TPU:0, one launch (start us, length us, event | category | flops | bytes accessed | tf_op | source)
XLA Modules:
  0.0 175.6 jit_solution(8041367301574532766)
XLA Ops:
  0.0 2.7 %copy.6.refs_1_ = f32[2,36,5184]{2,1,0:T(8,128)} copy(f32[2,36,5184]{2,0,1:T(2,128)} %param.1) | data formatting | bytes 2985984 | tf_op args[0]
  2.7 3.7 %pack.2 = (f32[2,36,1872]{2,1,0:T(8,128)}, f32[2,36,1872]{2,1,0:T(8,128)}, f32[2,36,1872]{2,1,0:T(8,128)}, f32[2,36,1872]{2,1,0:T(8,128)}) custom-call(s32[1]{0:T(128)} %bitcast.refs_0_.chip_ref, f32[2,36,5184]{2,1,0:T(8,128)} %copy.6.refs_1_), custom_call_target="tpu_custom_call" | custom-call | bytes 3649540 | tf_op jit(solution)/shard_map/pack/pallas_call | solution.py:33
  6.4 1.4 copy.9
  7.8 3.0 %collective-permute-start.2 = (f32[2,36,1872]{2,0,1:T(2,128)S(1)}, f32[2,36,1872]{2,0,1:T(2,128)S(1)}, u32[]{:S(2)}, u32[]{:S(2)}) collective-permute-start(f32[2,36,1872]{2,0,1:T(2,128)S(1)} %copy.9), channel_id=1, source_target_pairs={{0,8},{4,12},{8,16},{12,20},{16,24},{20,28},{24,0},{28,4},{1,9},{5... | collective-permute-start | bytes 1617416 | tf_op jit(solution)/shard_map/ppermute | solution.py:339
  10.8 1.4 copy.8
  12.2 1.6 collective-permute-start.1
  14.1 1.5 collective-permute-start
  15.6 1.1 fusion
  16.7 3.7 %collective-permute-start.4 = (f32[2,4,5184]{2,1,0:T(4,128)S(1)}, f32[2,4,5184]{2,1,0:T(4,128)S(1)}, u32[]{:S(2)}, u32[]{:S(2)}) collective-permute-start(f32[2,4,5184]{2,1,0:T(4,128)S(1)} %get-tuple-element.37), channel_id=1, source_target_pairs={{1,0},{2,1},{3,2},{0,3},{5,4},{6,5},{7,6},{4,7},{9,8},{10,9},{11,1... | collective-permute-start | bytes 497672 | tf_op jit(solution)/shard_map/ppermute | solution.py:348
  20.3 4.5 %collective-permute-done.4.refs_2_ = f32[2,4,5184]{2,1,0:T(4,128)S(1)} collective-permute-done((f32[2,4,5184]{2,1,0:T(4,128)S(1)}, f32[2,4,5184]{2,1,0:T(4,128)S(1)}, u32[]{:S(2)}, u32[]{:S(2)}) %collective-permute-start.4) | collective-permute-done | bytes 165920 | tf_op jit(solution)/shard_map/ppermute | solution.py:348
  24.9 2.9 %collective-permute-done.3.refs_1_ = f32[2,4,5184]{2,1,0:T(4,128)} collective-permute-done((f32[2,4,5184]{2,1,0:T(4,128)S(1)}, f32[2,4,5184]{2,1,0:T(4,128)}, u32[]{:S(2)}, u32[]{:S(2)}) %collective-permute-start.3) | collective-permute-done | bytes 165920 | tf_op jit(solution)/shard_map/ppermute | solution.py:347
  27.8 2.3 %pack.3 = (f32[2,8,1872]{2,1,0:T(8,128)}, f32[2,8,1872]{2,1,0:T(8,128)}, f32[2,8,1872]{2,1,0:T(8,128)}, f32[2,8,1872]{2,1,0:T(8,128)}) custom-call(s32[1]{0:T(128)} %bitcast.refs_0_.chip_ref, f32[2,4,5184]{2,1,0:T(4,128)} %collective-permute-done.3.refs_1_, f32[2,4,5184]{2,1,0:T(4,128)} %copy-done.6), custom_call_target="tpu_custom_call" | custom-call | bytes 811012 | tf_op jit(solution)/shard_map/pack/pallas_call | solution.py:33
  30.6 1.5 collective-permute-start.6
  32.6 0.9 copy.14.refs_3_
  33.5 2.8 %collective-permute-done.1 = f32[2,36,1872]{2,0,1:T(2,128)S(1)} collective-permute-done((f32[2,36,1872]{2,0,1:T(2,128)S(1)}, f32[2,36,1872]{2,0,1:T(2,128)S(1)}, u32[]{:S(2)}, u32[]{:S(2)}) %collective-permute-start.1) | collective-permute-done | bytes 539168 | tf_op jit(solution)/shard_map/ppermute | solution.py:339
  36.3 0.9 copy.13.refs_2_
  37.6 0.9 copy.12.refs_1_
  38.5 1.7 collective-permute-done.5.refs_5_
  40.2 1.2 collective-permute-done.7.refs_7_
  42.1 3.8 %gather.1.refs_0_ = f32[44,8,1872]{2,1,0:T(8,128)} custom-call(f32[2,36,1872]{2,1,0:T(8,128)} %get-tuple-element.21.refs_0_, f32[2,36,1872]{2,1,0:T(8,128)} %copy.12.refs_1_, f32[2,36,1872]{2,1,0:T(8,128)} %copy.13.refs_2_, f32[2,36,1872]{2,1,0:T(8,128)} %copy.14.refs_3_, f32[2,8,1872]{2,1,0:T(8,128)} %get-tuple-element.25.refs_4_, f32[2,8,1872]{2,1,0:T(8,128)} %copy-done.7, ...), custom_call_target="tpu_custom_call" | custom-call | bytes 5271552 | tf_op jit(solution)/shard_map/gather/pallas_call | solution.py:33
  45.9 27.4 %same.1 = (f32[44,26,8,128]{3,2,1,0:T(8,128)}, f32[36,18,8,128]{3,2,1,0:T(8,128)}) custom-call(f32[44,8,1872]{2,1,0:T(8,128)} %gather.1.refs_0_), custom_call_target="tpu_custom_call" | custom-call | flops 38338560 | bytes 9975808 | tf_op jit(solution)/shard_map/same/pallas_call | solution.py:33
  73.3 1.5 copy-done
  74.9 43.8 %cross.1 = (f32[36,18,8,128]{3,2,1,0:T(8,128)}, f32[36,8,1296]{2,1,0:T(8,128)}) custom-call(s32[1]{0:T(128)} %bitcast.1.core_ref, f32[44,26,8,128]{3,2,1,0:T(8,128)} %get-tuple-element.29.planes.refs_0_, f32[36,18,8,128]{3,2,1,0:T(8,128)} %get-tuple-element.30.acc_in, f32[44,8,1872]{2,1,0:T(8,128)} %copy-done), custom_call_target="tpu_custom_call" | custom-call | flops 76677120 | bytes 14123012 | tf_op jit(solution)/shard_map/cross/pallas_call | solution.py:33
  119.2 20.1 %same_swapped.1.refs_0_ = f32[36,8,1296]{2,1,0:T(8,128)} custom-call(f32[44,26,8,128]{3,2,1,0:T(8,128)} %get-tuple-element.29.planes.refs_0_, f32[36,18,8,128]{3,2,1,0:T(8,128)} %get-tuple-element.31.refs_1_), custom_call_target="tpu_custom_call" | custom-call | flops 38338560 | bytes 8833024 | tf_op jit(solution)/shard_map/same_swapped/pallas_call | solution.py:33
  139.3 1.2 copy-done.1
  140.5 3.4 %split.1 = (f32[2,36,1296]{2,1,0:T(8,128)}, f32[2,36,1296]{2,1,0:T(8,128)}, f32[2,36,1296]{2,1,0:T(8,128)}, f32[2,36,1296]{2,1,0:T(8,128)}) custom-call(f32[36,8,1296]{2,1,0:T(8,128)} %same_swapped.1.refs_0_, f32[36,8,1296]{2,1,0:T(8,128)} %copy-done.1), custom_call_target="tpu_custom_call" | custom-call | bytes 4478976 | tf_op jit(solution)/shard_map/split/pallas_call | solution.py:33
  143.9 3.9 %collective-permute-start.10 = (f32[2,36,1296]{2,1,0:T(8,128)}, f32[2,36,1296]{2,1,0:T(8,128)S(1)}, u32[]{:S(2)}, u32[]{:S(2)}) collective-permute-start(f32[2,36,1296]{2,1,0:T(8,128)} %get-tuple-element.34), channel_id=1, source_target_pairs={{0,8},{4,12},{8,16},{12,20},{16,24},{20,28},{24,0},{28,4},{1,9},{5... | collective-permute-start | bytes 1119752 | tf_op jit(solution)/shard_map/ppermute | solution.py:339
  147.9 1.3 collective-permute-start.12
  149.2 9.6 %collective-permute-done.10.refs_1_ = f32[2,36,1296]{2,1,0:T(8,128)S(1)} collective-permute-done((f32[2,36,1296]{2,1,0:T(8,128)}, f32[2,36,1296]{2,1,0:T(8,128)S(1)}, u32[]{:S(2)}, u32[]{:S(2)}) %collective-permute-start.10) | collective-permute-done | bytes 373280 | tf_op jit(solution)/shard_map/ppermute | solution.py:339
  158.8 8.9 %collective-permute-done.11.refs_2_ = f32[2,36,1296]{2,1,0:T(8,128)S(1)} collective-permute-done((f32[2,36,1296]{2,1,0:T(8,128)}, f32[2,36,1296]{2,1,0:T(8,128)S(1)}, u32[]{:S(2)}, u32[]{:S(2)}) %collective-permute-start.11) | collective-permute-done | bytes 373280 | tf_op jit(solution)/shard_map/ppermute | solution.py:339
  169.0 3.3 %place.1 = f32[2,36,5184]{2,1,0:T(8,128)} custom-call(s32[1]{0:T(128)} %bitcast.refs_0_.chip_ref, f32[2,36,1296]{2,1,0:T(8,128)} %get-tuple-element.33.refs_0_, f32[2,36,1296]{2,1,0:T(8,128)} %copy-done.3, f32[2,36,1296]{2,1,0:T(8,128)} %copy-done.4, f32[2,36,1296]{2,1,0:T(8,128)} %copy-done.5), custom_call_target="tpu_custom_call" | custom-call | bytes 2985988 | tf_op jit(solution)/shard_map/place/pallas_call | solution.py:33
  172.2 3.3 %copy.15 = f32[2,36,5184]{2,0,1:T(2,128)} copy(f32[2,36,5184]{2,1,0:T(8,128)} %place.1) | data formatting | bytes 2985984 | tf_op jit(solution)/shard_map/place/pallas_call | solution.py:33
  (29 shorter events, 4.3 us)
Async XLA Ops:
  6.4 7.4 %copy-start.2 = (f32[2,36,1872]{2,1,0:T(8,128)S(1)}, f32[2,36,1872]{2,1,0:T(8,128)}, u32[]{:S(2)}) copy-start(f32[2,36,1872]{2,1,0:T(8,128)} %get-tuple-element.22) | copy-start | bytes 1617412
  7.8 24.3 %collective-permute-start.2 = (f32[2,36,1872]{2,0,1:T(2,128)S(1)}, f32[2,36,1872]{2,0,1:T(2,128)S(1)}, u32[]{:S(2)}, u32[]{:S(2)}) collective-permute-start(f32[2,36,1872]{2,0,1:T(2,128)S(1)} %copy.9), channel_id=1, source_target_pairs={{0,8},{4,12},{8,16},{12,20},{16,24},{20,28},{24,0},{28,4},{1,9},{5... | collective-permute-start | bytes 1617416 | tf_op jit(solution)/shard_map/ppermute | solution.py:339
  12.2 24.1 %collective-permute-start.1 = (f32[2,36,1872]{2,0,1:T(2,128)S(1)}, f32[2,36,1872]{2,0,1:T(2,128)S(1)}, u32[]{:S(2)}, u32[]{:S(2)}) collective-permute-start(f32[2,36,1872]{2,0,1:T(2,128)S(1)} %copy.8), channel_id=1, source_target_pairs={{0,16},{4,20},{8,24},{12,28},{16,0},{20,4},{24,8},{28,12},{1,17},{... | collective-permute-start | bytes 1617416 | tf_op jit(solution)/shard_map/ppermute | solution.py:339
  14.1 23.5 %collective-permute-start = (f32[2,36,1872]{2,0,1:T(2,128)S(1)}, f32[2,36,1872]{2,0,1:T(2,128)S(1)}, u32[]{:S(2)}, u32[]{:S(2)}) collective-permute-start(f32[2,36,1872]{2,0,1:T(2,128)S(1)} %copy.7), channel_id=1, source_target_pairs={{0,24},{4,28},{8,0},{12,4},{16,8},{20,12},{24,16},{28,20},{1,25},{... | collective-permute-start | bytes 1617416 | tf_op jit(solution)/shard_map/ppermute | solution.py:339
  16.7 8.2 %collective-permute-start.4 = (f32[2,4,5184]{2,1,0:T(4,128)S(1)}, f32[2,4,5184]{2,1,0:T(4,128)S(1)}, u32[]{:S(2)}, u32[]{:S(2)}) collective-permute-start(f32[2,4,5184]{2,1,0:T(4,128)S(1)} %get-tuple-element.37), channel_id=1, source_target_pairs={{1,0},{2,1},{3,2},{0,3},{5,4},{6,5},{7,6},{4,7},{9,8},{10,9},{11,1... | collective-permute-start | bytes 497672 | tf_op jit(solution)/shard_map/ppermute | solution.py:348
  20.3 7.5 %collective-permute-start.3 = (f32[2,4,5184]{2,1,0:T(4,128)S(1)}, f32[2,4,5184]{2,1,0:T(4,128)}, u32[]{:S(2)}, u32[]{:S(2)}) collective-permute-start(f32[2,4,5184]{2,1,0:T(4,128)S(1)} %get-tuple-element.38), channel_id=1, source_target_pairs={{0,1},{1,2},{2,3},{3,0},{4,5},{5,6},{6,7},{7,4},{8,9},{9,10},{10,1... | collective-permute-start | bytes 497672 | tf_op jit(solution)/shard_map/ppermute | solution.py:347
  24.9 2.9 %copy-start.6 = (f32[2,4,5184]{2,1,0:T(4,128)}, f32[2,4,5184]{2,1,0:T(4,128)S(1)}, u32[]{:S(2)}) copy-start(f32[2,4,5184]{2,1,0:T(4,128)S(1)} %collective-permute-done.4.refs_2_) | copy-start | bytes 497668
  30.1 10.2 %collective-permute-start.5 = (f32[2,8,1872]{2,1,0:T(8,128)}, f32[2,8,1872]{2,1,0:T(8,128)S(1)}, u32[]{:S(2)}, u32[]{:S(2)}) collective-permute-start(f32[2,8,1872]{2,1,0:T(8,128)} %get-tuple-element.26), channel_id=1, source_target_pairs={{0,24},{4,28},{8,0},{12,4},{16,8},{20,12},{24,16},{28,20},{1,25},{... | collective-permute-start | bytes 359432 | tf_op jit(solution)/shard_map/ppermute | solution.py:339
  30.6 9.6 %collective-permute-start.6 = (f32[2,8,1872]{2,1,0:T(8,128)}, f32[2,8,1872]{2,1,0:T(8,128)}, u32[]{:S(2)}, u32[]{:S(2)}) collective-permute-start(f32[2,8,1872]{2,1,0:T(8,128)} %get-tuple-element.27), channel_id=1, source_target_pairs={{0,16},{4,20},{8,24},{12,28},{16,0},{20,4},{24,8},{28,12},{1,17},{... | collective-permute-start | bytes 359432 | tf_op jit(solution)/shard_map/ppermute | solution.py:339
  32.1 9.4 %collective-permute-start.7 = (f32[2,8,1872]{2,1,0:T(8,128)}, f32[2,8,1872]{2,1,0:T(8,128)S(1)}, u32[]{:S(2)}, u32[]{:S(2)}) collective-permute-start(f32[2,8,1872]{2,1,0:T(8,128)} %get-tuple-element.28), channel_id=1, source_target_pairs={{0,8},{4,12},{8,16},{12,20},{16,24},{20,28},{24,0},{28,4},{1,9},{5... | collective-permute-start | bytes 359432 | tf_op jit(solution)/shard_map/ppermute | solution.py:339
  40.2 1.3 copy-start.7
  41.5 0.6 copy-start.8
  45.9 27.4 %collective-permute-start.8 = (f32[44,8,1872]{2,1,0:T(8,128)}, f32[44,8,1872]{2,1,0:T(8,128)S(1)}, u32[]{:S(2)}, u32[]{:S(2)}) collective-permute-start(f32[44,8,1872]{2,1,0:T(8,128)} %gather.1.refs_0_), channel_id=1, source_target_pairs={{0,4},{4,0},{8,12},{12,8},{16,20},{20,16},{24,28},{28,24},{1,5},{5... | collective-permute-start | bytes 7907336 | tf_op jit(solution)/shard_map/ppermute | solution.py:342
  73.3 1.5 copy-start
  118.7 20.6 %collective-permute-start.9 = (f32[36,8,1296]{2,1,0:T(8,128)}, f32[36,8,1296]{2,1,0:T(8,128)S(1)}, u32[]{:S(2)}, u32[]{:S(2)}) collective-permute-start(f32[36,8,1296]{2,1,0:T(8,128)} %get-tuple-element.32), channel_id=1, source_target_pairs={{0,4},{4,0},{8,12},{12,8},{16,20},{20,16},{24,28},{28,24},{1,5},{5... | collective-permute-start | bytes 4478984 | tf_op jit(solution)/shard_map/ppermute | solution.py:342
  139.3 1.2 copy-start.1
  143.9 14.9 %collective-permute-start.10 = (f32[2,36,1296]{2,1,0:T(8,128)}, f32[2,36,1296]{2,1,0:T(8,128)S(1)}, u32[]{:S(2)}, u32[]{:S(2)}) collective-permute-start(f32[2,36,1296]{2,1,0:T(8,128)} %get-tuple-element.34), channel_id=1, source_target_pairs={{0,8},{4,12},{8,16},{12,20},{16,24},{20,28},{24,0},{28,4},{1,9},{5... | collective-permute-start | bytes 1119752 | tf_op jit(solution)/shard_map/ppermute | solution.py:339
  147.7 19.9 %collective-permute-start.11 = (f32[2,36,1296]{2,1,0:T(8,128)}, f32[2,36,1296]{2,1,0:T(8,128)S(1)}, u32[]{:S(2)}, u32[]{:S(2)}) collective-permute-start(f32[2,36,1296]{2,1,0:T(8,128)} %get-tuple-element.35), channel_id=1, source_target_pairs={{0,16},{4,20},{8,24},{12,28},{16,0},{20,4},{24,8},{28,12},{1,17},{... | collective-permute-start | bytes 1119752 | tf_op jit(solution)/shard_map/ppermute | solution.py:339
  147.9 20.3 %collective-permute-start.12 = (f32[2,36,1296]{2,1,0:T(8,128)}, f32[2,36,1296]{2,1,0:T(8,128)S(1)}, u32[]{:S(2)}, u32[]{:S(2)}) collective-permute-start(f32[2,36,1296]{2,1,0:T(8,128)} %get-tuple-element.36), channel_id=1, source_target_pairs={{0,24},{4,28},{8,0},{12,4},{16,8},{20,12},{24,16},{28,20},{1,25},{... | collective-permute-start | bytes 1119752 | tf_op jit(solution)/shard_map/ppermute | solution.py:339
  158.8 9.4 %copy-start.3 = (f32[2,36,1296]{2,1,0:T(8,128)}, f32[2,36,1296]{2,1,0:T(8,128)S(1)}, u32[]{:S(2)}) copy-start(f32[2,36,1296]{2,1,0:T(8,128)S(1)} %collective-permute-done.10.refs_1_) | copy-start | bytes 1119748
  167.7 0.8 copy-start.4
  168.2 0.8 copy-start.5

commit v2 on v1

v2 whole, which is shorter than its diff:
```python
import functools

import jax
import jax.numpy as jnp
from jax import lax
from jax.experimental import pallas as pl
from jax.experimental.pallas import tpu as pltpu
from jax.sharding import PartitionSpec as P

NY = 72
LANES = 128
TILE = 256
WINDOW = 3 * TILE
REACH = 2
HALO = 4
CENTRE = 8.5
ALPHA = 1.0 / (12.0 * CENTRE)
VMEM = pl.BlockSpec(memory_space=pltpu.VMEM)
SMEM = pl.BlockSpec(memory_space=pltpu.SMEM)


def params(limit=None):
    return pltpu.CompilerParams(vmem_limit_bytes=limit)


def sds(*shape):
    return jax.ShapeDtypeStruct(shape, jnp.float32)


def call(body, out, inputs, scratch=(), flops=0, smem=False, limit=None, name=None):
    nbytes = sum(4 * x.size for x in inputs) + sum(4 * o.size for o in out)
    specs = [VMEM] * len(inputs)
    if smem:
        specs[0] = SMEM
    return pl.pallas_call(
        body,
        out_shape=out,
        in_specs=specs,
        out_specs=[VMEM] * len(out),
        scratch_shapes=scratch,
        compiler_params=params(limit),
        cost_estimate=pl.CostEstimate(flops=flops, bytes_accessed=nbytes, transcendentals=0),
        name=name,
    )(*inputs)


def pack_body(chips, width, n_in, *refs):
    chip_ref, ins, outs = refs[0], refs[1 : 1 + n_in], refs[1 + n_in :]
    chip = chip_ref[0]
    total = ins[0].shape[2]
    span = (width + 2 * HALO) * NY
    for ahead in range(chips):
        for target in range(chips):

            @pl.when(lax.rem(chip + ahead, chips) == target)
            def _(ahead=ahead, target=target):
                start = (target * width - HALO) * NY
                row = 0
                for ref in ins:
                    rows = ref.shape[1]
                    for orb in range(ref.shape[0]):
                        lo, hi = start, start + span
                        if lo < 0:
                            value = jnp.concatenate(
                                [ref[orb, :, lo + total : total], ref[orb, :, 0:hi]], axis=-1
                            )
                        elif hi > total:
                            value = jnp.concatenate(
                                [ref[orb, :, lo:total], ref[orb, :, 0 : hi - total]], axis=-1
                            )
                        else:
                            value = ref[orb, :, lo:hi]
                        outs[ahead][orb, row : row + rows, :] = value
                    row += rows


def pack(chip, pieces, chips, width):
    orbs = pieces[0].shape[0]
    rows = sum(p.shape[1] for p in pieces)
    span = (width + 2 * HALO) * NY
    return call(
        functools.partial(pack_body, chips, width, len(pieces)),
        [sds(orbs, rows, span)] * chips,
        [chip, *pieces],
        smem=True,
        name="pack",
    )


def gather_body(chips, *refs):
    main, edge, out = refs[:chips], refs[chips : 2 * chips], refs[2 * chips]
    orbs, depth, span = main[0].shape

    def move(sources, lo, hi, at):
        for a in range(0, span, LANES):
            b = min(a + LANES, span)
            value = jnp.concatenate([ref[:, lo:hi, a:b] for ref in sources], axis=0)
            out[at : at + hi - lo, :, a:b] = jnp.swapaxes(value, 0, 1)

    move(edge, 0, HALO, 0)
    for z in range(0, depth, 8):
        move(main, z, min(z + 8, depth), HALO + z)
    move(edge, HALO, 2 * HALO, HALO + depth)


def gather(main, edge):
    orbs, depth, span = main[0].shape
    chips = len(main)
    return call(
        functools.partial(gather_body, chips),
        [sds(depth + 2 * HALO, orbs * chips, span)],
        [*main, *edge],
        name="gather",
    )[0]


def row_mixed(value, even, odd):
    rows = value.shape[1]
    row = lax.broadcasted_iota(jnp.int32, value.shape, 1)
    return jnp.where(row % 2 == 0, roll_rows(value, even), roll_rows(value, odd))


def roll_rows(value, shift):
    return pltpu.roll(value, shift % value.shape[1], 1)


def n_tiles(span, sweeps):
    return -(-(span - sweeps * REACH * NY - LANES) // TILE)


def weights_body(out):
    i = lax.broadcasted_iota(jnp.int32, (WINDOW, TILE), 0)
    lane = lax.broadcasted_iota(jnp.int32, (1, TILE), 1)

    def tile(t, _):
        y = lax.rem(lane + (t * TILE + LANES), NY)
        at = lane + 2 * LANES
        near = (i == at - NY) | (i == at + NY)
        far = (i == at - 2 * NY) | (i == at + 2 * NY)
        for step in (1, -1):
            near |= i == at + step - jnp.where(y + step >= NY, NY, jnp.where(y + step < 0, -NY, 0))
        for step in (2, -2):
            far |= i == at + step - jnp.where(y + step >= NY, NY, jnp.where(y + step < 0, -NY, 0))
        value = jnp.where(near, 16.0, jnp.where(far, -1.0, 0.0))
        out[t] = value.astype(jnp.bfloat16)
        return 0

    lax.fori_loop(0, out.shape[0], tile, 0)


def weights(span):
    return pl.pallas_call(
        weights_body,
        out_shape=jax.ShapeDtypeStruct((n_tiles(span, 1), WINDOW, TILE), jnp.bfloat16),
        out_specs=VMEM,
        name="weights",
    )()


def halves(value):
    high = value.astype(jnp.bfloat16)
    return high, (value - high.astype(jnp.float32)).astype(jnp.bfloat16)


def in_plane(split_ref, first, rows, t, weight):
    lanes = pl.ds(pl.multiple_of(t * TILE, TILE), WINDOW)
    total = None
    for half in range(2):
        part = jnp.dot(
            split_ref[half, first : first + rows, lanes],
            weight,
            preferred_element_type=jnp.float32,
        )
        total = part if total is None else total + part
    return total


def off(split_ref, full_ref, n_rows, depth, t, weight):
    lanes = pl.ds(pl.multiple_of(t * TILE, TILE), TILE)

    def planes(z):
        return full_ref[z * n_rows : (z + depth) * n_rows, lanes]

    inside = in_plane(split_ref, REACH * n_rows, depth * n_rows, t, weight)
    near = planes(1) + planes(3)
    far = planes(0) + planes(4)
    return planes(2), inside + (16.0 * near - far)


def potentials(first, to_partner, second, w_ref, work, finish):
    rho_split, rho, mid_split, mid = work
    depth, n_rows, span = first.shape
    for ref in (rho_split, mid_split):
        edge = jnp.zeros((2, ref.shape[1], 2 * LANES), jnp.bfloat16)
        ref[:, :, 0 : 2 * LANES] = edge
    tail = (LANES + span) // LANES * LANES
    rho_split[:, :, tail:] = jnp.zeros(
        (2, rho_split.shape[1], rho_split.shape[2] - tail), jnp.bfloat16
    )
    held = rho.shape[1]
    tail = (span - LANES) // LANES * LANES
    if tail < held:
        rho[:, tail:] = jnp.zeros((rho.shape[0], held - tail), jnp.float32)
    step = 4

    def density(s, _):
        z = pl.multiple_of(s * step, step)
        rows = pl.ds(pl.multiple_of(s * (step * n_rows), step * n_rows), step * n_rows)
        for lo in range(0, span, LANES):
            hi = min(lo + LANES, span)
            value = first[pl.ds(z, step), :, lo:hi] * to_partner(second[pl.ds(z, step), :, lo:hi])
            value = value.reshape(step * n_rows, hi - lo)
            high, low = halves(value)
            rho_split[0, rows, lo + LANES : hi + LANES] = high
            rho_split[1, rows, lo + LANES : hi + LANES] = low
            if LANES <= lo < held + LANES:
                rho[rows, lo - LANES : hi - LANES] = value
        return 0

    lax.fori_loop(0, depth // step, density, 0)

    def sweep(t, _):
        centre, total = off(rho_split, rho, n_rows, depth - 2 * REACH, t, w_ref[t])
        value = centre + ALPHA * total
        high, low = halves(value)
        lanes = pl.ds(pl.multiple_of(t * TILE, TILE), TILE)
        mid[:, lanes] = value
        lanes = pl.ds(pl.multiple_of(t * TILE + 2 * LANES, LANES), TILE)
        mid_split[0, :, lanes] = high
        mid_split[1, :, lanes] = low
        return 0

    lax.fori_loop(0, w_ref.shape[0], sweep, 0)

    inner = depth - 2 * HALO

    def last(t, _):
        lanes = pl.ds(pl.multiple_of(t * TILE, TILE), TILE)
        _, total = off(mid_split, mid, n_rows, inner, t, w_ref[t])
        value = rho[HALO * n_rows : (HALO + inner) * n_rows, lanes] + ALPHA * total
        finish(lanes, pl.ds(pl.multiple_of(t * TILE + LANES, LANES), TILE), value.reshape(inner, n_rows, TILE))
        return 0

    lax.fori_loop(0, n_tiles(span, 2), last, 0)


def same_body(swapped, final, planes, w_ref, *refs):
    acc_in = refs[0] if final else None
    acc, *work = refs[1:] if final else refs
    inner = acc.shape[0]

    def to_partner(value):
        return row_mixed(value, 1, 3) if swapped else roll_rows(value, 2)

    def from_partner(value):
        return row_mixed(value, -3, -1) if swapped else roll_rows(value, -2)

    def finish(lanes, at, value):
        mine = planes[HALO : HALO + inner, :, at]
        total = value * to_partner(mine) + from_partner(value * mine)
        if final:
            total = (total + acc_in[:, :, lanes]) * (-1.0 / CENTRE)
        acc[:, :, lanes] = total

    potentials(planes, to_partner, planes, w_ref, work, finish)


def cross_body(core_ref, planes, w_ref, acc_in, flat, acc, travel, partner, *work):
    depth, n_rows, span = planes.shape
    inner = depth - 2 * HALO
    odd = core_ref[0] == 1

    def shift(z, _):
        for lo in range(0, span, LANES):
            hi = min(lo + LANES, span)
            value = flat[pl.ds(z * 4, 4), :, lo:hi]
            partner[pl.ds(z * 4, 4), :, lo:hi] = jnp.where(odd, value, roll_rows(value, 2))
        return 0

    lax.fori_loop(0, depth // 4, shift, 0)

    def straight(lanes, at, value):
        acc[:, :, lanes] = acc_in[:, :, lanes] + value * partner[HALO : HALO + inner, :, at]
        travel[:, :, lanes] = value * planes[HALO : HALO + inner, :, at]

    potentials(planes, lambda v: v, partner, w_ref, work, straight)

    def swap(value):
        return row_mixed(value, -1, 1)

    def swapped(lanes, at, value):
        acc[:, :, lanes] = acc[:, :, lanes] + value * swap(partner[HALO : HALO + inner, :, at])
        total = travel[:, :, lanes] + swap(value * planes[HALO : HALO + inner, :, at])
        travel[:, :, lanes] = jnp.where(odd, total, roll_rows(total, -2)) * (-1.0 / CENTRE)

    potentials(planes, swap, partner, w_ref, work, swapped)


def split_body(first, *refs):
    mine, theirs, outs = refs[0], refs[1], refs[2:]
    depth = mine.shape[0]
    orbs, _, span = outs[0].shape
    for z in range(0, depth, 8):
        top = min(z + 8, depth)
        for a in range(0, span, LANES):
            b = min(a + LANES, span)
            value = mine[z:top, :, first + a : first + b] + theirs[z:top, :, a:b]
            value = jnp.swapaxes(value, 0, 1)
            for slot, out in enumerate(outs):
                out[:, z:top, a:b] = value[slot * orbs : (slot + 1) * orbs]


def place_body(chips, first, chip_ref, *refs):
    ins, out = refs[:chips], refs[chips]
    chip = chip_ref[0]
    span = out.shape[2] // chips
    for behind in range(chips):
        for source in range(chips):

            @pl.when(lax.rem(chip + chips - behind, chips) == source)
            def _(behind=behind, source=source):
                out[:, :, source * span : (source + 1) * span] = ins[behind][
                    :, :, first : first + span
                ]


def per_device(n_band, orbitals):
    orbs, depth, total = orbitals.shape
    chips = n_band // 2
    width = total // NY // chips
    index = lax.axis_index("band")
    chip = (index // 2).astype(jnp.int32).reshape(1)
    core = (index % 2).astype(jnp.int32).reshape(1)

    def along(value, steps):
        pairs = [(i, (i + 2 * steps) % n_band) for i in range(n_band)]
        return lax.ppermute(value, "band", pairs)

    def partner_core(value):
        return lax.ppermute(value, "band", [(i, i ^ 1) for i in range(n_band)])

    n_slab = lax.axis_size("slab")
    up = [(i, (i + 1) % n_slab) for i in range(n_slab)]
    down = [(j, i) for i, j in up]
    below = lax.ppermute(orbitals[:, depth - HALO :], "slab", up)
    above = lax.ppermute(orbitals[:, :HALO], "slab", down)

    main = pack(chip, [orbitals], chips, width)
    main = [main[0]] + [along(main[s], s) for s in range(1, chips)]
    edge = pack(chip, [below, above], chips, width)
    edge = [edge[0]] + [along(edge[s], s) for s in range(1, chips)]
    order = [0] + list(range(chips - 1, 0, -1))
    flat = gather([main[s] for s in order], [edge[s] for s in order])
    other = partner_core(flat)

    rows = orbs * chips
    span = (width + 2 * HALO) * NY
    banded = weights(span)
    full = depth + 2 * HALO
    swept = depth + 2 * REACH
    tiles = n_tiles(span, 1)
    lanes = n_tiles(span, 2) * TILE
    work = [
        pltpu.VMEM((2, full * rows, tiles * TILE + WINDOW - TILE), jnp.bfloat16),
        pltpu.VMEM((full * rows, tiles * TILE), jnp.float32),
        pltpu.VMEM((2, swept * rows, tiles * TILE + WINDOW - TILE), jnp.bfloat16),
        pltpu.VMEM((swept * rows, tiles * TILE), jnp.float32),
    ]
    inner = sds(depth, rows, lanes)
    flops = 4 * WINDOW * TILE * tiles * full * rows * 2
    acc = call(
        functools.partial(same_body, False, False),
        [inner],
        [flat, banded],
        scratch=work,
        flops=flops,
        name="same",
    )[0]
    acc, travel = call(
        cross_body,
        [inner, inner],
        [core, flat, banded, acc, other],
        scratch=[pltpu.VMEM((full, rows, span), jnp.float32), *work],
        flops=2 * flops,
        smem=True,
        name="cross",
    )
    start = HALO * NY - LANES
    cut = start // LANES * LANES
    sent = start - cut + width * NY
    back = partner_core(travel[:, :, cut : cut + sent])
    mine = call(
        functools.partial(same_body, True, True),
        [inner],
        [flat, banded, acc],
        scratch=work,
        flops=flops,
        name="same_swapped",
    )[0]
    parts = call(
        functools.partial(split_body, cut),
        [sds(orbs, depth, sent)] * chips,
        [mine, back],
        name="split",
    )
    parts = [parts[0]] + [along(parts[s], s) for s in range(1, chips)]
    return call(
        functools.partial(place_body, chips, start - cut),
        [sds(orbs, depth, total)],
        [chip, *parts],
        smem=True,
        name="place",
    )[0]


def solution(mesh):
    return jax.shard_map(
        functools.partial(per_device, mesh.shape["band"]),
        mesh=mesh,
        in_specs=(P("band", "slab", None),),
        out_specs=P("band", "slab", None),
        check_vma=False,
    )
```

time: 176 us -> 131 us (0.74)
  Pallas kernels: 108 us -> 61 us
    pallas_call x8, Pallas kernels: 108 us -> 57.3 us  [call(): pl.pallas_call(body, out_shape=out, in_specs=specs, out_specs=[VMEM] * le...]
    pallas_call x0 -> x1, Pallas kernels: none -> 3.75 us  [weights(): pl.pallas_call(weights_body, out_shape=jax.ShapeDtypeStruct((n_tiles(span...]
  transfers between devices with their start and end apart: 13 -> 13, of which waited for: 9 -> 9; matrix products, arithmetic and copies ran while one was open for 3% -> 4% of each run, Pallas kernels for 28% -> 21%
where the time goes in v2:
time: 131 us
  Pallas kernels  61 us (47%)
  waiting for transfers between devices  32.7 us (25%)
  local copies, waits for them, and re-layouts  18.6 us (14%)
  starting transfers between devices  18.2 us (14%)
    pallas_call x8, Pallas kernels, call(): pl.pallas_call(body, out_shape=out, in_specs=specs, out_specs=[VMEM] * le...  57.3 us
    ppermute x9, waiting for transfers between devices, along(): return lax.ppermute(value, 'band', pairs)  25.2 us
    ppermute x9, starting transfers between devices, along(): return lax.ppermute(value, 'band', pairs)  14 us
    unnamed x19, local copies, waits for them, and re-layouts  6.9 us
    pallas_call x4, local copies, waits for them, and re-layouts, call(): pl.pallas_call(body, out_shape=out, in_specs=specs, out_specs=[VMEM] * le...  6.41 us
    ppermute x1, waiting for transfers between devices, per_device(): above = lax.ppermute(orbitals[:, :HALO], 'slab', down)  4.54 us
    pallas_call x1, Pallas kernels, weights(): pl.pallas_call(weights_body, out_shape=jax.ShapeDtypeStruct((n_tiles(span...  3.75 us
    ppermute x1, starting transfers between devices, per_device(): above = lax.ppermute(orbitals[:, :HALO], 'slab', down)  3.66 us
  transfers between devices with their start and end apart: 13, of which 9 were waited for; matrix products, arithmetic and copies ran while one was open for 4% of the time, Pallas kernels for 21%

profile of v2, /device:TPU:0, one launch (start us, length us, event | category | flops | bytes accessed | tf_op | source)
XLA Modules:
  0.0 130.6 jit_solution(3437909060903414202)
XLA Ops:
  0.0 2.7 %copy.6.refs_1_ = f32[2,36,5184]{2,1,0:T(8,128)} copy(f32[2,36,5184]{2,0,1:T(2,128)} %param.1) | data formatting | bytes 2985984 | tf_op args[0]
  2.7 3.7 %pack.2 = (f32[2,36,1872]{2,1,0:T(8,128)}, f32[2,36,1872]{2,1,0:T(8,128)}, f32[2,36,1872]{2,1,0:T(8,128)}, f32[2,36,1872]{2,1,0:T(8,128)}) custom-call(s32[1]{0:T(128)} %bitcast.refs_0_.chip_ref, f32[2,36,5184]{2,1,0:T(8,128)} %copy.6.refs_1_), custom_call_target="tpu_custom_call" | custom-call | bytes 3649540 | tf_op jit(solution)/shard_map/pack/pallas_call | solution.py:35
  6.4 1.4 %copy.9 = f32[2,36,1872]{2,0,1:T(2,128)S(1)} copy(f32[2,36,1872]{2,1,0:T(8,128)} %get-tuple-element.22) | data formatting | bytes 1078272 | tf_op jit(solution)/shard_map/pack/pallas_call | solution.py:35
  7.8 3.0 %collective-permute-start.2 = (f32[2,36,1872]{2,0,1:T(2,128)S(1)}, f32[2,36,1872]{2,0,1:T(2,128)S(1)}, u32[]{:S(2)}, u32[]{:S(2)}) collective-permute-start(f32[2,36,1872]{2,0,1:T(2,128)S(1)} %copy.9), channel_id=1, source_target_pairs={{0,8},{4,12},{8,16},{12,20},{16,24},{20,28},{24,0},{28,4},{1,9},{5... | collective-permute-start | bytes 1617416 | tf_op jit(solution)/shard_map/ppermute | solution.py:337
  10.9 1.4 %copy.8 = f32[2,36,1872]{2,0,1:T(2,128)S(1)} copy(f32[2,36,1872]{2,1,0:T(8,128)} %get-tuple-element.21) | data formatting | bytes 1078272 | tf_op jit(solution)/shard_map/pack/pallas_call | solution.py:35
  12.2 1.6 %collective-permute-start.1 = (f32[2,36,1872]{2,0,1:T(2,128)S(1)}, f32[2,36,1872]{2,0,1:T(2,128)S(1)}, u32[]{:S(2)}, u32[]{:S(2)}) collective-permute-start(f32[2,36,1872]{2,0,1:T(2,128)S(1)} %copy.8), channel_id=1, source_target_pairs={{0,16},{4,20},{8,24},{12,28},{16,0},{20,4},{24,8},{28,12},{1,17},{... | collective-permute-start | bytes 1617416 | tf_op jit(solution)/shard_map/ppermute | solution.py:337
  14.1 1.5 %collective-permute-start = (f32[2,36,1872]{2,0,1:T(2,128)S(1)}, f32[2,36,1872]{2,0,1:T(2,128)S(1)}, u32[]{:S(2)}, u32[]{:S(2)}) collective-permute-start(f32[2,36,1872]{2,0,1:T(2,128)S(1)} %copy.7), channel_id=1, source_target_pairs={{0,24},{4,28},{8,0},{12,4},{16,8},{20,12},{24,16},{28,20},{1,25},{... | collective-permute-start | bytes 1617416 | tf_op jit(solution)/shard_map/ppermute | solution.py:337
  15.6 1.1 fusion
  16.7 3.7 %collective-permute-start.4 = (f32[2,4,5184]{2,1,0:T(4,128)S(1)}, f32[2,4,5184]{2,1,0:T(4,128)S(1)}, u32[]{:S(2)}, u32[]{:S(2)}) collective-permute-start(f32[2,4,5184]{2,1,0:T(4,128)S(1)} %get-tuple-element.33), channel_id=1, source_target_pairs={{1,0},{2,1},{3,2},{0,3},{5,4},{6,5},{7,6},{4,7},{9,8},{10,9},{11,1... | collective-permute-start | bytes 497672 | tf_op jit(solution)/shard_map/ppermute | solution.py:346
  20.3 4.5 %collective-permute-done.4.refs_2_ = f32[2,4,5184]{2,1,0:T(4,128)S(1)} collective-permute-done((f32[2,4,5184]{2,1,0:T(4,128)S(1)}, f32[2,4,5184]{2,1,0:T(4,128)S(1)}, u32[]{:S(2)}, u32[]{:S(2)}) %collective-permute-start.4) | collective-permute-done | bytes 165920 | tf_op jit(solution)/shard_map/ppermute | solution.py:346
  24.9 2.9 %collective-permute-done.3.refs_1_ = f32[2,4,5184]{2,1,0:T(4,128)} collective-permute-done((f32[2,4,5184]{2,1,0:T(4,128)S(1)}, f32[2,4,5184]{2,1,0:T(4,128)}, u32[]{:S(2)}, u32[]{:S(2)}) %collective-permute-start.3) | collective-permute-done | bytes 165920 | tf_op jit(solution)/shard_map/ppermute | solution.py:345
  27.8 2.2 %pack.3 = (f32[2,8,1872]{2,1,0:T(8,128)}, f32[2,8,1872]{2,1,0:T(8,128)}, f32[2,8,1872]{2,1,0:T(8,128)}, f32[2,8,1872]{2,1,0:T(8,128)}) custom-call(s32[1]{0:T(128)} %bitcast.refs_0_.chip_ref, f32[2,4,5184]{2,1,0:T(4,128)} %collective-permute-done.3.refs_1_, f32[2,4,5184]{2,1,0:T(4,128)} %copy-done.5), custom_call_target="tpu_custom_call" | custom-call | bytes 811012 | tf_op jit(solution)/shard_map/pack/pallas_call | solution.py:35
  30.6 1.5 %collective-permute-start.6 = (f32[2,8,1872]{2,1,0:T(8,128)}, f32[2,8,1872]{2,1,0:T(8,128)}, u32[]{:S(2)}, u32[]{:S(2)}) collective-permute-start(f32[2,8,1872]{2,1,0:T(8,128)} %get-tuple-element.25), channel_id=1, source_target_pairs={{0,16},{4,20},{8,24},{12,28},{16,0},{20,4},{24,8},{28,12},{1,17},{... | collective-permute-start | bytes 359432 | tf_op jit(solution)/shard_map/ppermute | solution.py:337
  33.5 2.8 %collective-permute-done.1 = f32[2,36,1872]{2,0,1:T(2,128)S(1)} collective-permute-done((f32[2,36,1872]{2,0,1:T(2,128)S(1)}, f32[2,36,1872]{2,0,1:T(2,128)S(1)}, u32[]{:S(2)}, u32[]{:S(2)}) %collective-permute-start.1) | collective-permute-done | bytes 539168 | tf_op jit(solution)/shard_map/ppermute | solution.py:337
  37.6 0.9 copy.12.refs_1_
  38.5 1.7 %collective-permute-done.5.refs_5_ = f32[2,8,1872]{2,1,0:T(8,128)S(1)} collective-permute-done((f32[2,8,1872]{2,1,0:T(8,128)}, f32[2,8,1872]{2,1,0:T(8,128)S(1)}, u32[]{:S(2)}, u32[]{:S(2)}) %collective-permute-start.5) | collective-permute-done | bytes 119840 | tf_op jit(solution)/shard_map/ppermute | solution.py:337
  40.2 1.2 collective-permute-done.7.refs_7_
  42.1 3.8 %gather.1.planes = f32[44,8,1872]{2,1,0:T(8,128)} custom-call(f32[2,36,1872]{2,1,0:T(8,128)} %get-tuple-element.19.refs_0_, f32[2,36,1872]{2,1,0:T(8,128)} %copy.12.refs_1_, f32[2,36,1872]{2,1,0:T(8,128)} %copy.13.refs_2_, f32[2,36,1872]{2,1,0:T(8,128)} %copy.14.refs_3_, f32[2,8,1872]{2,1,0:T(8,128)} %get-tuple-element.23.refs_4_, f32[2,8,1872]{2,1,0:T(8,128)} %copy-done.6, ...), custom_call_target="tpu_custom_call" | custom-call | bytes 5271552 | tf_op jit(solution)/shard_map/gather/pallas_call | solution.py:35
  46.0 3.8 %weights.1.w_ref = bf16[7,768,256]{2,1,0:T(8,128)(2,1)} custom-call(), custom_call_target="tpu_custom_call" | custom-call | tf_op jit(solution)/shard_map/weights/pallas_call | solution.py:152
  49.7 10.2 %same.1.acc_in = f32[36,8,1536]{2,1,0:T(8,128)} custom-call(f32[44,8,1872]{2,1,0:T(8,128)} %gather.1.planes, bf16[7,768,256]{2,1,0:T(8,128)(2,1)} %weights.1.w_ref), custom_call_target="tpu_custom_call" | custom-call | flops 3875536896 | bytes 9910272 | tf_op jit(solution)/shard_map/same/pallas_call | solution.py:35
  59.9 1.5 %copy-done.8 = f32[44,8,1872]{2,1,0:T(8,128)} copy-done((f32[44,8,1872]{2,1,0:T(8,128)}, f32[44,8,1872]{2,1,0:T(8,128)S(1)}, u32[]{:S(2)}) %copy-start.8) | copy-done | bytes 2635800
  61.4 19.5 %cross.1 = (f32[36,8,1536]{2,1,0:T(8,128)}, f32[36,8,1536]{2,1,0:T(8,128)}) custom-call(s32[1]{0:T(128)} %bitcast.1.core_ref, f32[44,8,1872]{2,1,0:T(8,128)} %gather.1.planes, bf16[7,768,256]{2,1,0:T(8,128)(2,1)} %weights.1.w_ref, f32[36,8,1536]{2,1,0:T(8,128)} %same.1.acc_in, f32[44,8,1872]{2,1,0:T(8,128)} %copy-done.8), custom_call_target="tpu_custom_call" | custom-call | flops 7751073792 | bytes 16084996 | tf_op jit(solution)/shard_map/cross/pallas_call | solution.py:35
  80.9 1.5 %slice.11 = f32[36,8,1328]{2,1,0:T(8,128)S(1)} slice(f32[36,8,1536]{2,1,0:T(8,128)} %get-tuple-element.28), slice={[0:36], [0:8], [128:1456]} | slice | bytes 3059712 | tf_op jit(solution)/shard_map/slice | solution.py:391
  83.0 11.2 %same_swapped.1.refs_0_ = f32[36,8,1536]{2,1,0:T(8,128)} custom-call(f32[44,8,1872]{2,1,0:T(8,128)} %gather.1.planes, bf16[7,768,256]{2,1,0:T(8,128)(2,1)} %weights.1.w_ref, f32[36,8,1536]{2,1,0:T(8,128)} %get-tuple-element.27.refs_0_), custom_call_target="tpu_custom_call" | custom-call | flops 3875536896 | bytes 11679744 | tf_op jit(solution)/shard_map/same_swapped/pallas_call | solution.py:35
  94.2 1.2 copy-done
  95.4 3.4 %split.1 = (f32[2,36,1328]{2,1,0:T(8,128)}, f32[2,36,1328]{2,1,0:T(8,128)}, f32[2,36,1328]{2,1,0:T(8,128)}, f32[2,36,1328]{2,1,0:T(8,128)}) custom-call(f32[36,8,1536]{2,1,0:T(8,128)} %same_swapped.1.refs_0_, f32[36,8,1328]{2,1,0:T(8,128)} %copy-done), custom_call_target="tpu_custom_call" | custom-call | bytes 4829184 | tf_op jit(solution)/shard_map/split/pallas_call | solution.py:35
  98.8 3.9 %collective-permute-start.10 = (f32[2,36,1328]{2,1,0:T(8,128)}, f32[2,36,1328]{2,1,0:T(8,128)S(1)}, u32[]{:S(2)}, u32[]{:S(2)}) collective-permute-start(f32[2,36,1328]{2,1,0:T(8,128)} %get-tuple-element.30), channel_id=1, source_target_pairs={{0,8},{4,12},{8,16},{12,20},{16,24},{20,28},{24,0},{28,4},{1,9},{5... | collective-permute-start | bytes 1147400 | tf_op jit(solution)/shard_map/ppermute | solution.py:337
  102.9 1.3 %collective-permute-start.12 = (f32[2,36,1328]{2,1,0:T(8,128)}, f32[2,36,1328]{2,1,0:T(8,128)S(1)}, u32[]{:S(2)}, u32[]{:S(2)}) collective-permute-start(f32[2,36,1328]{2,1,0:T(8,128)} %get-tuple-element.32), channel_id=1, source_target_pairs={{0,24},{4,28},{8,0},{12,4},{16,8},{20,12},{24,16},{28,20},{1,25},{... | collective-permute-start | bytes 1147400 | tf_op jit(solution)/shard_map/ppermute | solution.py:337
  104.2 9.6 %collective-permute-done.10.refs_1_ = f32[2,36,1328]{2,1,0:T(8,128)S(1)} collective-permute-done((f32[2,36,1328]{2,1,0:T(8,128)}, f32[2,36,1328]{2,1,0:T(8,128)S(1)}, u32[]{:S(2)}, u32[]{:S(2)}) %collective-permute-start.10) | collective-permute-done | bytes 382496 | tf_op jit(solution)/shard_map/ppermute | solution.py:337
  113.8 8.9 %collective-permute-done.11.refs_2_ = f32[2,36,1328]{2,1,0:T(8,128)S(1)} collective-permute-done((f32[2,36,1328]{2,1,0:T(8,128)}, f32[2,36,1328]{2,1,0:T(8,128)S(1)}, u32[]{:S(2)}, u32[]{:S(2)}) %collective-permute-start.11) | collective-permute-done | bytes 382496 | tf_op jit(solution)/shard_map/ppermute | solution.py:337
  124.0 3.3 %place.1 = f32[2,36,5184]{2,1,0:T(8,128)} custom-call(s32[1]{0:T(128)} %bitcast.refs_0_.chip_ref, f32[2,36,1328]{2,1,0:T(8,128)} %get-tuple-element.29.refs_0_, f32[2,36,1328]{2,1,0:T(8,128)} %copy-done.2, f32[2,36,1328]{2,1,0:T(8,128)} %copy-done.3, f32[2,36,1328]{2,1,0:T(8,128)} %copy-done.4), custom_call_target="tpu_custom_call" | custom-call | bytes 3022852 | tf_op jit(solution)/shard_map/place/pallas_call | solution.py:35
  127.2 3.3 %copy.15 = f32[2,36,5184]{2,0,1:T(2,128)} copy(f32[2,36,5184]{2,1,0:T(8,128)} %place.1) | data formatting | bytes 2985984 | tf_op jit(solution)/shard_map/place/pallas_call | solution.py:35
  (31 shorter events, 6.1 us)
Async XLA Ops:
  6.4 7.4 %copy-start.1 = (f32[2,36,1872]{2,1,0:T(8,128)S(1)}, f32[2,36,1872]{2,1,0:T(8,128)}, u32[]{:S(2)}) copy-start(f32[2,36,1872]{2,1,0:T(8,128)} %get-tuple-element.20) | copy-start | bytes 1617412
  7.8 24.3 %collective-permute-start.2 = (f32[2,36,1872]{2,0,1:T(2,128)S(1)}, f32[2,36,1872]{2,0,1:T(2,128)S(1)}, u32[]{:S(2)}, u32[]{:S(2)}) collective-permute-start(f32[2,36,1872]{2,0,1:T(2,128)S(1)} %copy.9), channel_id=1, source_target_pairs={{0,8},{4,12},{8,16},{12,20},{16,24},{20,28},{24,0},{28,4},{1,9},{5... | collective-permute-start | bytes 1617416 | tf_op jit(solution)/shard_map/ppermute | solution.py:337
  12.2 24.1 %collective-permute-start.1 = (f32[2,36,1872]{2,0,1:T(2,128)S(1)}, f32[2,36,1872]{2,0,1:T(2,128)S(1)}, u32[]{:S(2)}, u32[]{:S(2)}) collective-permute-start(f32[2,36,1872]{2,0,1:T(2,128)S(1)} %copy.8), channel_id=1, source_target_pairs={{0,16},{4,20},{8,24},{12,28},{16,0},{20,4},{24,8},{28,12},{1,17},{... | collective-permute-start | bytes 1617416 | tf_op jit(solution)/shard_map/ppermute | solution.py:337
  14.1 23.5 %collective-permute-start = (f32[2,36,1872]{2,0,1:T(2,128)S(1)}, f32[2,36,1872]{2,0,1:T(2,128)S(1)}, u32[]{:S(2)}, u32[]{:S(2)}) collective-permute-start(f32[2,36,1872]{2,0,1:T(2,128)S(1)} %copy.7), channel_id=1, source_target_pairs={{0,24},{4,28},{8,0},{12,4},{16,8},{20,12},{24,16},{28,20},{1,25},{... | collective-permute-start | bytes 1617416 | tf_op jit(solution)/shard_map/ppermute | solution.py:337
  16.7 8.2 %collective-permute-start.4 = (f32[2,4,5184]{2,1,0:T(4,128)S(1)}, f32[2,4,5184]{2,1,0:T(4,128)S(1)}, u32[]{:S(2)}, u32[]{:S(2)}) collective-permute-start(f32[2,4,5184]{2,1,0:T(4,128)S(1)} %get-tuple-element.33), channel_id=1, source_target_pairs={{1,0},{2,1},{3,2},{0,3},{5,4},{6,5},{7,6},{4,7},{9,8},{10,9},{11,1... | collective-permute-start | bytes 497672 | tf_op jit(solution)/shard_map/ppermute | solution.py:346
  20.3 7.5 %collective-permute-start.3 = (f32[2,4,5184]{2,1,0:T(4,128)S(1)}, f32[2,4,5184]{2,1,0:T(4,128)}, u32[]{:S(2)}, u32[]{:S(2)}) collective-permute-start(f32[2,4,5184]{2,1,0:T(4,128)S(1)} %get-tuple-element.34), channel_id=1, source_target_pairs={{0,1},{1,2},{2,3},{3,0},{4,5},{5,6},{6,7},{7,4},{8,9},{9,10},{10,1... | collective-permute-start | bytes 497672 | tf_op jit(solution)/shard_map/ppermute | solution.py:345
  24.9 2.9 %copy-start.5 = (f32[2,4,5184]{2,1,0:T(4,128)}, f32[2,4,5184]{2,1,0:T(4,128)S(1)}, u32[]{:S(2)}) copy-start(f32[2,4,5184]{2,1,0:T(4,128)S(1)} %collective-permute-done.4.refs_2_) | copy-start | bytes 497668
  30.1 10.2 %collective-permute-start.5 = (f32[2,8,1872]{2,1,0:T(8,128)}, f32[2,8,1872]{2,1,0:T(8,128)S(1)}, u32[]{:S(2)}, u32[]{:S(2)}) collective-permute-start(f32[2,8,1872]{2,1,0:T(8,128)} %get-tuple-element.24), channel_id=1, source_target_pairs={{0,24},{4,28},{8,0},{12,4},{16,8},{20,12},{24,16},{28,20},{1,25},{... | collective-permute-start | bytes 359432 | tf_op jit(solution)/shard_map/ppermute | solution.py:337
  30.6 9.6 %collective-permute-start.6 = (f32[2,8,1872]{2,1,0:T(8,128)}, f32[2,8,1872]{2,1,0:T(8,128)}, u32[]{:S(2)}, u32[]{:S(2)}) collective-permute-start(f32[2,8,1872]{2,1,0:T(8,128)} %get-tuple-element.25), channel_id=1, source_target_pairs={{0,16},{4,20},{8,24},{12,28},{16,0},{20,4},{24,8},{28,12},{1,17},{... | collective-permute-start | bytes 359432 | tf_op jit(solution)/shard_map/ppermute | solution.py:337
  32.1 9.4 %collective-permute-start.7 = (f32[2,8,1872]{2,1,0:T(8,128)}, f32[2,8,1872]{2,1,0:T(8,128)S(1)}, u32[]{:S(2)}, u32[]{:S(2)}) collective-permute-start(f32[2,8,1872]{2,1,0:T(8,128)} %get-tuple-element.26), channel_id=1, source_target_pairs={{0,8},{4,12},{8,16},{12,20},{16,24},{20,28},{24,0},{28,4},{1,9},{5... | collective-permute-start | bytes 359432 | tf_op jit(solution)/shard_map/ppermute | solution.py:337
  40.2 1.3 copy-start.6
  41.5 0.7 copy-start.7
  46.0 13.9 %collective-permute-start.8 = (f32[44,8,1872]{2,1,0:T(8,128)}, f32[44,8,1872]{2,1,0:T(8,128)S(1)}, u32[]{:S(2)}, u32[]{:S(2)}) collective-permute-start(f32[44,8,1872]{2,1,0:T(8,128)} %gather.1.planes), channel_id=1, source_target_pairs={{0,4},{4,0},{8,12},{12,8},{16,20},{20,16},{24,28},{28,24},{1,5},{5... | collective-permute-start | bytes 7907336 | tf_op jit(solution)/shard_map/ppermute | solution.py:340
  59.9 1.5 %copy-start.8 = (f32[44,8,1872]{2,1,0:T(8,128)}, f32[44,8,1872]{2,1,0:T(8,128)S(1)}, u32[]{:S(2)}) copy-start(f32[44,8,1872]{2,1,0:T(8,128)S(1)} %collective-permute-done.8.flat) | copy-start | bytes 7907332
  82.4 11.8 %collective-permute-start.9 = (f32[36,8,1328]{2,1,0:T(8,128)S(1)}, f32[36,8,1328]{2,1,0:T(8,128)S(1)}, u32[]{:S(2)}, u32[]{:S(2)}) collective-permute-start(f32[36,8,1328]{2,1,0:T(8,128)S(1)} %slice.11), channel_id=1, source_target_pairs={{0,4},{4,0},{8,12},{12,8},{16,20},{20,16},{24,28},{28,24},{1,5},{5... | collective-permute-start | bytes 4589576 | tf_op jit(solution)/shard_map/ppermute | solution.py:340
  94.2 1.2 copy-start
  98.8 14.9 %collective-permute-start.10 = (f32[2,36,1328]{2,1,0:T(8,128)}, f32[2,36,1328]{2,1,0:T(8,128)S(1)}, u32[]{:S(2)}, u32[]{:S(2)}) collective-permute-start(f32[2,36,1328]{2,1,0:T(8,128)} %get-tuple-element.30), channel_id=1, source_target_pairs={{0,8},{4,12},{8,16},{12,20},{16,24},{20,28},{24,0},{28,4},{1,9},{5... | collective-permute-start | bytes 1147400 | tf_op jit(solution)/shard_map/ppermute | solution.py:337
  102.7 20.0 %collective-permute-start.11 = (f32[2,36,1328]{2,1,0:T(8,128)}, f32[2,36,1328]{2,1,0:T(8,128)S(1)}, u32[]{:S(2)}, u32[]{:S(2)}) collective-permute-start(f32[2,36,1328]{2,1,0:T(8,128)} %get-tuple-element.31), channel_id=1, source_target_pairs={{0,16},{4,20},{8,24},{12,28},{16,0},{20,4},{24,8},{28,12},{1,17},{... | collective-permute-start | bytes 1147400 | tf_op jit(solution)/shard_map/ppermute | solution.py:337
  102.9 20.3 %collective-permute-start.12 = (f32[2,36,1328]{2,1,0:T(8,128)}, f32[2,36,1328]{2,1,0:T(8,128)S(1)}, u32[]{:S(2)}, u32[]{:S(2)}) collective-permute-start(f32[2,36,1328]{2,1,0:T(8,128)} %get-tuple-element.32), channel_id=1, source_target_pairs={{0,24},{4,28},{8,0},{12,4},{16,8},{20,12},{24,16},{28,20},{1,25},{... | collective-permute-start | bytes 1147400 | tf_op jit(solution)/shard_map/ppermute | solution.py:337
  113.8 9.4 %copy-start.2 = (f32[2,36,1328]{2,1,0:T(8,128)}, f32[2,36,1328]{2,1,0:T(8,128)S(1)}, u32[]{:S(2)}) copy-start(f32[2,36,1328]{2,1,0:T(8,128)S(1)} %collective-permute-done.10.refs_1_) | copy-start | bytes 1147396
  122.7 0.8 copy-start.3
  123.2 0.8 copy-start.4

commit v3 on v0

v3 whole, which is shorter than its diff:
```python
import functools

import jax
import jax.numpy as jnp
from jax import lax
from jax.experimental import pallas as pl
from jax.experimental.pallas import tpu as pltpu
from jax.sharding import PartitionSpec as P


NY = 72
LANES = 128
TILE = 256
WINDOW = 3 * TILE
REACH = 2
HALO = 4
STEP = 4
CENTRE = 8.5
DIAGONAL = 12.0 * CENTRE
SCALE = -1.0 / (CENTRE * DIAGONAL * DIAGONAL)
VMEM = pl.BlockSpec(memory_space=pltpu.VMEM)
SMEM = pl.BlockSpec(memory_space=pltpu.SMEM)
ANY = pl.BlockSpec(memory_space=pl.ANY)


def sds(*shape):
    return jax.ShapeDtypeStruct(shape, jnp.float32)


def call(body, out, inputs, scratch=(), flops=0, smem=False, after=None, limit=12):
    nbytes = sum(4 * x.size for x in inputs) + sum(4 * o.size for o in out)
    specs = [VMEM] * len(inputs)
    if smem:
        specs[0] = SMEM
    if after is not None:
        inner = body
        inputs = [*inputs, after]
        specs.append(ANY)
        skip = len(inputs) - 1

        def body(*refs):
            inner(*refs[:skip], *refs[skip + 1 :])

    return pl.pallas_call(
        body,
        out_shape=out,
        in_specs=specs,
        out_specs=[VMEM] * len(out),
        scratch_shapes=scratch,
        compiler_params=pltpu.CompilerParams(vmem_limit_bytes=limit << 20),
        cost_estimate=pl.CostEstimate(flops=flops, bytes_accessed=nbytes, transcendentals=0),
    )(*inputs)


def floor_to(value, unit):
    return value // unit * unit


def ceil_to(value, unit):
    return -(-value // unit) * unit


class Ranges:
    def __init__(self, chips, total):
        self.chips = chips
        self.total = total
        self.width = total // chips
        self.halo = HALO * NY
        starts = [j * self.width - self.halo for j in range(chips)]
        self.starts = [floor_to(s, LANES) for s in starts]
        shifts = [s - a for s, a in zip(starts, self.starts)]
        low, high = min(shifts), max(shifts)
        used = self.width + 2 * self.halo
        self.length = ceil_to(high + used, LANES)
        reach = REACH * NY
        self.first = floor_to(low + reach, LANES)
        self.n_first = ceil_to(high + used - reach - self.first, TILE) // TILE
        self.second = floor_to(low + 2 * reach, LANES)
        self.n_second = ceil_to(high + used - 2 * reach - self.second, TILE) // TILE
        self.out_starts = [floor_to(j * self.width, LANES) for j in range(chips)]
        self.out_length = max(
            ceil_to((j + 1) * self.width, LANES) - s for j, s in enumerate(self.out_starts)
        )

    def shift(self, chip):
        start = chip * self.width - self.halo + ceil_to(self.halo, LANES)
        return lax.rem(start, LANES)

    def out_at(self, chip):
        start = chip * self.width
        return lax.div(start, LANES) * LANES - (start - self.halo - self.shift(chip)) - self.second

    @property
    def pad(self):
        return max(0, TILE - self.first)

    @property
    def split_length(self):
        ends = (
            self.pad + self.first - TILE + self.n_first * TILE + WINDOW - TILE,
            self.pad + self.second - TILE + self.n_second * TILE + WINDOW - TILE,
            self.pad + self.first + self.n_first * TILE,
            self.pad + self.length,
        )
        return ceil_to(max(ends), LANES)

    @property
    def full_length(self):
        return max(
            self.first + self.n_first * TILE, self.second + self.n_second * TILE, self.length
        )


def pack_body(ranges, chip_ref, *refs):
    chips, total, length = ranges.chips, ranges.total, ranges.length
    ins, outs = refs[:-chips], refs[-chips:]
    chip = chip_ref[0]
    for ahead in range(chips):
        for target in range(chips):

            @pl.when(lax.rem(chip + ahead, chips) == target)
            def _(ahead=ahead, start=ranges.starts[target]):
                row = 0
                for ref in ins:

                    def plane(z, _, ref=ref, row=row):
                        lo, hi = start, start + length
                        pieces = []
                        if lo < 0:
                            pieces.append(ref[z, :, lo + total : total])
                        pieces.append(ref[z, :, max(lo, 0) : min(hi, total)])
                        if hi > total:
                            pieces.append(ref[z, :, 0 : hi - total])
                        value = pieces[0] if len(pieces) == 1 else jnp.concatenate(pieces, axis=-1)
                        outs[ahead][row + z] = value
                        return 0

                    lax.fori_loop(0, ref.shape[0], plane, 0)
                    row += ref.shape[0]


def pack(ranges, chip, pieces):
    orbs = pieces[0].shape[1]
    rows = sum(p.shape[0] for p in pieces)
    return call(
        functools.partial(pack_body, ranges),
        [sds(rows, orbs, ranges.length)] * ranges.chips,
        [chip, *pieces],
        smem=True,
    )


def gather_body(*refs):
    ins, out = refs[:-1], refs[-1]
    orbs = ins[0].shape[1]

    def plane(z, _):
        for slot, ref in enumerate(ins):
            out[z, slot * orbs : (slot + 1) * orbs, :] = ref[z]
        return 0

    lax.fori_loop(0, out.shape[0], plane, 0)


def gather(pieces, after=None):
    depth, orbs, span = pieces[0].shape
    return call(gather_body, [sds(depth, orbs * len(pieces), span)], pieces, after=after)[0]


def roll_rows(value, shift):
    if isinstance(shift, int):
        shift = shift % value.shape[1]
        if shift == 0:
            return value
    return pltpu.roll(value, shift, 1)


class Pairing:
    def __init__(self, rows, even, odd=None):
        self.rows, self.even, self.odd = rows, even, odd

    def apply(self, value, even, odd):
        if odd is None:
            return roll_rows(value, even)
        row = lax.broadcasted_iota(jnp.int32, value.shape, 1)
        return jnp.where(row % 2 == 0, roll_rows(value, even), roll_rows(value, odd))

    def negative(self, shift):
        return -shift if isinstance(shift, int) else lax.rem(self.rows - shift, self.rows)

    def partner(self, value):
        return self.apply(value, self.even, self.odd)

    def back(self, value):
        if self.odd is None:
            return self.apply(value, self.negative(self.even), None)
        return self.apply(value, self.negative(self.odd), self.negative(self.even))


def weights_body(ranges, chip_ref, out):
    i = lax.broadcasted_iota(jnp.int32, (WINDOW, TILE), 0)
    lane = lax.broadcasted_iota(jnp.int32, (1, TILE), 1)
    shift = ranges.shift(chip_ref[0])
    at = lane + TILE

    def tile(t, start, diagonal):
        y = lax.rem(lane + (start + 2 * NY) - shift, NY)
        near = (i == at - NY) | (i == at + NY)
        far = (i == at - 2 * NY) | (i == at + 2 * NY)

        def beside(step):
            wrap = jnp.where(y + step >= NY, NY, jnp.where(y + step < 0, -NY, 0))
            return i == at + step - wrap

        near = near | beside(1) | beside(-1)
        far = far | beside(2) | beside(-2)
        value = jnp.where(i == at, diagonal, 0.0)
        value = jnp.where(near, 16.0, jnp.where(far, -1.0, value))
        out[t] = value.astype(jnp.bfloat16)

    def first(t, _):
        tile(t, ranges.first + t * TILE, DIAGONAL)
        return 0

    def second(t, _):
        tile(ranges.n_first + t, ranges.second + t * TILE, 0.0)
        return 0

    lax.fori_loop(0, ranges.n_first, first, 0)
    lax.fori_loop(0, ranges.n_second, second, 0)


def weights(ranges, chip):
    shape = (ranges.n_first + ranges.n_second, WINDOW, TILE)
    return pl.pallas_call(
        functools.partial(weights_body, ranges),
        out_shape=jax.ShapeDtypeStruct(shape, jnp.bfloat16),
        in_specs=[SMEM],
        out_specs=VMEM,
        name="weights",
    )(chip)


def store_halves(ref, rows, lanes, value):
    high = value.astype(jnp.bfloat16)
    ref[0, rows, lanes] = high
    ref[1, rows, lanes] = (value - high.astype(jnp.float32)).astype(jnp.bfloat16)


def aligned(start, size):
    if isinstance(start, int):
        return slice(start, start + size)
    return pl.ds(pl.multiple_of(start, LANES), size)


def tiles(count, product, use, buffer):
    def tile(t, _):
        product(t, buffer)
        use(t, buffer)
        return 0

    lax.fori_loop(0, count, tile, 0)


def potentials(ranges, first, second, pairing, w_ref, work, finish):
    rho_split, rho, mid_split, mid, product = work
    main, _ = first
    inner, n_rows, span = main.shape
    pad = ranges.pad

    def density(part, z, row):
        rows = pl.ds(row, STEP * n_rows)
        for lo in range(0, span, LANES):
            lanes = slice(lo, lo + LANES)
            value = first[part][pl.ds(z, STEP), :, lanes]
            value = value * pairing.partner(second[part][pl.ds(z, STEP), :, lanes])
            value = value.reshape(STEP * n_rows, LANES)
            store_halves(rho_split, rows, slice(lo + pad, lo + pad + LANES), value)
            rho[rows, lanes] = value

    density(1, 0, 0)

    def chunk(s, _):
        z = pl.multiple_of(s * STEP, STEP)
        density(0, z, pl.multiple_of(s * (STEP * n_rows) + HALO * n_rows, STEP * n_rows))
        return 0

    lax.fori_loop(0, inner // STEP, chunk, 0)
    density(1, HALO, (HALO + inner) * n_rows)

    def in_plane(source, planes, start, weight, out):
        lanes = aligned(start - TILE + pad, WINDOW)
        rows = planes * n_rows
        value = source[:, REACH * n_rows : REACH * n_rows + rows, lanes].reshape(2 * rows, WINDOW)
        out[0 : 2 * rows] = jnp.dot(value, weight, preferred_element_type=jnp.float32)

    def off(source, planes, start, inside):
        rows = planes * n_rows

        def shifted(z):
            return source[z * n_rows : z * n_rows + rows, aligned(start, TILE)]

        near = shifted(1) + shifted(3)
        far = shifted(0) + shifted(4)
        return (inside[0:rows] + inside[rows : 2 * rows]) + (16.0 * near - far)

    swept = inner + 2 * REACH

    def product_1(t, out):
        in_plane(rho_split, swept, ranges.first + t * TILE, w_ref[t], out)

    def use_1(t, inside):
        start = ranges.first + t * TILE
        value = off(rho, swept, start, inside)
        rows = slice(0, swept * n_rows)
        mid[rows, aligned(start, TILE)] = value
        store_halves(mid_split, rows, aligned(start + pad, TILE), value)

    tiles(ranges.n_first, product_1, use_1, product)

    def product_2(t, out):
        in_plane(mid_split, inner, ranges.second + t * TILE, w_ref[t + ranges.n_first], out)

    def use_2(t, inside):
        start = ranges.second + t * TILE
        here = aligned(start, TILE)
        value = off(mid, inner, start, inside)
        value = value + (DIAGONAL * DIAGONAL) * rho[HALO * n_rows : (HALO + inner) * n_rows, here]
        finish(here, aligned(t * TILE, TILE), value.reshape(inner, n_rows, TILE))

    tiles(ranges.n_second, product_2, use_2, product)


def clear(ranges, work):
    rho_split, rho, mid_split, mid = work[:4]
    span = ranges.length

    def zero(ref, lo, hi):
        if lo < hi:
            shape = ref.shape[:-1] + (hi - lo,)
            ref[..., lo:hi] = jnp.zeros(shape, ref.dtype)

    pad, end = ranges.pad, ranges.split_length
    zero(rho_split, 0, pad)
    zero(rho_split, pad + span, end)
    zero(rho, span, rho.shape[-1])
    zero(mid_split, 0, pad + ranges.first)
    zero(mid_split, pad + ranges.first + ranges.n_first * TILE, end)
    zero(mid, 0, ranges.first)
    zero(mid, ranges.first + ranges.n_first * TILE, mid.shape[-1])


def same_body(ranges, swapped, final, main, edge, w_ref, *refs):
    acc_in = refs[0] if final else None
    acc, *work = refs[1:] if final else refs
    n_rows = main.shape[1]
    pairing = Pairing(n_rows, 1, 3) if swapped else Pairing(n_rows, 2)

    def finish(here, lanes, value):
        mine = main[:, :, here]
        total = value * pairing.partner(mine) + pairing.back(value * mine)
        if final:
            total = (total + acc_in[:, :, lanes]) * SCALE
        acc[:, :, lanes] = total

    clear(ranges, work)
    planes = (main, edge)
    potentials(ranges, planes, planes, pairing, w_ref, work, finish)


def cross_body(ranges, core_ref, main, edge, w_ref, acc_in, other, other_edge, acc, travel, *work):
    n_rows = main.shape[1]
    odd = core_ref[0] == 1
    straight = Pairing(n_rows, jnp.where(odd, 0, 2))
    swapped = Pairing(n_rows, jnp.where(odd, n_rows - 1, 1), jnp.where(odd, 1, 3))

    def finish_straight(here, lanes, value):
        acc[:, :, lanes] = acc_in[:, :, lanes] + value * straight.partner(other[:, :, here])
        travel[:, :, lanes] = straight.back(value * main[:, :, here])

    def finish_swapped(here, lanes, value):
        acc[:, :, lanes] = acc[:, :, lanes] + value * swapped.partner(other[:, :, here])
        total = travel[:, :, lanes] + swapped.back(value * main[:, :, here])
        travel[:, :, lanes] = total * SCALE

    clear(ranges, work)
    planes, others = (main, edge), (other, other_edge)
    potentials(ranges, planes, others, straight, w_ref, work, finish_straight)
    potentials(ranges, planes, others, swapped, w_ref, work, finish_swapped)


def split_body(ranges, chip_ref, mine, theirs, *outs):
    orbs = outs[0].shape[1]
    lanes = aligned(ranges.out_at(chip_ref[0]), ranges.out_length)

    def plane(z, _):
        value = mine[z, :, lanes] + theirs[z, :, lanes]
        for slot, out in enumerate(outs):
            out[z] = value[slot * orbs : (slot + 1) * orbs]
        return 0

    lax.fori_loop(0, outs[0].shape[0], plane, 0)


def place_body(ranges, chip_ref, *refs):
    chips = ranges.chips
    ins, out = refs[:chips], refs[chips]
    chip = chip_ref[0]
    for behind in range(chips):
        for source in range(chips):

            @pl.when(lax.rem(chip + chips - behind, chips) == source)
            def _(ref=ins[behind], source=source):
                base = ranges.out_starts[source]
                lo, hi = source * ranges.width, (source + 1) * ranges.width

                def plane(z, _):
                    at = lo
                    while at < hi:
                        stop = min(floor_to(at, LANES) + LANES, hi)
                        if at % LANES == 0:
                            whole = max(floor_to(hi, LANES), stop)
                            stop = whole
                        out[z, :, at:stop] = ref[z, :, at - base : stop - base]
                        at = stop
                    return 0

                lax.fori_loop(0, out.shape[0], plane, 0)


def per_device(n_band, orbitals):
    orbs, depth, total = orbitals.shape
    chips = n_band // 2
    ranges = Ranges(chips, total)
    index = lax.axis_index("band")
    chip = (index // 2).astype(jnp.int32).reshape(1)
    core = (index % 2).astype(jnp.int32).reshape(1)
    planes = jnp.transpose(orbitals, (1, 0, 2))

    def along(value, steps):
        pairs = [(i, (i + 2 * steps) % n_band) for i in range(n_band)]
        return lax.ppermute(value, "band", pairs)

    def partner_core(value):
        return lax.ppermute(value, "band", [(i, i ^ 1) for i in range(n_band)])

    n_slab = lax.axis_size("slab")
    up = [(i, (i + 1) % n_slab) for i in range(n_slab)]
    down = [(j, i) for i, j in up]
    below = lax.ppermute(planes[depth - HALO :], "slab", up)
    above = lax.ppermute(planes[:HALO], "slab", down)

    order = [0] + list(range(chips - 1, 0, -1))

    def spread(pieces):
        sent = pack(ranges, chip, pieces)
        got = [sent[0]]
        for s in range(1, chips):
            got.append(along(sent[s], s))
        return [got[s] for s in order]

    banded = weights(ranges, chip)
    main = gather(spread([planes]), after=banded)
    edge = gather(spread([below, above]))
    other, other_edge = partner_core(main), partner_core(edge)

    rows = orbs * chips
    full, swept = (depth + 2 * HALO) * rows, (depth + 2 * REACH) * rows
    work = [
        pltpu.VMEM((2, full, ranges.split_length), jnp.bfloat16),
        pltpu.VMEM((full, ranges.full_length), jnp.float32),
        pltpu.VMEM((2, swept, ranges.split_length), jnp.bfloat16),
        pltpu.VMEM((swept, ranges.full_length), jnp.float32),
        pltpu.VMEM((2 * swept, TILE), jnp.float32),
    ]
    inner = sds(depth, rows, ranges.n_second * TILE)
    flops = 4 * WINDOW * TILE * (ranges.n_first + ranges.n_second) * full
    acc = call(
        functools.partial(same_body, ranges, False, False),
        [inner],
        [main, edge, banded],
        scratch=work,
        flops=flops,
        limit=40,
    )[0]
    acc, travel = call(
        functools.partial(cross_body, ranges),
        [inner, inner],
        [core, main, edge, banded, acc, other, other_edge],
        scratch=work,
        flops=2 * flops,
        smem=True,
        limit=40,
    )
    back = partner_core(travel)
    mine = call(
        functools.partial(same_body, ranges, True, True),
        [inner],
        [main, edge, banded, acc],
        scratch=work,
        flops=flops,
        limit=40,
    )[0]
    parts = call(
        functools.partial(split_body, ranges),
        [sds(depth, orbs, ranges.out_length)] * chips,
        [chip, mine, back],
        smem=True,
    )
    parts = [parts[0]] + [along(parts[s], s) for s in range(1, chips)]
    result = call(
        functools.partial(place_body, ranges), [sds(depth, orbs, total)], [chip, *parts], smem=True
    )[0]
    return jnp.transpose(result, (1, 0, 2))


def solution(mesh):
    def body(orbitals):
        return per_device(mesh.shape["band"], orbitals)

    return jax.shard_map(
        body,
        mesh=mesh,
        in_specs=(P("band", "slab", None),),
        out_specs=P("band", "slab", None),
        check_vma=False,
    )
```

time: 595 us -> 127 us (0.21); the launches traced: 585 us -> 127 us
  other arithmetic: 323 us -> 0.01 us
  local copies, waits for them, and re-layouts: 152 us -> 11.1 us
  Pallas kernels: 0 us -> 48.8 us
  waiting for transfers between devices: 87.6 us -> 50.5 us
    div x3 -> x0, other arithmetic: 203 us -> none  [the longest x2 200 us: per_device(): field = (density + trim_off(padded)) / centre_weight]
    slice x40 -> x1, local copies, waits for them, and re-layouts: 146 us -> 1.02 us  [per_device(): above = lax.ppermute(planes[:HALO], 'slab', down)]
    reduce_sum x1 -> x0, other arithmetic: 111 us -> none  [per_device(): total = -jnp.sum(field * block_ext[None], axis=1)]
    pallas_call x0 -> x10, Pallas kernels: none -> 48.8 us  [the longest x9 42.1 us: call(): pl.pallas_call(body, out_shape=out, in_specs=specs, out_specs=[VMEM] * le...]
    ppermute x12 -> x14, waiting for transfers between devices: 87.6 us -> 50.5 us  [the longest x9 41.7 us: along(): return lax.ppermute(value, 'band', pairs)]
    unnamed x21 -> x18, local copies, waits for them, and re-layouts: 2.2 us -> 10 us
    ppermute x12 -> x14, starting transfers between devices: 21.8 us -> 16 us  [the longest x9 11.7 us: along(): return lax.ppermute(value, 'band', pairs)]
  transfers between devices with their start and end apart: 12 -> 14, of which waited for: 8 -> 9; matrix products, arithmetic and copies ran while one was open for 20% -> 1% of each run, Pallas kernels for 0% -> 17%
where the time goes in v3:
time: 127 us
  waiting for transfers between devices  50.5 us (40%)
  Pallas kernels  48.8 us (38%)
  starting transfers between devices  16 us (13%)
  local copies, waits for them, and re-layouts  11.1 us (9%)
    pallas_call x9, Pallas kernels, call(): pl.pallas_call(body, out_shape=out, in_specs=specs, out_specs=[VMEM] * le...  42.1 us
    ppermute x9, waiting for transfers between devices, along(): return lax.ppermute(value, 'band', pairs)  41.7 us
    ppermute x9, starting transfers between devices, along(): return lax.ppermute(value, 'band', pairs)  11.7 us
    unnamed x18, local copies, waits for them, and re-layouts  10 us
    pallas_call x1, Pallas kernels, weights(): pl.pallas_call(functools.partial(weights_body, ranges), out_shape=jax.Sha...  6.75 us
    ppermute x1, waiting for transfers between devices, per_device(): above = lax.ppermute(planes[:HALO], 'slab', down)  4.72 us
    ppermute x1, waiting for transfers between devices, per_device(): below = lax.ppermute(planes[depth - HALO:], 'slab', up)  3.98 us
    ppermute x1, starting transfers between devices, per_device(): above = lax.ppermute(planes[:HALO], 'slab', down)  3.65 us
  transfers between devices with their start and end apart: 14, of which 9 were waited for; matrix products, arithmetic and copies ran while one was open for 1% of the time, Pallas kernels for 17%

profile of v3, /device:TPU:0, one launch (start us, length us, event | category | flops | bytes accessed | tf_op | source)
XLA Modules:
  0.0 126.5 jit_solution(705338355282332919)
XLA Ops:
  0.0 1.4 %copy-done.2 = f32[2,36,5184]{2,0,1:T(2,128)S(1)} copy-done((f32[2,36,5184]{2,0,1:T(2,128)S(1)}, f32[2,36,5184]{2,0,1:T(2,128)}, u32[]{:S(2)}) %copy-start.2) | copy-done | bytes 1493016
  1.4 6.9 %shard_map.17 = (f32[36,2,2048]{2,1,0:T(2,128)S(1)}, f32[36,2,2048]{2,1,0:T(2,128)S(1)}, f32[36,2,2048]{2,1,0:T(2,128)S(1)}, f32[36,2,2048]{2,1,0:T(2,128)}) custom-call(s32[1]{0:T(128)} %bitcast.chip_ref, f32[36,2,5184]{2,1,0:T(2,128)S(1)} %bitcast.7), custom_call_target="tpu_custom_call" | custom-call | bytes 3852292 | tf_op jit(solution)/shard_map/pallas_call | solution.py:44
  8.3 3.9 %collective-permute-start = (f32[36,2,2048]{2,1,0:T(2,128)}, f32[36,2,2048]{2,1,0:T(2,128)S(1)}, u32[]{:S(2)}, u32[]{:S(2)}) collective-permute-start(f32[36,2,2048]{2,1,0:T(2,128)} %get-tuple-element.20), channel_id=1, source_target_pairs={{0,24},{4,28},{8,0},{12,4},{16,8},{20,12},{24,16},{28,20},{1,25},{... | collective-permute-start | bytes 1769480 | tf_op jit(solution)/shard_map/ppermute | solution.py:442
  12.8 0.6 collective-permute-start.2
  13.3 6.7 %weights.1.refs_4_.w_ref = bf16[13,768,256]{2,1,0:T(8,128)(2,1)} custom-call(s32[1]{0:T(128)} %bitcast.chip_ref), custom_call_target="tpu_custom_call" | custom-call | tf_op jit(solution)/shard_map/weights/pallas_call | solution.py:235
  20.1 6.2 %collective-permute-done.refs_1_ = f32[36,2,2048]{2,1,0:T(2,128)S(1)} collective-permute-done((f32[36,2,2048]{2,1,0:T(2,128)}, f32[36,2,2048]{2,1,0:T(2,128)S(1)}, u32[]{:S(2)}, u32[]{:S(2)}) %collective-permute-start) | collective-permute-done | bytes 589856 | tf_op jit(solution)/shard_map/ppermute | solution.py:442
  26.3 13.4 %collective-permute-done.1.refs_2_ = f32[36,2,2048]{2,1,0:T(2,128)S(1)} collective-permute-done((f32[36,2,2048]{2,1,0:T(2,128)S(1)}, f32[36,2,2048]{2,1,0:T(2,128)S(1)}, u32[]{:S(2)}, u32[]{:S(2)}) %collective-permute-start.1) | collective-permute-done | bytes 589856 | tf_op jit(solution)/shard_map/ppermute | solution.py:442
  39.7 0.8 copy-done.3
  40.5 0.8 copy-done.5
  41.3 2.4 %copy-done = bf16[13,768,256]{2,1,0:T(8,128)(2,1)S(1)} copy-done((bf16[13,768,256]{2,1,0:T(8,128)(2,1)S(1)}, bf16[13,768,256]{2,1,0:T(8,128)(2,1)}, u32[]{:S(2)}) %copy-start) | copy-done | bytes 5111832
  43.8 1.1 copy-done.4
  44.8 1.1 copy-done.6
  45.9 0.7 shard_map.18.main
  46.7 1.0 fusion
  47.7 3.7 %collective-permute-start.4 = (f32[4,2,5184]{2,1,0:T(2,128)S(1)}, f32[4,2,5184]{2,1,0:T(2,128)S(1)}, u32[]{:S(2)}, u32[]{:S(2)}) collective-permute-start(f32[4,2,5184]{2,1,0:T(2,128)S(1)} %get-tuple-element.33), channel_id=1, source_target_pairs={{1,0},{2,1},{3,2},{0,3},{5,4},{6,5},{7,6},{4,7},{9,8},{10,9},{11,1... | collective-permute-start | bytes 497672 | tf_op jit(solution)/shard_map/ppermute | solution.py:451
  51.4 4.7 %collective-permute-done.4.refs_1_ = f32[4,2,5184]{2,1,0:T(2,128)S(1)} collective-permute-done((f32[4,2,5184]{2,1,0:T(2,128)S(1)}, f32[4,2,5184]{2,1,0:T(2,128)S(1)}, u32[]{:S(2)}, u32[]{:S(2)}) %collective-permute-start.4) | collective-permute-done | bytes 165920 | tf_op jit(solution)/shard_map/ppermute | solution.py:451
  56.1 4.0 %collective-permute-done.3.refs_0_ = f32[4,2,5184]{2,1,0:T(2,128)S(1)} collective-permute-done((f32[4,2,5184]{2,1,0:T(2,128)S(1)}, f32[4,2,5184]{2,1,0:T(2,128)S(1)}, u32[]{:S(2)}, u32[]{:S(2)}) %collective-permute-start.3) | collective-permute-done | bytes 165920 | tf_op jit(solution)/shard_map/ppermute | solution.py:450
  60.1 1.4 %shard_map.19 = (f32[8,2,2048]{2,1,0:T(2,128)S(1)}, f32[8,2,2048]{2,1,0:T(2,128)S(1)}, f32[8,2,2048]{2,1,0:T(2,128)S(1)}, f32[8,2,2048]{2,1,0:T(2,128)S(1)}) custom-call(s32[1]{0:T(128)} %bitcast.chip_ref, f32[4,2,5184]{2,1,0:T(2,128)S(1)} %collective-permute-done.3.refs_0_, f32[4,2,5184]{2,1,0:T(2,128)S(1)} %collective-permute-done.4.refs_1_), custom_call_target="tpu_custom_call" | custom-call | bytes 856068 | tf_op jit(solution)/shard_map/pallas_call | solution.py:44
  62.0 0.6 collective-permute-start.6
  62.6 1.4 %collective-permute-start.7 = (f32[8,2,2048]{2,1,0:T(2,128)S(1)}, f32[8,2,2048]{2,1,0:T(2,128)S(1)}, u32[]{:S(2)}, u32[]{:S(2)}) collective-permute-start(f32[8,2,2048]{2,1,0:T(2,128)S(1)} %get-tuple-element.26), channel_id=1, source_target_pairs={{0,8},{4,12},{8,16},{12,20},{16,24},{20,28},{24,0},{28,4},{1,9},{5... | collective-permute-start | bytes 393224 | tf_op jit(solution)/shard_map/ppermute | solution.py:442
  64.0 3.8 %collective-permute-done.5.refs_1_ = f32[8,2,2048]{2,1,0:T(2,128)S(1)} collective-permute-done((f32[8,2,2048]{2,1,0:T(2,128)S(1)}, f32[8,2,2048]{2,1,0:T(2,128)S(1)}, u32[]{:S(2)}, u32[]{:S(2)}) %collective-permute-start.5) | collective-permute-done | bytes 131104 | tf_op jit(solution)/shard_map/ppermute | solution.py:442
  67.8 1.8 %collective-permute-done.6.refs_2_ = f32[8,2,2048]{2,1,0:T(2,128)S(1)} collective-permute-done((f32[8,2,2048]{2,1,0:T(2,128)S(1)}, f32[8,2,2048]{2,1,0:T(2,128)S(1)}, u32[]{:S(2)}, u32[]{:S(2)}) %collective-permute-start.6) | collective-permute-done | bytes 131104 | tf_op jit(solution)/shard_map/ppermute | solution.py:442
  69.9 2.4 %copy-done.1 = bf16[13,768,256]{2,1,0:T(8,128)(2,1)S(1)} copy-done((bf16[13,768,256]{2,1,0:T(8,128)(2,1)S(1)}, bf16[13,768,256]{2,1,0:T(8,128)(2,1)}, u32[]{:S(2)}) %copy-start.1) | copy-done | bytes 5111832
  72.3 6.4 %shard_map.21.acc_in = f32[36,8,1536]{2,1,0:T(8,128)S(1)} custom-call(f32[36,8,2048]{2,1,0:T(8,128)S(1)} %shard_map.18.main, f32[8,8,2048]{2,1,0:T(8,128)S(1)} %shard_map.20.edge, bf16[13,768,256]{2,1,0:T(8,128)(2,1)S(1)} %copy-done.1), custom_call_target="tpu_custom_call" | custom-call | flops 3598712832 | bytes 14876672 | tf_op jit(solution)/shard_map/pallas_call | solution.py:44
  78.8 17.0 %shard_map.22 = (f32[36,8,1536]{2,1,0:T(8,128)S(1)}, f32[36,8,1536]{2,1,0:T(8,128)S(1)}) custom-call(s32[1]{0:T(128)} %bitcast.2.core_ref, f32[36,8,2048]{2,1,0:T(8,128)S(1)} %shard_map.18.main, f32[8,8,2048]{2,1,0:T(8,128)S(1)} %shard_map.20.edge, bf16[13,768,256]{2,1,0:T(8,128)(2,1)} %weights.1.refs_4_.w_ref, f32[36,8,1536]{2,1,0:T(8,128)S(1)} %shard_map.21.acc_in, ...), custom_call_target="tpu_custom_call" | custom-call | flops 7197425664 | bytes 21299204 | tf_op jit(solution)/shard_map/pallas_call | solution.py:44
  96.3 7.0 %shard_map.23.mine = f32[36,8,1536]{2,1,0:T(8,128)S(1)} custom-call(f32[36,8,2048]{2,1,0:T(8,128)S(1)} %shard_map.18.main, f32[8,8,2048]{2,1,0:T(8,128)S(1)} %shard_map.20.edge, bf16[13,768,256]{2,1,0:T(8,128)(2,1)S(1)} %bitcast.5, f32[36,8,1536]{2,1,0:T(8,128)S(1)} %get-tuple-element.27.refs_0_), custom_call_target="tpu_custom_call" | custom-call | flops 3598712832 | bytes 16646144 | tf_op jit(solution)/shard_map/pallas_call | solution.py:44
  104.2 1.4 %collective-permute-start.12 = (f32[36,2,1408]{2,1,0:T(2,128)S(1)}, f32[36,2,1408]{2,1,0:T(2,128)S(1)}, u32[]{:S(2)}, u32[]{:S(2)}) collective-permute-start(f32[36,2,1408]{2,1,0:T(2,128)S(1)} %get-tuple-element.31), channel_id=1, source_target_pairs={{0,16},{4,20},{8,24},{12,28},{16,0},{20,4},{24,8},{28,12},{1,17},{... | collective-permute-start | bytes 1216520 | tf_op jit(solution)/shard_map/ppermute | solution.py:442
  105.6 2.4 %collective-permute-start.13 = (f32[36,2,1408]{2,1,0:T(2,128)S(1)}, f32[36,2,1408]{2,1,0:T(2,128)S(1)}, u32[]{:S(2)}, u32[]{:S(2)}) collective-permute-start(f32[36,2,1408]{2,1,0:T(2,128)S(1)} %get-tuple-element.32), channel_id=1, source_target_pairs={{0,24},{4,28},{8,0},{12,4},{16,8},{20,12},{24,16},{28,20},{1,25},{... | collective-permute-start | bytes 1216520 | tf_op jit(solution)/shard_map/ppermute | solution.py:442
  107.9 9.1 %collective-permute-done.11.refs_1_ = f32[36,2,1408]{2,1,0:T(2,128)S(1)} collective-permute-done((f32[36,2,1408]{2,1,0:T(2,128)S(1)}, f32[36,2,1408]{2,1,0:T(2,128)S(1)}, u32[]{:S(2)}, u32[]{:S(2)}) %collective-permute-start.11) | collective-permute-done | bytes 405536 | tf_op jit(solution)/shard_map/ppermute | solution.py:442
  117.0 6.9 %collective-permute-done.12.refs_2_ = f32[36,2,1408]{2,1,0:T(2,128)S(1)} collective-permute-done((f32[36,2,1408]{2,1,0:T(2,128)S(1)}, f32[36,2,1408]{2,1,0:T(2,128)S(1)}, u32[]{:S(2)}, u32[]{:S(2)}) %collective-permute-start.12) | collective-permute-done | bytes 405536 | tf_op jit(solution)/shard_map/ppermute | solution.py:442
  123.9 0.6 collective-permute-done.13.refs_3_
  124.5 2.0 %shard_map.25 = f32[36,2,5184]{2,1,0:T(2,128)} custom-call(s32[1]{0:T(128)} %bitcast.chip_ref, f32[36,2,1408]{2,1,0:T(2,128)S(1)} %get-tuple-element.29.refs_0_, f32[36,2,1408]{2,1,0:T(2,128)S(1)} %collective-permute-done.11.refs_1_, f32[36,2,1408]{2,1,0:T(2,128)S(1)} %collective-permute-done.12.refs_2_, f32[36,2,1408]{2,1,0:T(2,128)S(1)} %collective-permute-done.13.refs_3_), custom_call_target="tpu_custom_call" | custom-call | bytes 3115012 | tf_op jit(solution)/shard_map/pallas_call | solution.py:44
  (26 shorter events, 2.8 us)
Async XLA Ops:
  0.0 1.4 %copy-start.2 = (f32[2,36,5184]{2,0,1:T(2,128)S(1)}, f32[2,36,5184]{2,0,1:T(2,128)}, u32[]{:S(2)}) copy-start(f32[2,36,5184]{2,0,1:T(2,128)} %param.1) | copy-start | bytes 4478980
  8.3 17.9 %collective-permute-start = (f32[36,2,2048]{2,1,0:T(2,128)}, f32[36,2,2048]{2,1,0:T(2,128)S(1)}, u32[]{:S(2)}, u32[]{:S(2)}) collective-permute-start(f32[36,2,2048]{2,1,0:T(2,128)} %get-tuple-element.20), channel_id=1, source_target_pairs={{0,24},{4,28},{8,0},{12,4},{16,8},{20,12},{24,16},{28,20},{1,25},{... | collective-permute-start | bytes 1769480 | tf_op jit(solution)/shard_map/ppermute | solution.py:442
  12.2 27.4 %collective-permute-start.1 = (f32[36,2,2048]{2,1,0:T(2,128)S(1)}, f32[36,2,2048]{2,1,0:T(2,128)S(1)}, u32[]{:S(2)}, u32[]{:S(2)}) collective-permute-start(f32[36,2,2048]{2,1,0:T(2,128)S(1)} %get-tuple-element.21), channel_id=1, source_target_pairs={{0,16},{4,20},{8,24},{12,28},{16,0},{20,4},{24,8},{28,12},{1,17},{... | collective-permute-start | bytes 1769480 | tf_op jit(solution)/shard_map/ppermute | solution.py:442
  12.8 27.7 %collective-permute-start.2 = (f32[36,2,2048]{2,1,0:T(2,128)S(1)}, f32[36,2,2048]{2,1,0:T(2,128)S(1)}, u32[]{:S(2)}, u32[]{:S(2)}) collective-permute-start(f32[36,2,2048]{2,1,0:T(2,128)S(1)} %get-tuple-element.22), channel_id=1, source_target_pairs={{0,8},{4,12},{8,16},{12,20},{16,24},{20,28},{24,0},{28,4},{1,9},{5... | collective-permute-start | bytes 1769480 | tf_op jit(solution)/shard_map/ppermute | solution.py:442
  39.7 0.8 copy-start.3
  40.5 0.8 copy-start.5
  41.3 2.4 %copy-start = (bf16[13,768,256]{2,1,0:T(8,128)(2,1)S(1)}, bf16[13,768,256]{2,1,0:T(8,128)(2,1)}, u32[]{:S(2)}) copy-start(bf16[13,768,256]{2,1,0:T(8,128)(2,1)} %weights.1.refs_4_.w_ref) | copy-start | bytes 15335428
  43.8 1.1 copy-start.4
  44.8 1.1 copy-start.6
  46.6 32.2 %collective-permute-start.8 = (f32[36,8,2048]{2,1,0:T(8,128)S(1)}, f32[36,8,2048]{2,1,0:T(8,128)}, u32[]{:S(2)}, u32[]{:S(2)}) collective-permute-start(f32[36,8,2048]{2,1,0:T(8,128)S(1)} %shard_map.18.main), channel_id=1, source_target_pairs={{0,4},{4,0},{8,12},{12,8},{16,20},{20,16},{24,28},{28,24},{1,5},{5... | collective-permute-start | bytes 7077896 | tf_op jit(solution)/shard_map/ppermute | solution.py:445
  47.7 8.4 %collective-permute-start.4 = (f32[4,2,5184]{2,1,0:T(2,128)S(1)}, f32[4,2,5184]{2,1,0:T(2,128)S(1)}, u32[]{:S(2)}, u32[]{:S(2)}) collective-permute-start(f32[4,2,5184]{2,1,0:T(2,128)S(1)} %get-tuple-element.33), channel_id=1, source_target_pairs={{1,0},{2,1},{3,2},{0,3},{5,4},{6,5},{7,6},{4,7},{9,8},{10,9},{11,1... | collective-permute-start | bytes 497672 | tf_op jit(solution)/shard_map/ppermute | solution.py:451
  51.4 8.7 %collective-permute-start.3 = (f32[4,2,5184]{2,1,0:T(2,128)S(1)}, f32[4,2,5184]{2,1,0:T(2,128)S(1)}, u32[]{:S(2)}, u32[]{:S(2)}) collective-permute-start(f32[4,2,5184]{2,1,0:T(2,128)S(1)} %get-tuple-element.34), channel_id=1, source_target_pairs={{0,1},{1,2},{2,3},{3,0},{4,5},{5,6},{6,7},{7,4},{8,9},{9,10},{10,1... | collective-permute-start | bytes 497672 | tf_op jit(solution)/shard_map/ppermute | solution.py:450
  61.5 6.4 %collective-permute-start.5 = (f32[8,2,2048]{2,1,0:T(2,128)S(1)}, f32[8,2,2048]{2,1,0:T(2,128)S(1)}, u32[]{:S(2)}, u32[]{:S(2)}) collective-permute-start(f32[8,2,2048]{2,1,0:T(2,128)S(1)} %get-tuple-element.24), channel_id=1, source_target_pairs={{0,24},{4,28},{8,0},{12,4},{16,8},{20,12},{24,16},{28,20},{1,25},{... | collective-permute-start | bytes 393224 | tf_op jit(solution)/shard_map/ppermute | solution.py:442
  62.0 7.6 %collective-permute-start.6 = (f32[8,2,2048]{2,1,0:T(2,128)S(1)}, f32[8,2,2048]{2,1,0:T(2,128)S(1)}, u32[]{:S(2)}, u32[]{:S(2)}) collective-permute-start(f32[8,2,2048]{2,1,0:T(2,128)S(1)} %get-tuple-element.25), channel_id=1, source_target_pairs={{0,16},{4,20},{8,24},{12,28},{16,0},{20,4},{24,8},{28,12},{1,17},{... | collective-permute-start | bytes 393224 | tf_op jit(solution)/shard_map/ppermute | solution.py:442
  62.6 7.0 %collective-permute-start.7 = (f32[8,2,2048]{2,1,0:T(2,128)S(1)}, f32[8,2,2048]{2,1,0:T(2,128)S(1)}, u32[]{:S(2)}, u32[]{:S(2)}) collective-permute-start(f32[8,2,2048]{2,1,0:T(2,128)S(1)} %get-tuple-element.26), channel_id=1, source_target_pairs={{0,8},{4,12},{8,16},{12,20},{16,24},{20,28},{24,0},{28,4},{1,9},{5... | collective-permute-start | bytes 393224 | tf_op jit(solution)/shard_map/ppermute | solution.py:442
  69.8 9.0 %collective-permute-start.9 = (f32[8,8,2048]{2,1,0:T(8,128)S(1)}, f32[8,8,2048]{2,1,0:T(8,128)S(1)}, u32[]{:S(2)}, u32[]{:S(2)}) collective-permute-start(f32[8,8,2048]{2,1,0:T(8,128)S(1)} %shard_map.20.edge), channel_id=1, source_target_pairs={{0,4},{4,0},{8,12},{12,8},{16,20},{20,16},{24,28},{28,24},{1,5},{5... | collective-permute-start | bytes 1572872 | tf_op jit(solution)/shard_map/ppermute | solution.py:445
  69.9 2.5 %copy-start.1 = (bf16[13,768,256]{2,1,0:T(8,128)(2,1)S(1)}, bf16[13,768,256]{2,1,0:T(8,128)(2,1)}, u32[]{:S(2)}) copy-start(bf16[13,768,256]{2,1,0:T(8,128)(2,1)} %weights.1.refs_4_.w_ref) | copy-start | bytes 15335428
  72.3 24.0 %slice-start = ((s8[5111808]{0:T(1024)(128)(4,1)}), s8[4194304]{0:T(1024)(128)(4,1)S(1)}, s32[]{:S(2)}) async-start(s8[5111808]{0:T(1024)(128)(4,1)} %bitcast.4), calls=%async_computation | async-start | bytes 8388608
  78.8 17.5 %slice-start.1 = ((s8[5111808]{0:T(1024)(128)(4,1)}), s8[917504]{0:T(1024)(128)(4,1)S(1)}, s32[]{:S(2)}) async-start(s8[5111808]{0:T(1024)(128)(4,1)} %bitcast.4), calls=%async_computation.1 | async-start | bytes 1835008
  95.8 7.5 %collective-permute-start.10 = (f32[36,8,1536]{2,1,0:T(8,128)S(1)}, f32[36,8,1536]{2,1,0:T(8,128)S(1)}, u32[]{:S(2)}, u32[]{:S(2)}) collective-permute-start(f32[36,8,1536]{2,1,0:T(8,128)S(1)} %get-tuple-element.28), channel_id=1, source_target_pairs={{0,4},{4,0},{8,12},{12,8},{16,20},{20,16},{24,28},{28,24},{1,5},{5... | collective-permute-start | bytes 5308424 | tf_op jit(solution)/shard_map/ppermute | solution.py:445
  103.8 13.3 %collective-permute-start.11 = (f32[36,2,1408]{2,1,0:T(2,128)S(1)}, f32[36,2,1408]{2,1,0:T(2,128)S(1)}, u32[]{:S(2)}, u32[]{:S(2)}) collective-permute-start(f32[36,2,1408]{2,1,0:T(2,128)S(1)} %get-tuple-element.30), channel_id=1, source_target_pairs={{0,8},{4,12},{8,16},{12,20},{16,24},{20,28},{24,0},{28,4},{1,9},{5... | collective-permute-start | bytes 1216520 | tf_op jit(solution)/shard_map/ppermute | solution.py:442
  104.2 19.8 %collective-permute-start.12 = (f32[36,2,1408]{2,1,0:T(2,128)S(1)}, f32[36,2,1408]{2,1,0:T(2,128)S(1)}, u32[]{:S(2)}, u32[]{:S(2)}) collective-permute-start(f32[36,2,1408]{2,1,0:T(2,128)S(1)} %get-tuple-element.31), channel_id=1, source_target_pairs={{0,16},{4,20},{8,24},{12,28},{16,0},{20,4},{24,8},{28,12},{1,17},{... | collective-permute-start | bytes 1216520 | tf_op jit(solution)/shard_map/ppermute | solution.py:442
  105.6 18.9 %collective-permute-start.13 = (f32[36,2,1408]{2,1,0:T(2,128)S(1)}, f32[36,2,1408]{2,1,0:T(2,128)S(1)}, u32[]{:S(2)}, u32[]{:S(2)}) collective-permute-start(f32[36,2,1408]{2,1,0:T(2,128)S(1)} %get-tuple-element.32), channel_id=1, source_target_pairs={{0,24},{4,28},{8,0},{12,4},{16,8},{20,12},{24,16},{28,20},{1,25},{... | collective-permute-start | bytes 1216520 | tf_op jit(solution)/shard_map/ppermute | solution.py:442

commit v4 on v3

v4 whole, which is shorter than its diff:
```python
import functools

import jax
import jax.numpy as jnp
from jax import lax
from jax.experimental import pallas as pl
from jax.experimental.pallas import tpu as pltpu
from jax.sharding import PartitionSpec as P


NY = 72
LANES = 128
TILE = 256
WINDOW = 3 * TILE
REACH = 2
HALO = 4
KERNEL_MIB = 36
CHUNKS = 2
STEP = 2
CENTRE = 8.5
DIAGONAL = 12.0 * CENTRE
SCALE = -1.0 / (CENTRE * DIAGONAL * DIAGONAL)
VMEM = pl.BlockSpec(memory_space=pltpu.VMEM)
SMEM = pl.BlockSpec(memory_space=pltpu.SMEM)


def sds(*shape):
    return jax.ShapeDtypeStruct(shape, jnp.float32)


def call(body, out, inputs, scratch=(), flops=0, smem=False, limit=12):
    nbytes = sum(4 * x.size for x in inputs) + sum(4 * o.size for o in out)
    specs = [VMEM] * len(inputs)
    if smem:
        specs[0] = SMEM
    return pl.pallas_call(
        body,
        out_shape=out,
        in_specs=specs,
        out_specs=[VMEM] * len(out),
        scratch_shapes=scratch,
        compiler_params=pltpu.CompilerParams(vmem_limit_bytes=limit << 20),
        cost_estimate=pl.CostEstimate(flops=flops, bytes_accessed=nbytes, transcendentals=0),
    )(*inputs)


def floor_to(value, unit):
    return value // unit * unit


def ceil_to(value, unit):
    return -(-value // unit) * unit


class Ranges:
    def __init__(self, chips, total):
        self.chips = chips
        self.total = total
        self.width = total // chips
        self.halo = HALO * NY
        starts = [j * self.width - self.halo for j in range(chips)]
        self.starts = [floor_to(s, LANES) for s in starts]
        shifts = [s - a for s, a in zip(starts, self.starts)]
        low, high = min(shifts), max(shifts)
        used = self.width + 2 * self.halo
        self.length = ceil_to(high + used, LANES)
        reach = REACH * NY
        self.first = floor_to(low + reach, LANES)
        self.n_first = ceil_to(high + used - reach - self.first, TILE) // TILE
        self.second = floor_to(low + 2 * reach, LANES)
        self.n_second = ceil_to(high + used - 2 * reach - self.second, TILE) // TILE
        self.out_starts = [floor_to(j * self.width, LANES) for j in range(chips)]
        self.out_length = max(
            ceil_to((j + 1) * self.width, LANES) - s for j, s in enumerate(self.out_starts)
        )

    def shift(self, chip):
        start = chip * self.width - self.halo + ceil_to(self.halo, LANES)
        return lax.rem(start, LANES)

    def out_at(self, chip):
        start = chip * self.width
        return lax.div(start, LANES) * LANES - (start - self.halo - self.shift(chip)) - self.second

    @property
    def pad(self):
        return max(0, TILE - self.first)

    @property
    def split_length(self):
        ends = (
            self.pad + self.first - TILE + self.n_first * TILE + WINDOW - TILE,
            self.pad + self.second - TILE + self.n_second * TILE + WINDOW - TILE,
            self.pad + self.first + self.n_first * TILE,
            self.pad + self.length,
        )
        return ceil_to(max(ends), LANES)

    @property
    def full_length(self):
        return max(
            self.first + self.n_first * TILE, self.second + self.n_second * TILE, self.length
        )


def pack_body(ranges, bounds, chip_ref, *refs):
    chips, total, length = ranges.chips, ranges.total, ranges.length
    ins, outs = refs[:-chips], refs[-chips:]
    chip = chip_ref[0]
    for ahead in range(chips):
        for target in range(chips):

            @pl.when(lax.rem(chip + ahead, chips) == target)
            def _(ahead=ahead, start=ranges.starts[target]):
                row = 0
                for ref, (low, high) in zip(ins, bounds):

                    def plane(s, _, ref=ref, row=row - low, low=low):
                        z = low + s * STEP
                        lo, hi = start, start + length
                        at = pl.ds(z, STEP)
                        pieces = []
                        if lo < 0:
                            pieces.append(ref[at, :, lo + total : total])
                        pieces.append(ref[at, :, max(lo, 0) : min(hi, total)])
                        if hi > total:
                            pieces.append(ref[at, :, 0 : hi - total])
                        value = pieces[0] if len(pieces) == 1 else jnp.concatenate(pieces, axis=-1)
                        outs[ahead][pl.ds(row + z, STEP)] = value
                        return 0

                    lax.fori_loop(0, (high - low) // STEP, plane, 0)
                    row += high - low


def pack(ranges, chip, pieces):
    orbs = pieces[0][0].shape[1]
    bounds = [(low, high) for _, low, high in pieces]
    rows = sum(high - low for low, high in bounds)
    return call(
        functools.partial(pack_body, ranges, bounds),
        [sds(rows, orbs, ranges.length)] * ranges.chips,
        [chip, *(array for array, _, _ in pieces)],
        smem=True,
    )


def gather_body(groups, kept, *refs):
    out = refs[-1]
    row = 0
    if kept:
        before = refs[0]
        out[0:kept] = before[before.shape[0] - kept :]
        refs, row = refs[1:], kept
    slots = (len(refs) - 1) // groups
    for group in range(groups):
        ins = refs[group * slots : (group + 1) * slots]
        orbs = ins[0].shape[1]

        def plane(s, _, ins=ins, row=row):
            z = s * STEP
            for slot, ref in enumerate(ins):
                value = ref[pl.ds(z, STEP)]
                out[pl.ds(row + z, STEP), slot * orbs : (slot + 1) * orbs, :] = value
            return 0

        lax.fori_loop(0, ins[0].shape[0] // STEP, plane, 0)
        row += ins[0].shape[0]


def gather(groups, before=None, kept=0):
    depth = kept + sum(g[0].shape[0] for g in groups)
    _, orbs, span = groups[0][0].shape
    return call(
        functools.partial(gather_body, len(groups), kept),
        [sds(depth, orbs * len(groups[0]), span)],
        [*([before] if kept else []), *(p for g in groups for p in g)],
    )[0]


def roll_rows(value, shift):
    if isinstance(shift, int):
        shift = shift % value.shape[1]
        if shift == 0:
            return value
    return pltpu.roll(value, shift, 1)


class Pairing:
    def __init__(self, rows, even, odd=None):
        self.rows, self.even, self.odd = rows, even, odd

    def apply(self, value, even, odd):
        if odd is None:
            return roll_rows(value, even)
        row = lax.broadcasted_iota(jnp.int32, value.shape, 1)
        return jnp.where(row % 2 == 0, roll_rows(value, even), roll_rows(value, odd))

    def negative(self, shift):
        return -shift if isinstance(shift, int) else lax.rem(self.rows - shift, self.rows)

    def partner(self, value):
        return self.apply(value, self.even, self.odd)

    def back(self, value):
        if self.odd is None:
            return self.apply(value, self.negative(self.even), None)
        return self.apply(value, self.negative(self.odd), self.negative(self.even))


def weights_body(ranges, chip_ref, out):
    i = lax.broadcasted_iota(jnp.int32, (WINDOW, TILE), 0)
    lane = lax.broadcasted_iota(jnp.int32, (1, TILE), 1)
    shift = ranges.shift(chip_ref[0])
    at = lane + TILE

    def tile(t, start, diagonal):
        y = lax.rem(lane + (start + 2 * NY) - shift, NY)
        near = (i == at - NY) | (i == at + NY)
        far = (i == at - 2 * NY) | (i == at + 2 * NY)

        def beside(step):
            wrap = jnp.where(y + step >= NY, NY, jnp.where(y + step < 0, -NY, 0))
            return i == at + step - wrap

        near = near | beside(1) | beside(-1)
        far = far | beside(2) | beside(-2)
        value = jnp.where(i == at, diagonal, 0.0)
        value = jnp.where(near, 16.0, jnp.where(far, -1.0, value))
        out[t] = value.astype(jnp.bfloat16)

    def first(t, _):
        tile(t, ranges.first + t * TILE, DIAGONAL)
        return 0

    def second(t, _):
        tile(ranges.n_first + t, ranges.second + t * TILE, 0.0)
        return 0

    lax.fori_loop(0, ranges.n_first, first, 0)
    lax.fori_loop(0, ranges.n_second, second, 0)


def weights(ranges, chip):
    shape = (ranges.n_first + ranges.n_second, WINDOW, TILE)
    out = jax.ShapeDtypeStruct(shape, jnp.bfloat16)
    return call(functools.partial(weights_body, ranges), [out], [chip], smem=True)[0]


def store_halves(ref, rows, lanes, value):
    high = value.astype(jnp.bfloat16)
    ref[0, rows, lanes] = high
    ref[1, rows, lanes] = (value - high.astype(jnp.float32)).astype(jnp.bfloat16)


def aligned(start, size):
    if isinstance(start, int):
        return slice(start, start + size)
    return pl.ds(pl.multiple_of(start, LANES), size)


def potentials(ranges, first, seconds, pairings, w_ref, work, finish):
    rho_split, rho, mid_split, mid, product = work
    depth, n_rows, span = first.shape
    inner = depth - 2 * HALO
    swept = inner + 2 * REACH
    pad = ranges.pad
    kinds = len(seconds)

    def density(s, _):
        planes = pl.ds(s * STEP, STEP)
        rows = pl.ds(pl.multiple_of(s * (STEP * n_rows), STEP * n_rows), STEP * n_rows)
        for lo in range(0, span, LANES):
            lanes = slice(lo, lo + LANES)
            mine = first[planes, :, lanes]
            for k, (second, pairing) in enumerate(zip(seconds, pairings)):
                value = mine * pairing.partner(second[planes, :, lanes])
                value = value.reshape(STEP * n_rows, LANES)
                store_halves(rho_split.at[k], rows, slice(lo + pad, lo + pad + LANES), value)
                rho[k, rows, lanes] = value
        return 0

    lax.fori_loop(0, depth // STEP, density, 0)

    def in_plane(source, planes, start, weight):
        lanes = aligned(start - TILE + pad, WINDOW)
        rows = planes * n_rows
        value = source[:, :, REACH * n_rows : REACH * n_rows + rows, lanes]
        value = value.reshape(2 * kinds * rows, WINDOW)
        product[0 : 2 * kinds * rows] = jnp.dot(value, weight, preferred_element_type=jnp.float32)

    def off(source, k, planes, start):
        rows = planes * n_rows

        def shifted(z):
            return source[k, z * n_rows : z * n_rows + rows, aligned(start, TILE)]

        near = shifted(1) + shifted(3)
        far = shifted(0) + shifted(4)
        row = 2 * k * rows
        inside = product[row : row + rows] + product[row + rows : row + 2 * rows]
        return inside + (16.0 * near - far)

    def sweep(t, _):
        start = ranges.first + t * TILE
        in_plane(rho_split, swept, start, w_ref[t])
        for k in range(kinds):
            value = off(rho, k, swept, start)
            mid[k, :, aligned(start, TILE)] = value
            store_halves(mid_split.at[k], slice(None), aligned(start + pad, TILE), value)
        return 0

    lax.fori_loop(0, ranges.n_first, sweep, 0)

    def last(t, _):
        start = ranges.second + t * TILE
        here = aligned(start, TILE)
        in_plane(mid_split, inner, start, w_ref[t + ranges.n_first])
        values = []
        for k in range(kinds):
            value = off(mid, k, inner, start)
            source = rho[k, HALO * n_rows : (HALO + inner) * n_rows, here]
            value = value + (DIAGONAL * DIAGONAL) * source
            values.append(value.reshape(inner, n_rows, TILE))
        finish(here, aligned(t * TILE, TILE), values)
        return 0

    lax.fori_loop(0, ranges.n_second, last, 0)


def clear(ranges, work):
    rho_split, rho, mid_split, mid = work[:4]
    span = ranges.length

    def zero(ref, lo, hi):
        if lo < hi:
            shape = ref.shape[:-1] + (hi - lo,)
            ref[..., lo:hi] = jnp.zeros(shape, ref.dtype)

    pad, end = ranges.pad, ranges.split_length
    zero(rho_split, 0, pad)
    zero(rho_split, pad + span, end)
    zero(rho, span, rho.shape[-1])
    zero(mid_split, 0, pad + ranges.first)
    zero(mid_split, pad + ranges.first + ranges.n_first * TILE, end)
    zero(mid, 0, ranges.first)
    zero(mid, ranges.first + ranges.n_first * TILE, mid.shape[-1])


def total_of(acc_in, lanes, total):
    return total if acc_in is None else (total + acc_in[:, :, lanes]) * SCALE


def same_body(ranges, follows, planes, w_ref, *refs):
    acc_in = refs[0] if follows else None
    acc, *work = refs[1:] if follows else refs
    depth, n_rows, _ = planes.shape
    inner = slice(HALO, depth - HALO)
    pairings = (Pairing(n_rows, 2), Pairing(n_rows, 1, 3))

    def finish(here, lanes, values):
        mine = planes[inner, :, here]
        total = None
        for value, pairing in zip(values, pairings):
            part = value * pairing.partner(mine) + pairing.back(value * mine)
            total = part if total is None else total + part
        acc[:, :, lanes] = total_of(acc_in, lanes, total)

    clear(ranges, work)
    potentials(ranges, planes, (planes, planes), pairings, w_ref, work, finish)


def cross_body(ranges, follows, core_ref, planes, w_ref, other, *refs):
    acc_in = refs[0] if follows else None
    acc, travel, *work = refs[1:] if follows else refs
    depth, n_rows, _ = planes.shape
    inner = slice(HALO, depth - HALO)
    odd = core_ref[0] == 1
    pairings = (
        Pairing(n_rows, jnp.where(odd, 0, 2)),
        Pairing(n_rows, jnp.where(odd, n_rows - 1, 1), jnp.where(odd, 1, 3)),
    )

    def finish(here, lanes, values):
        mine, theirs = planes[inner, :, here], other[inner, :, here]
        own = away = None
        for value, pairing in zip(values, pairings):
            to_own = value * pairing.partner(theirs)
            to_away = pairing.back(value * mine)
            own = to_own if own is None else own + to_own
            away = to_away if away is None else away + to_away
        acc[:, :, lanes] = total_of(acc_in, lanes, own)
        travel[:, :, lanes] = away * SCALE

    clear(ranges, work)
    potentials(ranges, planes, (other, other), pairings, w_ref, work, finish)


def split_body(ranges, chip_ref, mine, theirs, *outs):
    orbs = outs[0].shape[1]
    lanes = aligned(ranges.out_at(chip_ref[0]), ranges.out_length)

    def plane(s, _):
        at = pl.ds(s * STEP, STEP)
        value = mine[at, :, lanes] + theirs[at, :, lanes]
        for slot, out in enumerate(outs):
            out[at] = value[:, slot * orbs : (slot + 1) * orbs]
        return 0

    lax.fori_loop(0, outs[0].shape[0] // STEP, plane, 0)


def place_body(ranges, chip_ref, *refs):
    chips = ranges.chips
    ins, out = refs[:-1], refs[-1]
    chip = chip_ref[0]
    for behind in range(chips):
        for source in range(chips):

            @pl.when(lax.rem(chip + chips - behind, chips) == source)
            def _(parts=ins[behind::chips], source=source):
                base = ranges.out_starts[source]
                lo, hi = source * ranges.width, (source + 1) * ranges.width
                row = 0
                for ref in parts:

                    def plane(s, _, ref=ref, row=row):
                        at = pl.ds(s * STEP, STEP)
                        into = pl.ds(row + s * STEP, STEP)
                        lane = lo
                        while lane < hi:
                            stop = min(floor_to(lane, LANES) + LANES, hi)
                            if lane % LANES == 0:
                                stop = max(floor_to(hi, LANES), stop)
                            out[into, :, lane:stop] = ref[at, :, lane - base : stop - base]
                            lane = stop
                        return 0

                    lax.fori_loop(0, ref.shape[0] // STEP, plane, 0)
                    row += ref.shape[0]


def per_device(n_band, orbitals):
    orbs, depth, total = orbitals.shape
    chips = n_band // 2
    ranges = Ranges(chips, total)
    index = lax.axis_index("band")
    chip = (index // 2).astype(jnp.int32).reshape(1)
    core = (index % 2).astype(jnp.int32).reshape(1)
    planes = jnp.transpose(orbitals, (1, 0, 2))

    def along(value, steps):
        pairs = [(i, (i + 2 * steps) % n_band) for i in range(n_band)]
        return lax.ppermute(value, "band", pairs)

    def partner_core(value):
        return lax.ppermute(value, "band", [(i, i ^ 1) for i in range(n_band)])

    n_slab = lax.axis_size("slab")
    up = [(i, (i + 1) % n_slab) for i in range(n_slab)]
    down = [(j, i) for i, j in up]
    below = lax.ppermute(planes[depth - HALO :], "slab", up)
    above = lax.ppermute(planes[:HALO], "slab", down)

    order = [0] + list(range(chips - 1, 0, -1))

    def spread(sent):
        got = [sent[0]]
        for s in range(1, chips):
            got.append(along(sent[s], s))
        return got

    def fetch(pieces):
        sent = pack(ranges, chip, pieces)
        got = spread(sent)
        return [got[s] for s in order]

    inner = depth // CHUNKS
    cut = inner + HALO
    got_a = fetch([(planes, 0, cut)])
    banded = weights(ranges, chip)
    got_low = fetch([(below, 0, HALO)])
    got_b = fetch([(planes, cut, depth), (above, 0, HALO)])
    planes_a = gather([got_low, got_a])
    planes_b = gather([got_b], before=planes_a, kept=2 * HALO)

    rows = orbs * chips
    full, swept = (inner + 2 * HALO) * rows, (inner + 2 * REACH) * rows
    work = [
        pltpu.VMEM((2, 2, full, ranges.split_length), jnp.bfloat16),
        pltpu.VMEM((2, full, ranges.full_length), jnp.float32),
        pltpu.VMEM((2, 2, swept, ranges.split_length), jnp.bfloat16),
        pltpu.VMEM((2, swept, ranges.full_length), jnp.float32),
        pltpu.VMEM((4 * swept, TILE), jnp.float32),
    ]
    result = sds(inner, rows, ranges.n_second * TILE)
    flops = 8 * WINDOW * TILE * (ranges.n_first + ranges.n_second) * full

    def same(mine, *acc):
        return call(
            functools.partial(same_body, ranges, bool(acc)),
            [result],
            [mine, banded, *acc],
            scratch=work,
            flops=flops,
            limit=KERNEL_MIB,
        )[0]

    def cross(mine, other, *acc):
        own, travel = call(
            functools.partial(cross_body, ranges, bool(acc)),
            [result, result],
            [core, mine, banded, other, *acc],
            scratch=work,
            flops=flops,
            smem=True,
            limit=KERNEL_MIB,
        )
        return own, partner_core(travel)

    def give(acc, back):
        parts = call(
            functools.partial(split_body, ranges),
            [sds(inner, orbs, ranges.out_length)] * chips,
            [chip, acc, back],
            smem=True,
        )
        return spread(parts)

    other_a = partner_core(planes_a)
    acc_a = same(planes_a)
    other_b = partner_core(planes_b)
    acc_a, back_a = cross(planes_a, other_a, acc_a)
    acc_b, back_b = cross(planes_b, other_b)
    home = give(acc_a, back_a)
    acc_b = same(planes_b, acc_b)
    home += give(acc_b, back_b)
    out = call(
        functools.partial(place_body, ranges), [sds(depth, orbs, total)], [chip, *home], smem=True
    )[0]
    return jnp.transpose(out, (1, 0, 2))


def solution(mesh):
    def body(orbitals):
        return per_device(mesh.shape["band"], orbitals)

    return jax.shard_map(
        body,
        mesh=mesh,
        in_specs=(P("band", "slab", None),),
        out_specs=P("band", "slab", None),
        check_vma=False,
    )
```

time: 127 us -> 113 us (0.89); the launches traced: 127 us -> 111 us
  waiting for transfers between devices: 50.5 us -> 32.6 us
  starting transfers between devices: 16 us -> 29 us
  Pallas kernels: 48.8 us -> 42.7 us
  local copies, waits for them, and re-layouts: 11.1 us -> 6.17 us
    ppermute x9 -> x15, waiting for transfers between devices: 41.7 us -> 24.8 us  [along(): return lax.ppermute(value, 'band', pairs)]
    ppermute x9 -> x15, starting transfers between devices: 11.7 us -> 23 us  [along(): return lax.ppermute(value, 'band', pairs)]
    pallas_call x1 -> x0, Pallas kernels: 6.75 us -> none  [weights(): pl.pallas_call(functools.partial(weights_body, ranges), out_shape=jax.Sha...]
    unnamed x18 -> x8, local copies, waits for them, and re-layouts: 10 us -> 6.14 us
    ppermute x1, waiting for transfers between devices: 4.72 us -> 2.24 us  [per_device(): above = lax.ppermute(planes[:HALO], 'slab', down)]
    ppermute x1, starting transfers between devices: 0.01 us -> 1.63 us  [per_device(): below = lax.ppermute(planes[depth - HALO:], 'slab', up)]
    ppermute x1, waiting for transfers between devices: 3.98 us -> 5.58 us  [per_device(): below = lax.ppermute(planes[depth - HALO:], 'slab', up)]
    pallas_call x9 -> x13, Pallas kernels: 42.1 us -> 42.7 us  [call(): pl.pallas_call(body, out_shape=out, in_specs=specs, out_specs=[VMEM] * le...]
  transfers between devices with their start and end apart: 14 -> 21, of which waited for: 9 -> 10; matrix products, arithmetic and copies ran while one was open for 1% -> 0% of each run, Pallas kernels for 17% -> 35%
where the time goes in v4:
time: 113 us; the launch traced here: 111 us
  Pallas kernels  42.7 us (38%)
  waiting for transfers between devices  32.6 us (29%)
  starting transfers between devices  29 us (26%)
  local copies, waits for them, and re-layouts  6.17 us (5%)
    pallas_call x13, Pallas kernels, call(): pl.pallas_call(body, out_shape=out, in_specs=specs, out_specs=[VMEM] * le...  42.7 us
    ppermute x15, waiting for transfers between devices, along(): return lax.ppermute(value, 'band', pairs)  24.8 us
    ppermute x15, starting transfers between devices, along(): return lax.ppermute(value, 'band', pairs)  23 us
    unnamed x8, local copies, waits for them, and re-layouts  6.14 us
    ppermute x1, waiting for transfers between devices, per_device(): below = lax.ppermute(planes[depth - HALO:], 'slab', up)  5.58 us
    ppermute x1, starting transfers between devices, per_device(): above = lax.ppermute(planes[:HALO], 'slab', down)  3.6 us
  transfers between devices with their start and end apart: 21, of which 10 were waited for; matrix products, arithmetic and copies ran while one was open for 0% of the time, Pallas kernels for 35%

profile of v4, /device:TPU:0, one launch (start us, length us, event | category | flops | bytes accessed | tf_op | source)
XLA Modules:
  0.0 110.7 jit_solution(436882858880339971)
XLA Ops:
  0.0 1.4 %copy-done = f32[2,36,5184]{2,0,1:T(2,128)S(1)} copy-done((f32[2,36,5184]{2,0,1:T(2,128)S(1)}, f32[2,36,5184]{2,0,1:T(2,128)}, u32[]{:S(2)}) %copy-start) | copy-done | bytes 1493016
  1.4 2.0 %shard_map.18 = (f32[22,2,2048]{2,1,0:T(2,128)S(1)}, f32[22,2,2048]{2,1,0:T(2,128)S(1)}, f32[22,2,2048]{2,1,0:T(2,128)S(1)}, f32[22,2,2048]{2,1,0:T(2,128)S(1)}) custom-call(s32[1]{0:T(128)} %bitcast.chip_ref, f32[36,2,5184]{2,1,0:T(2,128)S(1)} %bitcast.4), custom_call_target="tpu_custom_call" | custom-call | bytes 2934788 | tf_op jit(solution)/shard_map/pallas_call | solution.py:36
  3.4 4.0 %collective-permute-start.4 = (f32[22,2,2048]{2,1,0:T(2,128)S(1)}, f32[22,2,2048]{2,1,0:T(2,128)S(1)}, u32[]{:S(2)}, u32[]{:S(2)}) collective-permute-start(f32[22,2,2048]{2,1,0:T(2,128)S(1)} %get-tuple-element.34), channel_id=1, source_target_pairs={{0,24},{4,28},{8,0},{12,4},{16,8},{20,12},{24,16},{28,20},{1,25},{... | collective-permute-start | bytes 1081352 | tf_op jit(solution)/shard_map/ppermute | solution.py:454
  8.5 1.6 %collective-permute-start = (f32[4,2,5184]{2,1,0:T(2,128)S(1)}, f32[4,2,5184]{2,1,0:T(2,128)S(1)}, u32[]{:S(2)}, u32[]{:S(2)}) collective-permute-start(f32[4,2,5184]{2,1,0:T(2,128)S(1)} %get-tuple-element.54), channel_id=1, source_target_pairs={{0,1},{1,2},{2,3},{3,0},{4,5},{5,6},{6,7},{7,4},{8,9},{9,10},{10,1... | collective-permute-start | bytes 497672 | tf_op jit(solution)/shard_map/ppermute | solution.py:462
  10.1 5.6 %collective-permute-done.refs_0_ = f32[4,2,5184]{2,1,0:T(2,128)S(1)} collective-permute-done((f32[4,2,5184]{2,1,0:T(2,128)S(1)}, f32[4,2,5184]{2,1,0:T(2,128)S(1)}, u32[]{:S(2)}, u32[]{:S(2)}) %collective-permute-start) | collective-permute-done | bytes 165920 | tf_op jit(solution)/shard_map/ppermute | solution.py:462
  16.1 2.4 %collective-permute-start.1 = (f32[4,2,2048]{2,1,0:T(2,128)S(1)}, f32[4,2,2048]{2,1,0:T(2,128)S(1)}, u32[]{:S(2)}, u32[]{:S(2)}) collective-permute-start(f32[4,2,2048]{2,1,0:T(2,128)S(1)} %get-tuple-element.30), channel_id=1, source_target_pairs={{0,24},{4,28},{8,0},{12,4},{16,8},{20,12},{24,16},{28,20},{1,25},{... | collective-permute-start | bytes 196616 | tf_op jit(solution)/shard_map/ppermute | solution.py:454
  18.4 1.5 %collective-permute-start.2 = (f32[4,2,2048]{2,1,0:T(2,128)S(1)}, f32[4,2,2048]{2,1,0:T(2,128)S(1)}, u32[]{:S(2)}, u32[]{:S(2)}) collective-permute-start(f32[4,2,2048]{2,1,0:T(2,128)S(1)} %get-tuple-element.31), channel_id=1, source_target_pairs={{0,16},{4,20},{8,24},{12,28},{16,0},{20,4},{24,8},{28,12},{1,17},{... | collective-permute-start | bytes 196616 | tf_op jit(solution)/shard_map/ppermute | solution.py:454
  19.9 4.3 %collective-permute-done.1.refs_1_ = f32[4,2,2048]{2,1,0:T(2,128)S(1)} collective-permute-done((f32[4,2,2048]{2,1,0:T(2,128)S(1)}, f32[4,2,2048]{2,1,0:T(2,128)S(1)}, u32[]{:S(2)}, u32[]{:S(2)}) %collective-permute-start.1) | collective-permute-done | bytes 65568 | tf_op jit(solution)/shard_map/ppermute | solution.py:454
  24.2 2.5 %collective-permute-start.3 = (f32[4,2,2048]{2,1,0:T(2,128)S(1)}, f32[4,2,2048]{2,1,0:T(2,128)S(1)}, u32[]{:S(2)}, u32[]{:S(2)}) collective-permute-start(f32[4,2,2048]{2,1,0:T(2,128)S(1)} %get-tuple-element.32), channel_id=1, source_target_pairs={{0,8},{4,12},{8,16},{12,20},{16,24},{20,28},{24,0},{28,4},{1,9},{5... | collective-permute-start | bytes 196616 | tf_op jit(solution)/shard_map/ppermute | solution.py:454
  26.7 3.6 %collective-permute-start.12 = (f32[4,2,5184]{2,1,0:T(2,128)S(1)}, f32[4,2,5184]{2,1,0:T(2,128)S(1)}, u32[]{:S(2)}, u32[]{:S(2)}) collective-permute-start(f32[4,2,5184]{2,1,0:T(2,128)S(1)} %get-tuple-element.53), channel_id=1, source_target_pairs={{1,0},{2,1},{3,2},{0,3},{5,4},{6,5},{7,6},{4,7},{9,8},{10,9},{11,1... | collective-permute-start | bytes 497672 | tf_op jit(solution)/shard_map/ppermute | solution.py:463
  30.9 2.2 %collective-permute-done.12.refs_1_ = f32[4,2,5184]{2,1,0:T(2,128)S(1)} collective-permute-done((f32[4,2,5184]{2,1,0:T(2,128)S(1)}, f32[4,2,5184]{2,1,0:T(2,128)S(1)}, u32[]{:S(2)}, u32[]{:S(2)}) %collective-permute-start.12) | collective-permute-done | bytes 165920 | tf_op jit(solution)/shard_map/ppermute | solution.py:463
  33.2 1.6 %shard_map.24 = (f32[18,2,2048]{2,1,0:T(2,128)S(1)}, f32[18,2,2048]{2,1,0:T(2,128)S(1)}, f32[18,2,2048]{2,1,0:T(2,128)S(1)}, f32[18,2,2048]{2,1,0:T(2,128)S(1)}) custom-call(s32[1]{0:T(128)} %bitcast.chip_ref, f32[36,2,5184]{2,1,0:T(2,128)S(1)} %bitcast.6, f32[4,2,5184]{2,1,0:T(2,128)S(1)} %collective-permute-done.12.refs_1_), custom_call_target="tpu_custom_call" | custom-call | bytes 2838532 | tf_op jit(solution)/shard_map/pallas_call | solution.py:36
  34.8 1.6 %collective-permute-start.13 = (f32[18,2,2048]{2,1,0:T(2,128)S(1)}, f32[18,2,2048]{2,1,0:T(2,128)S(1)}, u32[]{:S(2)}, u32[]{:S(2)}) collective-permute-start(f32[18,2,2048]{2,1,0:T(2,128)S(1)} %get-tuple-element.44), channel_id=1, source_target_pairs={{0,24},{4,28},{8,0},{12,4},{16,8},{20,12},{24,16},{28,20},{1,25},{... | collective-permute-start | bytes 884744 | tf_op jit(solution)/shard_map/ppermute | solution.py:454
  36.9 1.5 %collective-permute-start.15 = (f32[18,2,2048]{2,1,0:T(2,128)S(1)}, f32[18,2,2048]{2,1,0:T(2,128)S(1)}, u32[]{:S(2)}, u32[]{:S(2)}) collective-permute-start(f32[18,2,2048]{2,1,0:T(2,128)S(1)} %get-tuple-element.46), channel_id=1, source_target_pairs={{0,8},{4,12},{8,16},{12,20},{16,24},{20,28},{24,0},{28,4},{1,9},{5... | collective-permute-start | bytes 884744 | tf_op jit(solution)/shard_map/ppermute | solution.py:454
  38.4 6.3 %collective-permute-done.13.refs_2_ = f32[18,2,2048]{2,1,0:T(2,128)S(1)} collective-permute-done((f32[18,2,2048]{2,1,0:T(2,128)S(1)}, f32[18,2,2048]{2,1,0:T(2,128)S(1)}, u32[]{:S(2)}, u32[]{:S(2)}) %collective-permute-start.13) | collective-permute-done | bytes 294944 | tf_op jit(solution)/shard_map/ppermute | solution.py:454
  44.7 4.9 %collective-permute-done.14.refs_3_ = f32[18,2,2048]{2,1,0:T(2,128)S(1)} collective-permute-done((f32[18,2,2048]{2,1,0:T(2,128)S(1)}, f32[18,2,2048]{2,1,0:T(2,128)S(1)}, u32[]{:S(2)}, u32[]{:S(2)}) %collective-permute-start.14) | collective-permute-done | bytes 294944 | tf_op jit(solution)/shard_map/ppermute | solution.py:454
  50.2 4.5 %shard_map.20.w_ref = bf16[13,768,256]{2,1,0:T(8,128)(2,1)S(1)} custom-call(s32[1]{0:T(128)} %bitcast.chip_ref), custom_call_target="tpu_custom_call" | custom-call | bytes 10223620 | tf_op jit(solution)/shard_map/pallas_call | solution.py:36
  54.7 2.3 %copy-done.2 = bf16[13,768,256]{2,1,0:T(8,128)(2,1)} copy-done((bf16[13,768,256]{2,1,0:T(8,128)(2,1)}, bf16[13,768,256]{2,1,0:T(8,128)(2,1)S(1)}, u32[]{:S(2)}) %copy-start.2) | copy-done | bytes 5111832
  57.0 2.4 %copy-done.3 = bf16[13,768,256]{2,1,0:T(8,128)(2,1)S(1)} copy-done((bf16[13,768,256]{2,1,0:T(8,128)(2,1)S(1)}, bf16[13,768,256]{2,1,0:T(8,128)(2,1)}, u32[]{:S(2)}) %copy-start.3) | copy-done | bytes 5111832
  59.4 7.0 %shard_map.21.refs_0_ = f32[18,8,1536]{2,1,0:T(8,128)S(1)} custom-call(f32[26,8,2048]{2,1,0:T(8,128)S(1)} %shard_map.19.planes.refs_0_, bf16[13,768,256]{2,1,0:T(8,128)(2,1)S(1)} %copy-done.3), custom_call_target="tpu_custom_call" | custom-call | flops 4253024256 | bytes 12812288 | tf_op jit(solution)/shard_map/pallas_call | solution.py:36
  66.4 8.7 %shard_map.22 = (f32[18,8,1536]{2,1,0:T(8,128)S(1)}, f32[18,8,1536]{2,1,0:T(8,128)S(1)}) custom-call(s32[1]{0:T(128)} %bitcast.1.core_ref, f32[26,8,2048]{2,1,0:T(8,128)S(1)} %shard_map.19.planes.refs_0_, bf16[13,768,256]{2,1,0:T(8,128)(2,1)S(1)} %copy-done.3, f32[26,8,2048]{2,1,0:T(8,128)} %collective-permute-done.7.other, f32[18,8,1536]{2,1,0:T(8,128)S(1)} %shard_map.21.refs_0_), custom_call_target="tpu_custom_call" | custom-call | flops 4253024256 | bytes 16285700 | tf_op jit(solution)/shard_map/pallas_call | solution.py:36
  75.7 8.6 %shard_map.26 = (f32[18,8,1536]{2,1,0:T(8,128)S(1)}, f32[18,8,1536]{2,1,0:T(8,128)S(1)}) custom-call(s32[1]{0:T(128)} %bitcast.1.core_ref, f32[26,8,2048]{2,1,0:T(8,128)S(1)} %shard_map.25.planes, bf16[13,768,256]{2,1,0:T(8,128)(2,1)S(1)} %copy-done.3, f32[26,8,2048]{2,1,0:T(8,128)} %collective-permute-done.16.other), custom_call_target="tpu_custom_call" | custom-call | flops 4253024256 | bytes 15400964 | tf_op jit(solution)/shard_map/pallas_call | solution.py:36
  84.9 7.0 %shard_map.27.mine = f32[18,8,1536]{2,1,0:T(8,128)S(1)} custom-call(f32[26,8,2048]{2,1,0:T(8,128)S(1)} %shard_map.25.planes, bf16[13,768,256]{2,1,0:T(8,128)(2,1)S(1)} %copy-done.3, f32[18,8,1536]{2,1,0:T(8,128)S(1)} %get-tuple-element.47.refs_0_), custom_call_target="tpu_custom_call" | custom-call | flops 4253024256 | bytes 13697024 | tf_op jit(solution)/shard_map/pallas_call | solution.py:36
  92.0 1.5 %collective-permute-start.10 = (f32[18,2,1408]{2,1,0:T(2,128)S(1)}, f32[18,2,1408]{2,1,0:T(2,128)S(1)}, u32[]{:S(2)}, u32[]{:S(2)}) collective-permute-start(f32[18,2,1408]{2,1,0:T(2,128)S(1)} %get-tuple-element.41), channel_id=1, source_target_pairs={{0,16},{4,20},{8,24},{12,28},{16,0},{20,4},{24,8},{28,12},{1,17},{... | collective-permute-start | bytes 608264 | tf_op jit(solution)/shard_map/ppermute | solution.py:454
  93.5 1.6 %collective-permute-start.11 = (f32[18,2,1408]{2,1,0:T(2,128)S(1)}, f32[18,2,1408]{2,1,0:T(2,128)S(1)}, u32[]{:S(2)}, u32[]{:S(2)}) collective-permute-start(f32[18,2,1408]{2,1,0:T(2,128)S(1)} %get-tuple-element.42), channel_id=1, source_target_pairs={{0,24},{4,28},{8,0},{12,4},{16,8},{20,12},{24,16},{28,20},{1,25},{... | collective-permute-start | bytes 608264 | tf_op jit(solution)/shard_map/ppermute | solution.py:454
  95.7 1.3 %collective-permute-start.19 = (f32[18,2,1408]{2,1,0:T(2,128)S(1)}, f32[18,2,1408]{2,1,0:T(2,128)S(1)}, u32[]{:S(2)}, u32[]{:S(2)}) collective-permute-start(f32[18,2,1408]{2,1,0:T(2,128)S(1)} %get-tuple-element.51), channel_id=1, source_target_pairs={{0,16},{4,20},{8,24},{12,28},{16,0},{20,4},{24,8},{28,12},{1,17},{... | collective-permute-start | bytes 608264 | tf_op jit(solution)/shard_map/ppermute | solution.py:454
  97.0 2.8 %collective-permute-start.20 = (f32[18,2,1408]{2,1,0:T(2,128)S(1)}, f32[18,2,1408]{2,1,0:T(2,128)S(1)}, u32[]{:S(2)}, u32[]{:S(2)}) collective-permute-start(f32[18,2,1408]{2,1,0:T(2,128)S(1)} %get-tuple-element.52), channel_id=1, source_target_pairs={{0,24},{4,28},{8,0},{12,4},{16,8},{20,12},{24,16},{28,20},{1,25},{... | collective-permute-start | bytes 608264 | tf_op jit(solution)/shard_map/ppermute | solution.py:454
  100.6 0.8 collective-permute-done.11.refs_3_
  101.4 4.4 %collective-permute-done.18.refs_5_ = f32[18,2,1408]{2,1,0:T(2,128)S(1)} collective-permute-done((f32[18,2,1408]{2,1,0:T(2,128)S(1)}, f32[18,2,1408]{2,1,0:T(2,128)S(1)}, u32[]{:S(2)}, u32[]{:S(2)}) %collective-permute-start.18) | collective-permute-done | bytes 202784 | tf_op jit(solution)/shard_map/ppermute | solution.py:454
  105.8 2.1 %collective-permute-done.19.refs_6_ = f32[18,2,1408]{2,1,0:T(2,128)S(1)} collective-permute-done((f32[18,2,1408]{2,1,0:T(2,128)S(1)}, f32[18,2,1408]{2,1,0:T(2,128)S(1)}, u32[]{:S(2)}, u32[]{:S(2)}) %collective-permute-start.19) | collective-permute-done | bytes 202784 | tf_op jit(solution)/shard_map/ppermute | solution.py:454
  107.9 1.2 %collective-permute-done.20.refs_7_ = f32[18,2,1408]{2,1,0:T(2,128)S(1)} collective-permute-done((f32[18,2,1408]{2,1,0:T(2,128)S(1)}, f32[18,2,1408]{2,1,0:T(2,128)S(1)}, u32[]{:S(2)}, u32[]{:S(2)}) %collective-permute-start.20) | collective-permute-done | bytes 202784 | tf_op jit(solution)/shard_map/ppermute | solution.py:454
  109.0 1.6 %shard_map.29 = f32[36,2,5184]{2,1,0:T(2,128)} custom-call(s32[1]{0:T(128)} %bitcast.chip_ref, f32[18,2,1408]{2,1,0:T(2,128)S(1)} %get-tuple-element.39.refs_0_, f32[18,2,1408]{2,1,0:T(2,128)S(1)} %collective-permute-done.9.refs_1_, f32[18,2,1408]{2,1,0:T(2,128)S(1)} %collective-permute-done.10.refs_2_, f32[18,2,1408]{2,1,0:T(2,128)S(1)} %collective-permute-done.11.refs_3_, ...), custom_call_target="tpu_custom_call" | custom-call | bytes 3115012 | tf_op jit(solution)/shard_map/pallas_call | solution.py:36
  (32 shorter events, 5.6 us)
Async XLA Ops:
  0.0 1.4 %copy-start = (f32[2,36,5184]{2,0,1:T(2,128)S(1)}, f32[2,36,5184]{2,0,1:T(2,128)}, u32[]{:S(2)}) copy-start(f32[2,36,5184]{2,0,1:T(2,128)} %param.1) | copy-start | bytes 4478980
  1.4 7.0 %copy-start.1 = (f32[2,36,5184]{2,0,1:T(2,128)S(1)}, f32[2,36,5184]{2,0,1:T(2,128)}, u32[]{:S(2)}) copy-start(f32[2,36,5184]{2,0,1:T(2,128)} %param.1) | copy-start | bytes 4478980
  3.4 26.9 %collective-permute-start.4 = (f32[22,2,2048]{2,1,0:T(2,128)S(1)}, f32[22,2,2048]{2,1,0:T(2,128)S(1)}, u32[]{:S(2)}, u32[]{:S(2)}) collective-permute-start(f32[22,2,2048]{2,1,0:T(2,128)S(1)} %get-tuple-element.34), channel_id=1, source_target_pairs={{0,24},{4,28},{8,0},{12,4},{16,8},{20,12},{24,16},{28,20},{1,25},{... | collective-permute-start | bytes 1081352 | tf_op jit(solution)/shard_map/ppermute | solution.py:454
  7.3 23.0 %collective-permute-start.5 = (f32[22,2,2048]{2,1,0:T(2,128)S(1)}, f32[22,2,2048]{2,1,0:T(2,128)S(1)}, u32[]{:S(2)}, u32[]{:S(2)}) collective-permute-start(f32[22,2,2048]{2,1,0:T(2,128)S(1)} %get-tuple-element.35), channel_id=1, source_target_pairs={{0,16},{4,20},{8,24},{12,28},{16,0},{20,4},{24,8},{28,12},{1,17},{... | collective-permute-start | bytes 1081352 | tf_op jit(solution)/shard_map/ppermute | solution.py:454
  7.8 22.5 %collective-permute-start.6 = (f32[22,2,2048]{2,1,0:T(2,128)S(1)}, f32[22,2,2048]{2,1,0:T(2,128)S(1)}, u32[]{:S(2)}, u32[]{:S(2)}) collective-permute-start(f32[22,2,2048]{2,1,0:T(2,128)S(1)} %get-tuple-element.36), channel_id=1, source_target_pairs={{0,8},{4,12},{8,16},{12,20},{16,24},{20,28},{24,0},{28,4},{1,9},{5... | collective-permute-start | bytes 1081352 | tf_op jit(solution)/shard_map/ppermute | solution.py:454
  8.5 7.2 %collective-permute-start = (f32[4,2,5184]{2,1,0:T(2,128)S(1)}, f32[4,2,5184]{2,1,0:T(2,128)S(1)}, u32[]{:S(2)}, u32[]{:S(2)}) collective-permute-start(f32[4,2,5184]{2,1,0:T(2,128)S(1)} %get-tuple-element.54), channel_id=1, source_target_pairs={{0,1},{1,2},{2,3},{3,0},{4,5},{5,6},{6,7},{7,4},{8,9},{9,10},{10,1... | collective-permute-start | bytes 497672 | tf_op jit(solution)/shard_map/ppermute | solution.py:462
  16.1 8.1 %collective-permute-start.1 = (f32[4,2,2048]{2,1,0:T(2,128)S(1)}, f32[4,2,2048]{2,1,0:T(2,128)S(1)}, u32[]{:S(2)}, u32[]{:S(2)}) collective-permute-start(f32[4,2,2048]{2,1,0:T(2,128)S(1)} %get-tuple-element.30), channel_id=1, source_target_pairs={{0,24},{4,28},{8,0},{12,4},{16,8},{20,12},{24,16},{28,20},{1,25},{... | collective-permute-start | bytes 196616 | tf_op jit(solution)/shard_map/ppermute | solution.py:454
  18.4 8.3 %collective-permute-start.2 = (f32[4,2,2048]{2,1,0:T(2,128)S(1)}, f32[4,2,2048]{2,1,0:T(2,128)S(1)}, u32[]{:S(2)}, u32[]{:S(2)}) collective-permute-start(f32[4,2,2048]{2,1,0:T(2,128)S(1)} %get-tuple-element.31), channel_id=1, source_target_pairs={{0,16},{4,20},{8,24},{12,28},{16,0},{20,4},{24,8},{28,12},{1,17},{... | collective-permute-start | bytes 196616 | tf_op jit(solution)/shard_map/ppermute | solution.py:454
  24.2 6.1 %collective-permute-start.3 = (f32[4,2,2048]{2,1,0:T(2,128)S(1)}, f32[4,2,2048]{2,1,0:T(2,128)S(1)}, u32[]{:S(2)}, u32[]{:S(2)}) collective-permute-start(f32[4,2,2048]{2,1,0:T(2,128)S(1)} %get-tuple-element.32), channel_id=1, source_target_pairs={{0,8},{4,12},{8,16},{12,20},{16,24},{20,28},{24,0},{28,4},{1,9},{5... | collective-permute-start | bytes 196616 | tf_op jit(solution)/shard_map/ppermute | solution.py:454
  26.7 6.5 %collective-permute-start.12 = (f32[4,2,5184]{2,1,0:T(2,128)S(1)}, f32[4,2,5184]{2,1,0:T(2,128)S(1)}, u32[]{:S(2)}, u32[]{:S(2)}) collective-permute-start(f32[4,2,5184]{2,1,0:T(2,128)S(1)} %get-tuple-element.53), channel_id=1, source_target_pairs={{1,0},{2,1},{3,2},{0,3},{5,4},{6,5},{7,6},{4,7},{9,8},{10,9},{11,1... | collective-permute-start | bytes 497672 | tf_op jit(solution)/shard_map/ppermute | solution.py:463
  30.8 35.5 %collective-permute-start.7 = (f32[26,8,2048]{2,1,0:T(8,128)S(1)}, f32[26,8,2048]{2,1,0:T(8,128)}, u32[]{:S(2)}, u32[]{:S(2)}) collective-permute-start(f32[26,8,2048]{2,1,0:T(8,128)S(1)} %shard_map.19.planes.refs_0_), channel_id=1, source_target_pairs={{0,4},{4,0},{8,12},{12,8},{16,20},{20,16},{24,28},{28,24},{1,5},{5... | collective-permute-start | bytes 5111816 | tf_op jit(solution)/shard_map/ppermute | solution.py:457
  34.8 9.9 %collective-permute-start.13 = (f32[18,2,2048]{2,1,0:T(2,128)S(1)}, f32[18,2,2048]{2,1,0:T(2,128)S(1)}, u32[]{:S(2)}, u32[]{:S(2)}) collective-permute-start(f32[18,2,2048]{2,1,0:T(2,128)S(1)} %get-tuple-element.44), channel_id=1, source_target_pairs={{0,24},{4,28},{8,0},{12,4},{16,8},{20,12},{24,16},{28,20},{1,25},{... | collective-permute-start | bytes 884744 | tf_op jit(solution)/shard_map/ppermute | solution.py:454
  36.4 13.3 %collective-permute-start.14 = (f32[18,2,2048]{2,1,0:T(2,128)S(1)}, f32[18,2,2048]{2,1,0:T(2,128)S(1)}, u32[]{:S(2)}, u32[]{:S(2)}) collective-permute-start(f32[18,2,2048]{2,1,0:T(2,128)S(1)} %get-tuple-element.45), channel_id=1, source_target_pairs={{0,16},{4,20},{8,24},{12,28},{16,0},{20,4},{24,8},{28,12},{1,17},{... | collective-permute-start | bytes 884744 | tf_op jit(solution)/shard_map/ppermute | solution.py:454
  36.9 12.8 %collective-permute-start.15 = (f32[18,2,2048]{2,1,0:T(2,128)S(1)}, f32[18,2,2048]{2,1,0:T(2,128)S(1)}, u32[]{:S(2)}, u32[]{:S(2)}) collective-permute-start(f32[18,2,2048]{2,1,0:T(2,128)S(1)} %get-tuple-element.46), channel_id=1, source_target_pairs={{0,8},{4,12},{8,16},{12,20},{16,24},{20,28},{24,0},{28,4},{1,9},{5... | collective-permute-start | bytes 884744 | tf_op jit(solution)/shard_map/ppermute | solution.py:454
  50.1 25.6 %collective-permute-start.16 = (f32[26,8,2048]{2,1,0:T(8,128)S(1)}, f32[26,8,2048]{2,1,0:T(8,128)}, u32[]{:S(2)}, u32[]{:S(2)}) collective-permute-start(f32[26,8,2048]{2,1,0:T(8,128)S(1)} %shard_map.25.planes), channel_id=1, source_target_pairs={{0,4},{4,0},{8,12},{12,8},{16,20},{20,16},{24,28},{28,24},{1,5},{5... | collective-permute-start | bytes 5111816 | tf_op jit(solution)/shard_map/ppermute | solution.py:457
  54.6 2.3 %copy-start.2 = (bf16[13,768,256]{2,1,0:T(8,128)(2,1)}, bf16[13,768,256]{2,1,0:T(8,128)(2,1)S(1)}, u32[]{:S(2)}) copy-start(bf16[13,768,256]{2,1,0:T(8,128)(2,1)S(1)} %shard_map.20.w_ref) | copy-start | bytes 15335428
  57.0 2.4 %copy-start.3 = (bf16[13,768,256]{2,1,0:T(8,128)(2,1)S(1)}, bf16[13,768,256]{2,1,0:T(8,128)(2,1)}, u32[]{:S(2)}) copy-start(bf16[13,768,256]{2,1,0:T(8,128)(2,1)} %copy-done.2) | copy-start | bytes 15335428
  75.1 9.3 %collective-permute-start.8 = (f32[18,8,1536]{2,1,0:T(8,128)S(1)}, f32[18,8,1536]{2,1,0:T(8,128)S(1)}, u32[]{:S(2)}, u32[]{:S(2)}) collective-permute-start(f32[18,8,1536]{2,1,0:T(8,128)S(1)} %get-tuple-element.38), channel_id=1, source_target_pairs={{0,4},{4,0},{8,12},{12,8},{16,20},{20,16},{24,28},{28,24},{1,5},{5... | collective-permute-start | bytes 2654216 | tf_op jit(solution)/shard_map/ppermute | solution.py:457
  84.3 10.8 %collective-permute-start.17 = (f32[18,8,1536]{2,1,0:T(8,128)S(1)}, f32[18,8,1536]{2,1,0:T(8,128)S(1)}, u32[]{:S(2)}, u32[]{:S(2)}) collective-permute-start(f32[18,8,1536]{2,1,0:T(8,128)S(1)} %get-tuple-element.48), channel_id=1, source_target_pairs={{0,4},{4,0},{8,12},{12,8},{16,20},{20,16},{24,28},{28,24},{1,5},{5... | collective-permute-start | bytes 2654216 | tf_op jit(solution)/shard_map/ppermute | solution.py:457
  84.5 12.4 %collective-permute-start.9 = (f32[18,2,1408]{2,1,0:T(2,128)S(1)}, f32[18,2,1408]{2,1,0:T(2,128)S(1)}, u32[]{:S(2)}, u32[]{:S(2)}) collective-permute-start(f32[18,2,1408]{2,1,0:T(2,128)S(1)} %get-tuple-element.40), channel_id=1, source_target_pairs={{0,8},{4,12},{8,16},{12,20},{16,24},{20,28},{24,0},{28,4},{1,9},{5... | collective-permute-start | bytes 608264 | tf_op jit(solution)/shard_map/ppermute | solution.py:454
  92.0 8.6 %collective-permute-start.10 = (f32[18,2,1408]{2,1,0:T(2,128)S(1)}, f32[18,2,1408]{2,1,0:T(2,128)S(1)}, u32[]{:S(2)}, u32[]{:S(2)}) collective-permute-start(f32[18,2,1408]{2,1,0:T(2,128)S(1)} %get-tuple-element.41), channel_id=1, source_target_pairs={{0,16},{4,20},{8,24},{12,28},{16,0},{20,4},{24,8},{28,12},{1,17},{... | collective-permute-start | bytes 608264 | tf_op jit(solution)/shard_map/ppermute | solution.py:454
  93.5 7.9 %collective-permute-start.11 = (f32[18,2,1408]{2,1,0:T(2,128)S(1)}, f32[18,2,1408]{2,1,0:T(2,128)S(1)}, u32[]{:S(2)}, u32[]{:S(2)}) collective-permute-start(f32[18,2,1408]{2,1,0:T(2,128)S(1)} %get-tuple-element.42), channel_id=1, source_target_pairs={{0,24},{4,28},{8,0},{12,4},{16,8},{20,12},{24,16},{28,20},{1,25},{... | collective-permute-start | bytes 608264 | tf_op jit(solution)/shard_map/ppermute | solution.py:454
  95.3 10.5 %collective-permute-start.18 = (f32[18,2,1408]{2,1,0:T(2,128)S(1)}, f32[18,2,1408]{2,1,0:T(2,128)S(1)}, u32[]{:S(2)}, u32[]{:S(2)}) collective-permute-start(f32[18,2,1408]{2,1,0:T(2,128)S(1)} %get-tuple-element.50), channel_id=1, source_target_pairs={{0,8},{4,12},{8,16},{12,20},{16,24},{20,28},{24,0},{28,4},{1,9},{5... | collective-permute-start | bytes 608264 | tf_op jit(solution)/shard_map/ppermute | solution.py:454
  95.7 12.1 %collective-permute-start.19 = (f32[18,2,1408]{2,1,0:T(2,128)S(1)}, f32[18,2,1408]{2,1,0:T(2,128)S(1)}, u32[]{:S(2)}, u32[]{:S(2)}) collective-permute-start(f32[18,2,1408]{2,1,0:T(2,128)S(1)} %get-tuple-element.51), channel_id=1, source_target_pairs={{0,16},{4,20},{8,24},{12,28},{16,0},{20,4},{24,8},{28,12},{1,17},{... | collective-permute-start | bytes 608264 | tf_op jit(solution)/shard_map/ppermute | solution.py:454
  97.0 12.1 %collective-permute-start.20 = (f32[18,2,1408]{2,1,0:T(2,128)S(1)}, f32[18,2,1408]{2,1,0:T(2,128)S(1)}, u32[]{:S(2)}, u32[]{:S(2)}) collective-permute-start(f32[18,2,1408]{2,1,0:T(2,128)S(1)} %get-tuple-element.52), channel_id=1, source_target_pairs={{0,24},{4,28},{8,0},{12,4},{16,8},{20,12},{24,16},{28,20},{1,25},{... | collective-permute-start | bytes 608264 | tf_op jit(solution)/shard_map/ppermute | solution.py:454

commit v5 on v4

--- a/solution.py
+++ b/solution.py
@@ -14,7 +14,6 @@
 WINDOW = 3 * TILE
 REACH = 2
 HALO = 4
-KERNEL_MIB = 36
 CHUNKS = 2
 STEP = 2
 CENTRE = 8.5
@@ -145,8 +144,8 @@
     )
 
 
-def gather_body(groups, kept, *refs):
-    out = refs[-1]
+def gather_body(groups, kept, unread, *refs):
+    refs, out = refs[unread:], refs[-1]
     row = 0
     if kept:
         before = refs[0]
@@ -168,13 +167,13 @@
         row += ins[0].shape[0]
 
 
-def gather(groups, before=None, kept=0):
+def gather(groups, before=None, kept=0, alive=()):
     depth = kept + sum(g[0].shape[0] for g in groups)
     _, orbs, span = groups[0][0].shape
     return call(
-        functools.partial(gather_body, len(groups), kept),
+        functools.partial(gather_body, len(groups), kept, len(alive)),
         [sds(depth, orbs * len(groups[0]), span)],
-        [*([before] if kept else []), *(p for g in groups for p in g)],
+        [*alive, *([before] if kept else []), *(p for g in groups for p in g)],
     )[0]
 
 
@@ -370,12 +369,12 @@
     potentials(ranges, planes, (planes, planes), pairings, w_ref, work, finish)
 
 
-def cross_body(ranges, follows, core_ref, planes, w_ref, other, *refs):
+def cross_body(ranges, follows, chip_ref, planes, w_ref, other, *refs):
     acc_in = refs[0] if follows else None
     acc, travel, *work = refs[1:] if follows else refs
     depth, n_rows, _ = planes.shape
     inner = slice(HALO, depth - HALO)
-    odd = core_ref[0] == 1
+    odd = chip_ref[1] == 1
     pairings = (
         Pairing(n_rows, jnp.where(odd, 0, 2)),
         Pairing(n_rows, jnp.where(odd, n_rows - 1, 1), jnp.where(odd, 1, 3)),
@@ -445,8 +444,7 @@
     chips = n_band // 2
     ranges = Ranges(chips, total)
     index = lax.axis_index("band")
-    chip = (index // 2).astype(jnp.int32).reshape(1)
-    core = (index % 2).astype(jnp.int32).reshape(1)
+    chip = jnp.stack([index // 2, index % 2]).astype(jnp.int32)
     planes = jnp.transpose(orbitals, (1, 0, 2))
 
     def along(value, steps):
@@ -482,7 +480,6 @@
     got_low = fetch([(below, 0, HALO)])
     got_b = fetch([(planes, cut, depth), (above, 0, HALO)])
     planes_a = gather([got_low, got_a])
-    planes_b = gather([got_b], before=planes_a, kept=2 * HALO)
 
     rows = orbs * chips
     full, swept = (inner + 2 * HALO) * rows, (inner + 2 * REACH) * rows
@@ -503,18 +500,18 @@
             [mine, banded, *acc],
             scratch=work,
             flops=flops,
-            limit=KERNEL_MIB,
+            limit=12 + 12 * (rows // 8),
         )[0]
 
     def cross(mine, other, *acc):
         own, travel = call(
             functools.partial(cross_body, ranges, bool(acc)),
             [result, result],
-            [core, mine, banded, other, *acc],
+            [chip, mine, banded, other, *acc],
             scratch=work,
             flops=flops,
             smem=True,
-            limit=KERNEL_MIB,
+            limit=12 + 12 * (rows // 8),
         )
         return own, partner_core(travel)
 
@@ -529,6 +526,7 @@
 
     other_a = partner_core(planes_a)
     acc_a = same(planes_a)
+    planes_b = gather([got_b], before=planes_a, kept=2 * HALO, alive=(banded, acc_a))
     other_b = partner_core(planes_b)
     acc_a, back_a = cross(planes_a, other_a, acc_a)
     acc_b, back_b = cross(planes_b, other_b)

time: 113 us -> 98.4 us (0.87)
  the two profiles are of different devices: /device:TPU:0 before, /device:TPU:26 now
where the time goes in v5:
time: 98.4 us; the launch traced here: 98.3 us
  Pallas kernels  45 us (46%)
  waiting for transfers between devices  32.1 us (33%)
  starting transfers between devices  19.5 us (20%)
  local copies, waits for them, and re-layouts  1.41 us (1%)
    pallas_call x13, Pallas kernels, call(): pl.pallas_call(body, out_shape=out, in_specs=specs, out_specs=[VMEM] * le...  45 us
    ppermute x15, waiting for transfers between devices, along(): return lax.ppermute(value, 'band', pairs)  25.2 us
    ppermute x15, starting transfers between devices, along(): return lax.ppermute(value, 'band', pairs)  16.6 us
    ppermute x1, waiting for transfers between devices, per_device(): below = lax.ppermute(planes[depth - HALO:], 'slab', up)  6.88 us
  transfers between devices with their start and end apart: 21, of which 6 were waited for; matrix products, arithmetic and copies ran while one was open for 0% of the time, Pallas kernels for 40%

profile of v5, /device:TPU:26, one launch (start us, length us, event | category | flops | bytes accessed | tf_op | source)
XLA Modules:
  0.0 98.3 jit_solution(16446549940002677436)
XLA Ops:
  0.1 1.4 %copy-done = f32[2,36,5184]{2,0,1:T(2,128)S(1)} copy-done((f32[2,36,5184]{2,0,1:T(2,128)S(1)}, f32[2,36,5184]{2,0,1:T(2,128)}, u32[]{:S(2)}) %copy-start) | copy-done | bytes 1493016
  1.5 2.5 %shard_map.18 = (f32[22,2,2048]{2,1,0:T(2,128)S(1)}, f32[22,2,2048]{2,1,0:T(2,128)S(1)}, f32[22,2,2048]{2,1,0:T(2,128)S(1)}, f32[22,2,2048]{2,1,0:T(2,128)S(1)}) custom-call(s32[2]{0:T(128)S(1)} %pad_add_fusion.chip_ref, f32[36,2,5184]{2,1,0:T(2,128)S(1)} %bitcast.4), custom_call_target="tpu_custom_call" | custom-call | bytes 2934792 | tf_op jit(solution)/shard_map/pallas_call | solution.py:35
  4.0 0.5 collective-permute-start.4
  4.5 1.6 %collective-permute-start.5 = (f32[22,2,2048]{2,1,0:T(2,128)S(1)}, f32[22,2,2048]{2,1,0:T(2,128)S(1)}, u32[]{:S(2)}, u32[]{:S(2)}) collective-permute-start(f32[22,2,2048]{2,1,0:T(2,128)S(1)} %get-tuple-element.35), channel_id=1, source_target_pairs={{0,16},{4,20},{8,24},{12,28},{16,0},{20,4},{24,8},{28,12},{1,17},{... | collective-permute-start | bytes 1081352 | tf_op jit(solution)/shard_map/ppermute | solution.py:452
  6.1 2.4 %collective-permute-start.6 = (f32[22,2,2048]{2,1,0:T(2,128)S(1)}, f32[22,2,2048]{2,1,0:T(2,128)S(1)}, u32[]{:S(2)}, u32[]{:S(2)}) collective-permute-start(f32[22,2,2048]{2,1,0:T(2,128)S(1)} %get-tuple-element.36), channel_id=1, source_target_pairs={{0,8},{4,12},{8,16},{12,20},{16,24},{20,28},{24,0},{28,4},{1,9},{5... | collective-permute-start | bytes 1081352 | tf_op jit(solution)/shard_map/ppermute | solution.py:452
  8.8 1.8 %collective-permute-start.12 = (f32[4,2,5184]{2,1,0:T(2,128)S(1)}, f32[4,2,5184]{2,1,0:T(2,128)S(1)}, u32[]{:S(2)}, u32[]{:S(2)}) collective-permute-start(f32[4,2,5184]{2,1,0:T(2,128)S(1)} %get-tuple-element.53), channel_id=1, source_target_pairs={{1,0},{2,1},{3,2},{0,3},{5,4},{6,5},{7,6},{4,7},{9,8},{10,9},{11,1... | collective-permute-start | bytes 497672 | tf_op jit(solution)/shard_map/ppermute | solution.py:461
  10.6 6.9 %collective-permute-done.refs_0_ = f32[4,2,5184]{2,1,0:T(2,128)S(1)} collective-permute-done((f32[4,2,5184]{2,1,0:T(2,128)S(1)}, f32[4,2,5184]{2,1,0:T(2,128)S(1)}, u32[]{:S(2)}, u32[]{:S(2)}) %collective-permute-start) | collective-permute-done | bytes 165920 | tf_op jit(solution)/shard_map/ppermute | solution.py:460
  17.5 1.0 shard_map.17
  18.5 0.7 collective-permute-start.2
  19.2 5.1 %collective-permute-done.1.refs_1_ = f32[4,2,2048]{2,1,0:T(2,128)S(1)} collective-permute-done((f32[4,2,2048]{2,1,0:T(2,128)S(1)}, f32[4,2,2048]{2,1,0:T(2,128)S(1)}, u32[]{:S(2)}, u32[]{:S(2)}) %collective-permute-start.1) | collective-permute-done | bytes 65568 | tf_op jit(solution)/shard_map/ppermute | solution.py:452
  24.9 5.0 %shard_map.20.w_ref.refs_0_ = bf16[13,768,256]{2,1,0:T(8,128)(2,1)S(1)} custom-call(s32[2]{0:T(128)S(1)} %pad_add_fusion.chip_ref), custom_call_target="tpu_custom_call" | custom-call | bytes 10223624 | tf_op jit(solution)/shard_map/pallas_call | solution.py:35
  29.9 2.2 %shard_map.24 = (f32[18,2,2048]{2,1,0:T(2,128)S(1)}, f32[18,2,2048]{2,1,0:T(2,128)S(1)}, f32[18,2,2048]{2,1,0:T(2,128)S(1)}, f32[18,2,2048]{2,1,0:T(2,128)S(1)}) custom-call(s32[2]{0:T(128)S(1)} %pad_add_fusion.chip_ref, f32[36,2,5184]{2,1,0:T(2,128)S(1)} %bitcast.6, f32[4,2,5184]{2,1,0:T(2,128)S(1)} %collective-permute-done.12.refs_1_), custom_call_target="tpu_custom_call" | custom-call | bytes 2838536 | tf_op jit(solution)/shard_map/pallas_call | solution.py:35
  32.1 0.5 shard_map.19.planes.refs_2_
  32.7 1.6 %collective-permute-start.13 = (f32[18,2,2048]{2,1,0:T(2,128)S(1)}, f32[18,2,2048]{2,1,0:T(2,128)S(1)}, u32[]{:S(2)}, u32[]{:S(2)}) collective-permute-start(f32[18,2,2048]{2,1,0:T(2,128)S(1)} %get-tuple-element.44), channel_id=1, source_target_pairs={{0,24},{4,28},{8,0},{12,4},{16,8},{20,12},{24,16},{28,20},{1,25},{... | collective-permute-start | bytes 884744 | tf_op jit(solution)/shard_map/ppermute | solution.py:452
  34.3 1.5 %collective-permute-start.14 = (f32[18,2,2048]{2,1,0:T(2,128)S(1)}, f32[18,2,2048]{2,1,0:T(2,128)S(1)}, u32[]{:S(2)}, u32[]{:S(2)}) collective-permute-start(f32[18,2,2048]{2,1,0:T(2,128)S(1)} %get-tuple-element.45), channel_id=1, source_target_pairs={{0,16},{4,20},{8,24},{12,28},{16,0},{20,4},{24,8},{28,12},{1,17},{... | collective-permute-start | bytes 884744 | tf_op jit(solution)/shard_map/ppermute | solution.py:452
  35.8 0.9 collective-permute-start.15
  36.7 7.0 %shard_map.21.refs_0_.refs_1_ = f32[18,8,1536]{2,1,0:T(8,128)S(1)} custom-call(f32[26,8,2048]{2,1,0:T(8,128)S(1)} %shard_map.19.planes.refs_2_, bf16[13,768,256]{2,1,0:T(8,128)(2,1)S(1)} %shard_map.20.w_ref.refs_0_), custom_call_target="tpu_custom_call" | custom-call | flops 4253024256 | bytes 12812288 | tf_op jit(solution)/shard_map/pallas_call | solution.py:35
  43.8 5.6 %collective-permute-done.14.refs_5_ = f32[18,2,2048]{2,1,0:T(2,128)S(1)} collective-permute-done((f32[18,2,2048]{2,1,0:T(2,128)S(1)}, f32[18,2,2048]{2,1,0:T(2,128)S(1)}, u32[]{:S(2)}, u32[]{:S(2)}) %collective-permute-start.14) | collective-permute-done | bytes 294944 | tf_op jit(solution)/shard_map/ppermute | solution.py:452
  49.9 7.8 %shard_map.22 = (f32[18,8,1536]{2,1,0:T(8,128)S(1)}, f32[18,8,1536]{2,1,0:T(8,128)S(1)}) custom-call(s32[2]{0:T(128)S(1)} %pad_add_fusion.chip_ref, f32[26,8,2048]{2,1,0:T(8,128)S(1)} %shard_map.19.planes.refs_2_, bf16[13,768,256]{2,1,0:T(8,128)(2,1)S(1)} %shard_map.20.w_ref.refs_0_, f32[26,8,2048]{2,1,0:T(8,128)S(1)} %collective-permute-done.7.other, ...), custom_call_target="tpu_custom_call" | custom-call | flops 4253024256 | bytes 16285704 | tf_op jit(solution)/shard_map/pallas_call | solution.py:35
  57.7 0.5 collective-permute-start.8
  58.3 7.8 %shard_map.26 = (f32[18,8,1536]{2,1,0:T(8,128)S(1)}, f32[18,8,1536]{2,1,0:T(8,128)S(1)}) custom-call(s32[2]{0:T(128)S(1)} %pad_add_fusion.chip_ref, f32[26,8,2048]{2,1,0:T(8,128)S(1)} %shard_map.25.planes, bf16[13,768,256]{2,1,0:T(8,128)(2,1)S(1)} %shard_map.20.w_ref.refs_0_, f32[26,8,2048]{2,1,0:T(8,128)S(1)} %collective-permute-done.16.other), custom_call_target="tpu_custom_call" | custom-call | flops 4253024256 | bytes 15400968 | tf_op jit(solution)/shard_map/pallas_call | solution.py:35
  66.2 0.7 shard_map.23
  66.9 1.8 %collective-permute-start.9 = (f32[18,2,1408]{2,1,0:T(2,128)S(1)}, f32[18,2,1408]{2,1,0:T(2,128)S(1)}, u32[]{:S(2)}, u32[]{:S(2)}) collective-permute-start(f32[18,2,1408]{2,1,0:T(2,128)S(1)} %get-tuple-element.40), channel_id=1, source_target_pairs={{0,8},{4,12},{8,16},{12,20},{16,24},{20,28},{24,0},{28,4},{1,9},{5... | collective-permute-start | bytes 608264 | tf_op jit(solution)/shard_map/ppermute | solution.py:452
  68.7 7.1 %shard_map.27.mine = f32[18,8,1536]{2,1,0:T(8,128)S(1)} custom-call(f32[26,8,2048]{2,1,0:T(8,128)S(1)} %shard_map.25.planes, bf16[13,768,256]{2,1,0:T(8,128)(2,1)S(1)} %shard_map.20.w_ref.refs_0_, f32[18,8,1536]{2,1,0:T(8,128)S(1)} %get-tuple-element.47.refs_0_), custom_call_target="tpu_custom_call" | custom-call | flops 4253024256 | bytes 13697024 | tf_op jit(solution)/shard_map/pallas_call | solution.py:35
  75.8 1.4 %collective-permute-start.10 = (f32[18,2,1408]{2,1,0:T(2,128)S(1)}, f32[18,2,1408]{2,1,0:T(2,128)S(1)}, u32[]{:S(2)}, u32[]{:S(2)}) collective-permute-start(f32[18,2,1408]{2,1,0:T(2,128)S(1)} %get-tuple-element.41), channel_id=1, source_target_pairs={{0,16},{4,20},{8,24},{12,28},{16,0},{20,4},{24,8},{28,12},{1,17},{... | collective-permute-start | bytes 608264 | tf_op jit(solution)/shard_map/ppermute | solution.py:452
  77.2 0.7 shard_map.28
  77.9 3.0 %collective-permute-start.18 = (f32[18,2,1408]{2,1,0:T(2,128)S(1)}, f32[18,2,1408]{2,1,0:T(2,128)S(1)}, u32[]{:S(2)}, u32[]{:S(2)}) collective-permute-start(f32[18,2,1408]{2,1,0:T(2,128)S(1)} %get-tuple-element.50), channel_id=1, source_target_pairs={{0,8},{4,12},{8,16},{12,20},{16,24},{20,28},{24,0},{28,4},{1,9},{5... | collective-permute-start | bytes 608264 | tf_op jit(solution)/shard_map/ppermute | solution.py:452
  80.9 0.7 collective-permute-start.19
  81.6 6.5 %collective-permute-done.10.refs_2_ = f32[18,2,1408]{2,1,0:T(2,128)S(1)} collective-permute-done((f32[18,2,1408]{2,1,0:T(2,128)S(1)}, f32[18,2,1408]{2,1,0:T(2,128)S(1)}, u32[]{:S(2)}, u32[]{:S(2)}) %collective-permute-start.10) | collective-permute-done | bytes 202784 | tf_op jit(solution)/shard_map/ppermute | solution.py:452
  88.1 1.5 %collective-permute-done.18.refs_5_ = f32[18,2,1408]{2,1,0:T(2,128)S(1)} collective-permute-done((f32[18,2,1408]{2,1,0:T(2,128)S(1)}, f32[18,2,1408]{2,1,0:T(2,128)S(1)}, u32[]{:S(2)}, u32[]{:S(2)}) %collective-permute-start.18) | collective-permute-done | bytes 202784 | tf_op jit(solution)/shard_map/ppermute | solution.py:452
  89.6 6.5 %collective-permute-done.19.refs_6_ = f32[18,2,1408]{2,1,0:T(2,128)S(1)} collective-permute-done((f32[18,2,1408]{2,1,0:T(2,128)S(1)}, f32[18,2,1408]{2,1,0:T(2,128)S(1)}, u32[]{:S(2)}, u32[]{:S(2)}) %collective-permute-start.19) | collective-permute-done | bytes 202784 | tf_op jit(solution)/shard_map/ppermute | solution.py:452
  96.1 2.2 %shard_map.29 = f32[36,2,5184]{2,1,0:T(2,128)} custom-call(s32[2]{0:T(128)S(1)} %pad_add_fusion.chip_ref, f32[18,2,1408]{2,1,0:T(2,128)S(1)} %get-tuple-element.39.refs_0_, f32[18,2,1408]{2,1,0:T(2,128)S(1)} %collective-permute-done.9.refs_1_, f32[18,2,1408]{2,1,0:T(2,128)S(1)} %collective-permute-done.10.refs_2_, ...), custom_call_target="tpu_custom_call" | custom-call | bytes 3115016 | tf_op jit(solution)/shard_map/pallas_call | solution.py:35
  (29 shorter events, 1.7 us)
Async XLA Ops:
  0.1 1.4 %copy-start = (f32[2,36,5184]{2,0,1:T(2,128)S(1)}, f32[2,36,5184]{2,0,1:T(2,128)}, u32[]{:S(2)}) copy-start(f32[2,36,5184]{2,0,1:T(2,128)} %param.1) | copy-start | bytes 4478980
  1.5 7.0 %copy-start.1 = (f32[2,36,5184]{2,0,1:T(2,128)S(1)}, f32[2,36,5184]{2,0,1:T(2,128)}, u32[]{:S(2)}) copy-start(f32[2,36,5184]{2,0,1:T(2,128)} %param.1) | copy-start | bytes 4478980
  4.0 28.1 %collective-permute-start.4 = (f32[22,2,2048]{2,1,0:T(2,128)S(1)}, f32[22,2,2048]{2,1,0:T(2,128)S(1)}, u32[]{:S(2)}, u32[]{:S(2)}) collective-permute-start(f32[22,2,2048]{2,1,0:T(2,128)S(1)} %get-tuple-element.34), channel_id=1, source_target_pairs={{0,24},{4,28},{8,0},{12,4},{16,8},{20,12},{24,16},{28,20},{1,25},{... | collective-permute-start | bytes 1081352 | tf_op jit(solution)/shard_map/ppermute | solution.py:452
  4.5 27.6 %collective-permute-start.5 = (f32[22,2,2048]{2,1,0:T(2,128)S(1)}, f32[22,2,2048]{2,1,0:T(2,128)S(1)}, u32[]{:S(2)}, u32[]{:S(2)}) collective-permute-start(f32[22,2,2048]{2,1,0:T(2,128)S(1)} %get-tuple-element.35), channel_id=1, source_target_pairs={{0,16},{4,20},{8,24},{12,28},{16,0},{20,4},{24,8},{28,12},{1,17},{... | collective-permute-start | bytes 1081352 | tf_op jit(solution)/shard_map/ppermute | solution.py:452
  6.1 26.0 %collective-permute-start.6 = (f32[22,2,2048]{2,1,0:T(2,128)S(1)}, f32[22,2,2048]{2,1,0:T(2,128)S(1)}, u32[]{:S(2)}, u32[]{:S(2)}) collective-permute-start(f32[22,2,2048]{2,1,0:T(2,128)S(1)} %get-tuple-element.36), channel_id=1, source_target_pairs={{0,8},{4,12},{8,16},{12,20},{16,24},{20,28},{24,0},{28,4},{1,9},{5... | collective-permute-start | bytes 1081352 | tf_op jit(solution)/shard_map/ppermute | solution.py:452
  8.5 9.0 %collective-permute-start = (f32[4,2,5184]{2,1,0:T(2,128)S(1)}, f32[4,2,5184]{2,1,0:T(2,128)S(1)}, u32[]{:S(2)}, u32[]{:S(2)}) collective-permute-start(f32[4,2,5184]{2,1,0:T(2,128)S(1)} %get-tuple-element.54), channel_id=1, source_target_pairs={{0,1},{1,2},{2,3},{3,0},{4,5},{5,6},{6,7},{7,4},{8,9},{9,10},{10,1... | collective-permute-start | bytes 497672 | tf_op jit(solution)/shard_map/ppermute | solution.py:460
  8.8 9.7 %collective-permute-start.12 = (f32[4,2,5184]{2,1,0:T(2,128)S(1)}, f32[4,2,5184]{2,1,0:T(2,128)S(1)}, u32[]{:S(2)}, u32[]{:S(2)}) collective-permute-start(f32[4,2,5184]{2,1,0:T(2,128)S(1)} %get-tuple-element.53), channel_id=1, source_target_pairs={{1,0},{2,1},{3,2},{0,3},{5,4},{6,5},{7,6},{4,7},{9,8},{10,9},{11,1... | collective-permute-start | bytes 497672 | tf_op jit(solution)/shard_map/ppermute | solution.py:461
  18.4 5.9 %collective-permute-start.1 = (f32[4,2,2048]{2,1,0:T(2,128)S(1)}, f32[4,2,2048]{2,1,0:T(2,128)S(1)}, u32[]{:S(2)}, u32[]{:S(2)}) collective-permute-start(f32[4,2,2048]{2,1,0:T(2,128)S(1)} %get-tuple-element.30), channel_id=1, source_target_pairs={{0,24},{4,28},{8,0},{12,4},{16,8},{20,12},{24,16},{28,20},{1,25},{... | collective-permute-start | bytes 196616 | tf_op jit(solution)/shard_map/ppermute | solution.py:452
  18.5 13.6 %collective-permute-start.2 = (f32[4,2,2048]{2,1,0:T(2,128)S(1)}, f32[4,2,2048]{2,1,0:T(2,128)S(1)}, u32[]{:S(2)}, u32[]{:S(2)}) collective-permute-start(f32[4,2,2048]{2,1,0:T(2,128)S(1)} %get-tuple-element.31), channel_id=1, source_target_pairs={{0,16},{4,20},{8,24},{12,28},{16,0},{20,4},{24,8},{28,12},{1,17},{... | collective-permute-start | bytes 196616 | tf_op jit(solution)/shard_map/ppermute | solution.py:452
  24.4 7.7 %collective-permute-start.3 = (f32[4,2,2048]{2,1,0:T(2,128)S(1)}, f32[4,2,2048]{2,1,0:T(2,128)S(1)}, u32[]{:S(2)}, u32[]{:S(2)}) collective-permute-start(f32[4,2,2048]{2,1,0:T(2,128)S(1)} %get-tuple-element.32), channel_id=1, source_target_pairs={{0,8},{4,12},{8,16},{12,20},{16,24},{20,28},{24,0},{28,4},{1,9},{5... | collective-permute-start | bytes 196616 | tf_op jit(solution)/shard_map/ppermute | solution.py:452
  32.7 17.2 %collective-permute-start.7 = (f32[26,8,2048]{2,1,0:T(8,128)S(1)}, f32[26,8,2048]{2,1,0:T(8,128)S(1)}, u32[]{:S(2)}, u32[]{:S(2)}) collective-permute-start(f32[26,8,2048]{2,1,0:T(8,128)S(1)} %shard_map.19.planes.refs_2_), channel_id=1, source_target_pairs={{0,4},{4,0},{8,12},{12,8},{16,20},{20,16},{24,28},{28,24},{1,5},{5... | collective-permute-start | bytes 5111816 | tf_op jit(solution)/shard_map/ppermute | solution.py:455
  32.7 11.0 %collective-permute-start.13 = (f32[18,2,2048]{2,1,0:T(2,128)S(1)}, f32[18,2,2048]{2,1,0:T(2,128)S(1)}, u32[]{:S(2)}, u32[]{:S(2)}) collective-permute-start(f32[18,2,2048]{2,1,0:T(2,128)S(1)} %get-tuple-element.44), channel_id=1, source_target_pairs={{0,24},{4,28},{8,0},{12,4},{16,8},{20,12},{24,16},{28,20},{1,25},{... | collective-permute-start | bytes 884744 | tf_op jit(solution)/shard_map/ppermute | solution.py:452
  34.3 15.1 %collective-permute-start.14 = (f32[18,2,2048]{2,1,0:T(2,128)S(1)}, f32[18,2,2048]{2,1,0:T(2,128)S(1)}, u32[]{:S(2)}, u32[]{:S(2)}) collective-permute-start(f32[18,2,2048]{2,1,0:T(2,128)S(1)} %get-tuple-element.45), channel_id=1, source_target_pairs={{0,16},{4,20},{8,24},{12,28},{16,0},{20,4},{24,8},{28,12},{1,17},{... | collective-permute-start | bytes 884744 | tf_op jit(solution)/shard_map/ppermute | solution.py:452
  35.8 13.5 %collective-permute-start.15 = (f32[18,2,2048]{2,1,0:T(2,128)S(1)}, f32[18,2,2048]{2,1,0:T(2,128)S(1)}, u32[]{:S(2)}, u32[]{:S(2)}) collective-permute-start(f32[18,2,2048]{2,1,0:T(2,128)S(1)} %get-tuple-element.46), channel_id=1, source_target_pairs={{0,8},{4,12},{8,16},{12,20},{16,24},{20,28},{24,0},{28,4},{1,9},{5... | collective-permute-start | bytes 884744 | tf_op jit(solution)/shard_map/ppermute | solution.py:452
  49.8 8.5 %collective-permute-start.16 = (f32[26,8,2048]{2,1,0:T(8,128)S(1)}, f32[26,8,2048]{2,1,0:T(8,128)S(1)}, u32[]{:S(2)}, u32[]{:S(2)}) collective-permute-start(f32[26,8,2048]{2,1,0:T(8,128)S(1)} %shard_map.25.planes), channel_id=1, source_target_pairs={{0,4},{4,0},{8,12},{12,8},{16,20},{20,16},{24,28},{28,24},{1,5},{5... | collective-permute-start | bytes 5111816 | tf_op jit(solution)/shard_map/ppermute | solution.py:455
  57.7 8.5 %collective-permute-start.8 = (f32[18,8,1536]{2,1,0:T(8,128)S(1)}, f32[18,8,1536]{2,1,0:T(8,128)S(1)}, u32[]{:S(2)}, u32[]{:S(2)}) collective-permute-start(f32[18,8,1536]{2,1,0:T(8,128)S(1)} %get-tuple-element.38), channel_id=1, source_target_pairs={{0,4},{4,0},{8,12},{12,8},{16,20},{20,16},{24,28},{28,24},{1,5},{5... | collective-permute-start | bytes 2654216 | tf_op jit(solution)/shard_map/ppermute | solution.py:455
  66.1 11.1 %collective-permute-start.17 = (f32[18,8,1536]{2,1,0:T(8,128)S(1)}, f32[18,8,1536]{2,1,0:T(8,128)S(1)}, u32[]{:S(2)}, u32[]{:S(2)}) collective-permute-start(f32[18,8,1536]{2,1,0:T(8,128)S(1)} %get-tuple-element.48), channel_id=1, source_target_pairs={{0,4},{4,0},{8,12},{12,8},{16,20},{20,16},{24,28},{28,24},{1,5},{5... | collective-permute-start | bytes 2654216 | tf_op jit(solution)/shard_map/ppermute | solution.py:455
  66.9 14.7 %collective-permute-start.9 = (f32[18,2,1408]{2,1,0:T(2,128)S(1)}, f32[18,2,1408]{2,1,0:T(2,128)S(1)}, u32[]{:S(2)}, u32[]{:S(2)}) collective-permute-start(f32[18,2,1408]{2,1,0:T(2,128)S(1)} %get-tuple-element.40), channel_id=1, source_target_pairs={{0,8},{4,12},{8,16},{12,20},{16,24},{20,28},{24,0},{28,4},{1,9},{5... | collective-permute-start | bytes 608264 | tf_op jit(solution)/shard_map/ppermute | solution.py:452
  75.8 12.3 %collective-permute-start.10 = (f32[18,2,1408]{2,1,0:T(2,128)S(1)}, f32[18,2,1408]{2,1,0:T(2,128)S(1)}, u32[]{:S(2)}, u32[]{:S(2)}) collective-permute-start(f32[18,2,1408]{2,1,0:T(2,128)S(1)} %get-tuple-element.41), channel_id=1, source_target_pairs={{0,16},{4,20},{8,24},{12,28},{16,0},{20,4},{24,8},{28,12},{1,17},{... | collective-permute-start | bytes 608264 | tf_op jit(solution)/shard_map/ppermute | solution.py:452
  77.2 11.0 %collective-permute-start.11 = (f32[18,2,1408]{2,1,0:T(2,128)S(1)}, f32[18,2,1408]{2,1,0:T(2,128)S(1)}, u32[]{:S(2)}, u32[]{:S(2)}) collective-permute-start(f32[18,2,1408]{2,1,0:T(2,128)S(1)} %get-tuple-element.42), channel_id=1, source_target_pairs={{0,24},{4,28},{8,0},{12,4},{16,8},{20,12},{24,16},{28,20},{1,25},{... | collective-permute-start | bytes 608264 | tf_op jit(solution)/shard_map/ppermute | solution.py:452
  77.9 11.7 %collective-permute-start.18 = (f32[18,2,1408]{2,1,0:T(2,128)S(1)}, f32[18,2,1408]{2,1,0:T(2,128)S(1)}, u32[]{:S(2)}, u32[]{:S(2)}) collective-permute-start(f32[18,2,1408]{2,1,0:T(2,128)S(1)} %get-tuple-element.50), channel_id=1, source_target_pairs={{0,8},{4,12},{8,16},{12,20},{16,24},{20,28},{24,0},{28,4},{1,9},{5... | collective-permute-start | bytes 608264 | tf_op jit(solution)/shard_map/ppermute | solution.py:452
  80.9 15.2 %collective-permute-start.19 = (f32[18,2,1408]{2,1,0:T(2,128)S(1)}, f32[18,2,1408]{2,1,0:T(2,128)S(1)}, u32[]{:S(2)}, u32[]{:S(2)}) collective-permute-start(f32[18,2,1408]{2,1,0:T(2,128)S(1)} %get-tuple-element.51), channel_id=1, source_target_pairs={{0,16},{4,20},{8,24},{12,28},{16,0},{20,4},{24,8},{28,12},{1,17},{... | collective-permute-start | bytes 608264 | tf_op jit(solution)/shard_map/ppermute | solution.py:452
  81.6 14.4 %collective-permute-start.20 = (f32[18,2,1408]{2,1,0:T(2,128)S(1)}, f32[18,2,1408]{2,1,0:T(2,128)S(1)}, u32[]{:S(2)}, u32[]{:S(2)}) collective-permute-start(f32[18,2,1408]{2,1,0:T(2,128)S(1)} %get-tuple-element.52), channel_id=1, source_target_pairs={{0,24},{4,28},{8,0},{12,4},{16,8},{20,12},{24,16},{28,20},{1,25},{... | collective-permute-start | bytes 608264 | tf_op jit(solution)/shard_map/ppermute | solution.py:452

commit v6 on v5

--- a/solution.py
+++ b/solution.py
@@ -259,7 +259,7 @@
 
 
 def potentials(ranges, first, seconds, pairings, w_ref, work, finish):
-    rho_split, rho, mid_split, mid, product = work
+    rho_split, rho, mid_split, mid, *products = work
     depth, n_rows, span = first.shape
     inner = depth - 2 * HALO
     swept = inner + 2 * REACH
@@ -281,14 +281,14 @@
 
     lax.fori_loop(0, depth // STEP, density, 0)
 
-    def in_plane(source, planes, start, weight):
+    def in_plane(source, planes, start, weight, product):
         lanes = aligned(start - TILE + pad, WINDOW)
         rows = planes * n_rows
         value = source[:, :, REACH * n_rows : REACH * n_rows + rows, lanes]
         value = value.reshape(2 * kinds * rows, WINDOW)
         product[0 : 2 * kinds * rows] = jnp.dot(value, weight, preferred_element_type=jnp.float32)
 
-    def off(source, k, planes, start):
+    def off(source, k, planes, start, product):
         rows = planes * n_rows
 
         def shifted(z):
@@ -300,31 +300,41 @@
         inside = product[row : row + rows] + product[row + rows : row + 2 * rows]
         return inside + (16.0 * near - far)
 
-    def sweep(t, _):
+    def pipelined(count, multiply, use):
+        multiply(0, products[0])
+        for t in range(count):
+            if t + 1 < count:
+                multiply(t + 1, products[(t + 1) % 2])
+            use(t, products[t % 2])
+
+    def multiply_1(t, product):
+        in_plane(rho_split, swept, ranges.first + t * TILE, w_ref[t], product)
+
+    def use_1(t, product):
         start = ranges.first + t * TILE
-        in_plane(rho_split, swept, start, w_ref[t])
         for k in range(kinds):
-            value = off(rho, k, swept, start)
+            value = off(rho, k, swept, start, product)
             mid[k, :, aligned(start, TILE)] = value
             store_halves(mid_split.at[k], slice(None), aligned(start + pad, TILE), value)
-        return 0
-
-    lax.fori_loop(0, ranges.n_first, sweep, 0)
-
-    def last(t, _):
+
+    pipelined(ranges.n_first, multiply_1, use_1)
+
+    def multiply_2(t, product):
+        start = ranges.second + t * TILE
+        in_plane(mid_split, inner, start, w_ref[t + ranges.n_first], product)
+
+    def use_2(t, product):
         start = ranges.second + t * TILE
         here = aligned(start, TILE)
-        in_plane(mid_split, inner, start, w_ref[t + ranges.n_first])
         values = []
         for k in range(kinds):
-            value = off(mid, k, inner, start)
+            value = off(mid, k, inner, start, product)
             source = rho[k, HALO * n_rows : (HALO + inner) * n_rows, here]
             value = value + (DIAGONAL * DIAGONAL) * source
             values.append(value.reshape(inner, n_rows, TILE))
         finish(here, aligned(t * TILE, TILE), values)
-        return 0
-
-    lax.fori_loop(0, ranges.n_second, last, 0)
+
+    pipelined(ranges.n_second, multiply_2, use_2)
 
 
 def clear(ranges, work):
@@ -488,6 +498,7 @@
         pltpu.VMEM((2, full, ranges.full_length), jnp.float32),
         pltpu.VMEM((2, 2, swept, ranges.split_length), jnp.bfloat16),
         pltpu.VMEM((2, swept, ranges.full_length), jnp.float32),
+        pltpu.VMEM((4 * swept, TILE), jnp.float32),
         pltpu.VMEM((4 * swept, TILE), jnp.float32),
     ]
     result = sds(inner, rows, ranges.n_second * TILE)

time: 98.4 us -> 92.2 us (0.937)
  Pallas kernels: 45 us -> 36.5 us
  waiting for transfers between devices: 32.1 us -> 34.2 us
    pallas_call x13, Pallas kernels: 45 us -> 36.5 us  [call(): pl.pallas_call(body, out_shape=out, in_specs=specs, out_specs=[VMEM] * le...]
    ppermute x15, waiting for transfers between devices: 25.2 us -> 27.3 us  [along(): return lax.ppermute(value, 'band', pairs)]
  transfers between devices with their start and end apart: 21 -> 21, of which waited for: 6 -> 7; matrix products, arithmetic and copies ran while one was open for 0% -> 0% of each run, Pallas kernels for 40% -> 34%
where the time goes in v6:
time: 92.2 us; the launch traced here: 92.1 us
  Pallas kernels  36.5 us (40%)
  waiting for transfers between devices  34.2 us (37%)
  starting transfers between devices  19.7 us (21%)
  local copies, waits for them, and re-layouts  1.41 us (2%)
    pallas_call x13, Pallas kernels, call(): pl.pallas_call(body, out_shape=out, in_specs=specs, out_specs=[VMEM] * le...  36.5 us
    ppermute x15, waiting for transfers between devices, along(): return lax.ppermute(value, 'band', pairs)  27.3 us
    ppermute x15, starting transfers between devices, along(): return lax.ppermute(value, 'band', pairs)  16.8 us
    ppermute x1, waiting for transfers between devices, per_device(): below = lax.ppermute(planes[depth - HALO:], 'slab', up)  6.88 us
  transfers between devices with their start and end apart: 21, of which 7 were waited for; matrix products, arithmetic and copies ran while one was open for 0% of the time, Pallas kernels for 34%

profile of v6, /device:TPU:26, one launch (start us, length us, event | category | flops | bytes accessed | tf_op | source)
XLA Modules:
  0.0 92.1 jit_solution(9150524891000254090)
XLA Ops:
  0.1 1.4 %copy-done = f32[2,36,5184]{2,0,1:T(2,128)S(1)} copy-done((f32[2,36,5184]{2,0,1:T(2,128)S(1)}, f32[2,36,5184]{2,0,1:T(2,128)}, u32[]{:S(2)}) %copy-start) | copy-done | bytes 1493016
  1.5 2.5 %shard_map.18 = (f32[22,2,2048]{2,1,0:T(2,128)S(1)}, f32[22,2,2048]{2,1,0:T(2,128)S(1)}, f32[22,2,2048]{2,1,0:T(2,128)S(1)}, f32[22,2,2048]{2,1,0:T(2,128)S(1)}) custom-call(s32[2]{0:T(128)S(1)} %pad_add_fusion.chip_ref, f32[36,2,5184]{2,1,0:T(2,128)S(1)} %bitcast.4), custom_call_target="tpu_custom_call" | custom-call | bytes 2934792 | tf_op jit(solution)/shard_map/pallas_call | solution.py:35
  4.0 0.5 collective-permute-start.4
  4.5 1.6 %collective-permute-start.5 = (f32[22,2,2048]{2,1,0:T(2,128)S(1)}, f32[22,2,2048]{2,1,0:T(2,128)S(1)}, u32[]{:S(2)}, u32[]{:S(2)}) collective-permute-start(f32[22,2,2048]{2,1,0:T(2,128)S(1)} %get-tuple-element.35), channel_id=1, source_target_pairs={{0,16},{4,20},{8,24},{12,28},{16,0},{20,4},{24,8},{28,12},{1,17},{... | collective-permute-start | bytes 1081352 | tf_op jit(solution)/shard_map/ppermute | solution.py:462
  6.1 2.4 %collective-permute-start.6 = (f32[22,2,2048]{2,1,0:T(2,128)S(1)}, f32[22,2,2048]{2,1,0:T(2,128)S(1)}, u32[]{:S(2)}, u32[]{:S(2)}) collective-permute-start(f32[22,2,2048]{2,1,0:T(2,128)S(1)} %get-tuple-element.36), channel_id=1, source_target_pairs={{0,8},{4,12},{8,16},{12,20},{16,24},{20,28},{24,0},{28,4},{1,9},{5... | collective-permute-start | bytes 1081352 | tf_op jit(solution)/shard_map/ppermute | solution.py:462
  8.8 1.8 %collective-permute-start.12 = (f32[4,2,5184]{2,1,0:T(2,128)S(1)}, f32[4,2,5184]{2,1,0:T(2,128)S(1)}, u32[]{:S(2)}, u32[]{:S(2)}) collective-permute-start(f32[4,2,5184]{2,1,0:T(2,128)S(1)} %get-tuple-element.53), channel_id=1, source_target_pairs={{1,0},{2,1},{3,2},{0,3},{5,4},{6,5},{7,6},{4,7},{9,8},{10,9},{11,1... | collective-permute-start | bytes 497672 | tf_op jit(solution)/shard_map/ppermute | solution.py:471
  10.6 6.9 %collective-permute-done.refs_0_ = f32[4,2,5184]{2,1,0:T(2,128)S(1)} collective-permute-done((f32[4,2,5184]{2,1,0:T(2,128)S(1)}, f32[4,2,5184]{2,1,0:T(2,128)S(1)}, u32[]{:S(2)}, u32[]{:S(2)}) %collective-permute-start) | collective-permute-done | bytes 165920 | tf_op jit(solution)/shard_map/ppermute | solution.py:470
  17.5 1.0 %shard_map.17 = (f32[4,2,2048]{2,1,0:T(2,128)S(1)}, f32[4,2,2048]{2,1,0:T(2,128)S(1)}, f32[4,2,2048]{2,1,0:T(2,128)S(1)}, f32[4,2,2048]{2,1,0:T(2,128)S(1)}) custom-call(s32[2]{0:T(128)S(1)} %pad_add_fusion.chip_ref, f32[4,2,5184]{2,1,0:T(2,128)S(1)} %collective-permute-done.refs_0_), custom_call_target="tpu_custom_call" | custom-call | bytes 428040 | tf_op jit(solution)/shard_map/pallas_call | solution.py:35
  18.5 0.7 collective-permute-start.2
  19.2 5.1 %collective-permute-done.1.refs_1_ = f32[4,2,2048]{2,1,0:T(2,128)S(1)} collective-permute-done((f32[4,2,2048]{2,1,0:T(2,128)S(1)}, f32[4,2,2048]{2,1,0:T(2,128)S(1)}, u32[]{:S(2)}, u32[]{:S(2)}) %collective-permute-start.1) | collective-permute-done | bytes 65568 | tf_op jit(solution)/shard_map/ppermute | solution.py:462
  24.9 5.0 %shard_map.20.w_ref.refs_0_ = bf16[13,768,256]{2,1,0:T(8,128)(2,1)S(1)} custom-call(s32[2]{0:T(128)S(1)} %pad_add_fusion.chip_ref), custom_call_target="tpu_custom_call" | custom-call | bytes 10223624 | tf_op jit(solution)/shard_map/pallas_call | solution.py:35
  29.9 2.2 %shard_map.24 = (f32[18,2,2048]{2,1,0:T(2,128)S(1)}, f32[18,2,2048]{2,1,0:T(2,128)S(1)}, f32[18,2,2048]{2,1,0:T(2,128)S(1)}, f32[18,2,2048]{2,1,0:T(2,128)S(1)}) custom-call(s32[2]{0:T(128)S(1)} %pad_add_fusion.chip_ref, f32[36,2,5184]{2,1,0:T(2,128)S(1)} %bitcast.6, f32[4,2,5184]{2,1,0:T(2,128)S(1)} %collective-permute-done.12.refs_1_), custom_call_target="tpu_custom_call" | custom-call | bytes 2838536 | tf_op jit(solution)/shard_map/pallas_call | solution.py:35
  32.7 1.6 %collective-permute-start.13 = (f32[18,2,2048]{2,1,0:T(2,128)S(1)}, f32[18,2,2048]{2,1,0:T(2,128)S(1)}, u32[]{:S(2)}, u32[]{:S(2)}) collective-permute-start(f32[18,2,2048]{2,1,0:T(2,128)S(1)} %get-tuple-element.44), channel_id=1, source_target_pairs={{0,24},{4,28},{8,0},{12,4},{16,8},{20,12},{24,16},{28,20},{1,25},{... | collective-permute-start | bytes 884744 | tf_op jit(solution)/shard_map/ppermute | solution.py:462
  34.3 1.5 %collective-permute-start.14 = (f32[18,2,2048]{2,1,0:T(2,128)S(1)}, f32[18,2,2048]{2,1,0:T(2,128)S(1)}, u32[]{:S(2)}, u32[]{:S(2)}) collective-permute-start(f32[18,2,2048]{2,1,0:T(2,128)S(1)} %get-tuple-element.45), channel_id=1, source_target_pairs={{0,16},{4,20},{8,24},{12,28},{16,0},{20,4},{24,8},{28,12},{1,17},{... | collective-permute-start | bytes 884744 | tf_op jit(solution)/shard_map/ppermute | solution.py:462
  35.8 0.9 collective-permute-start.15
  36.7 4.9 %shard_map.21.refs_0_.refs_1_ = f32[18,8,1536]{2,1,0:T(8,128)S(1)} custom-call(f32[26,8,2048]{2,1,0:T(8,128)S(1)} %shard_map.19.planes.refs_2_, bf16[13,768,256]{2,1,0:T(8,128)(2,1)S(1)} %shard_map.20.w_ref.refs_0_), custom_call_target="tpu_custom_call" | custom-call | flops 4253024256 | bytes 12812288 | tf_op jit(solution)/shard_map/pallas_call | solution.py:35
  41.7 1.9 %collective-permute-done.13.refs_4_ = f32[18,2,2048]{2,1,0:T(2,128)S(1)} collective-permute-done((f32[18,2,2048]{2,1,0:T(2,128)S(1)}, f32[18,2,2048]{2,1,0:T(2,128)S(1)}, u32[]{:S(2)}, u32[]{:S(2)}) %collective-permute-start.13) | collective-permute-done | bytes 294944 | tf_op jit(solution)/shard_map/ppermute | solution.py:462
  43.6 5.8 %collective-permute-done.14.refs_5_ = f32[18,2,2048]{2,1,0:T(2,128)S(1)} collective-permute-done((f32[18,2,2048]{2,1,0:T(2,128)S(1)}, f32[18,2,2048]{2,1,0:T(2,128)S(1)}, u32[]{:S(2)}, u32[]{:S(2)}) %collective-permute-start.14) | collective-permute-done | bytes 294944 | tf_op jit(solution)/shard_map/ppermute | solution.py:462
  49.9 5.7 %shard_map.22 = (f32[18,8,1536]{2,1,0:T(8,128)S(1)}, f32[18,8,1536]{2,1,0:T(8,128)S(1)}) custom-call(s32[2]{0:T(128)S(1)} %pad_add_fusion.chip_ref, f32[26,8,2048]{2,1,0:T(8,128)S(1)} %shard_map.19.planes.refs_2_, bf16[13,768,256]{2,1,0:T(8,128)(2,1)S(1)} %shard_map.20.w_ref.refs_0_, f32[26,8,2048]{2,1,0:T(8,128)S(1)} %collective-permute-done.7.other, ...), custom_call_target="tpu_custom_call" | custom-call | flops 4253024256 | bytes 16285704 | tf_op jit(solution)/shard_map/pallas_call | solution.py:35
  55.6 0.5 collective-permute-start.8
  56.1 5.7 %shard_map.26 = (f32[18,8,1536]{2,1,0:T(8,128)S(1)}, f32[18,8,1536]{2,1,0:T(8,128)S(1)}) custom-call(s32[2]{0:T(128)S(1)} %pad_add_fusion.chip_ref, f32[26,8,2048]{2,1,0:T(8,128)S(1)} %shard_map.25.planes, bf16[13,768,256]{2,1,0:T(8,128)(2,1)S(1)} %shard_map.20.w_ref.refs_0_, f32[26,8,2048]{2,1,0:T(8,128)S(1)} %collective-permute-done.16.other), custom_call_target="tpu_custom_call" | custom-call | flops 4253024256 | bytes 15400968 | tf_op jit(solution)/shard_map/pallas_call | solution.py:35
  61.9 0.7 shard_map.23
  62.6 2.0 %collective-permute-start.9 = (f32[18,2,1408]{2,1,0:T(2,128)S(1)}, f32[18,2,1408]{2,1,0:T(2,128)S(1)}, u32[]{:S(2)}, u32[]{:S(2)}) collective-permute-start(f32[18,2,1408]{2,1,0:T(2,128)S(1)} %get-tuple-element.40), channel_id=1, source_target_pairs={{0,8},{4,12},{8,16},{12,20},{16,24},{20,28},{24,0},{28,4},{1,9},{5... | collective-permute-start | bytes 608264 | tf_op jit(solution)/shard_map/ppermute | solution.py:462
  64.7 5.0 %shard_map.27.mine = f32[18,8,1536]{2,1,0:T(8,128)S(1)} custom-call(f32[26,8,2048]{2,1,0:T(8,128)S(1)} %shard_map.25.planes, bf16[13,768,256]{2,1,0:T(8,128)(2,1)S(1)} %shard_map.20.w_ref.refs_0_, f32[18,8,1536]{2,1,0:T(8,128)S(1)} %get-tuple-element.47.refs_0_), custom_call_target="tpu_custom_call" | custom-call | flops 4253024256 | bytes 13697024 | tf_op jit(solution)/shard_map/pallas_call | solution.py:35
  69.6 1.4 %collective-permute-start.10 = (f32[18,2,1408]{2,1,0:T(2,128)S(1)}, f32[18,2,1408]{2,1,0:T(2,128)S(1)}, u32[]{:S(2)}, u32[]{:S(2)}) collective-permute-start(f32[18,2,1408]{2,1,0:T(2,128)S(1)} %get-tuple-element.41), channel_id=1, source_target_pairs={{0,16},{4,20},{8,24},{12,28},{16,0},{20,4},{24,8},{28,12},{1,17},{... | collective-permute-start | bytes 608264 | tf_op jit(solution)/shard_map/ppermute | solution.py:462
  71.0 0.7 shard_map.28
  71.8 3.0 %collective-permute-start.18 = (f32[18,2,1408]{2,1,0:T(2,128)S(1)}, f32[18,2,1408]{2,1,0:T(2,128)S(1)}, u32[]{:S(2)}, u32[]{:S(2)}) collective-permute-start(f32[18,2,1408]{2,1,0:T(2,128)S(1)} %get-tuple-element.50), channel_id=1, source_target_pairs={{0,8},{4,12},{8,16},{12,20},{16,24},{20,28},{24,0},{28,4},{1,9},{5... | collective-permute-start | bytes 608264 | tf_op jit(solution)/shard_map/ppermute | solution.py:462
  74.7 0.7 collective-permute-start.19
  75.4 6.5 %collective-permute-done.10.refs_2_ = f32[18,2,1408]{2,1,0:T(2,128)S(1)} collective-permute-done((f32[18,2,1408]{2,1,0:T(2,128)S(1)}, f32[18,2,1408]{2,1,0:T(2,128)S(1)}, u32[]{:S(2)}, u32[]{:S(2)}) %collective-permute-start.10) | collective-permute-done | bytes 202784 | tf_op jit(solution)/shard_map/ppermute | solution.py:462
  82.0 1.5 %collective-permute-done.18.refs_5_ = f32[18,2,1408]{2,1,0:T(2,128)S(1)} collective-permute-done((f32[18,2,1408]{2,1,0:T(2,128)S(1)}, f32[18,2,1408]{2,1,0:T(2,128)S(1)}, u32[]{:S(2)}, u32[]{:S(2)}) %collective-permute-start.18) | collective-permute-done | bytes 202784 | tf_op jit(solution)/shard_map/ppermute | solution.py:462
  83.4 6.5 %collective-permute-done.19.refs_6_ = f32[18,2,1408]{2,1,0:T(2,128)S(1)} collective-permute-done((f32[18,2,1408]{2,1,0:T(2,128)S(1)}, f32[18,2,1408]{2,1,0:T(2,128)S(1)}, u32[]{:S(2)}, u32[]{:S(2)}) %collective-permute-start.19) | collective-permute-done | bytes 202784 | tf_op jit(solution)/shard_map/ppermute | solution.py:462
  89.9 2.2 %shard_map.29 = f32[36,2,5184]{2,1,0:T(2,128)} custom-call(s32[2]{0:T(128)S(1)} %pad_add_fusion.chip_ref, f32[18,2,1408]{2,1,0:T(2,128)S(1)} %get-tuple-element.39.refs_0_, f32[18,2,1408]{2,1,0:T(2,128)S(1)} %collective-permute-done.9.refs_1_, f32[18,2,1408]{2,1,0:T(2,128)S(1)} %collective-permute-done.10.refs_2_, ...), custom_call_target="tpu_custom_call" | custom-call | bytes 3115016 | tf_op jit(solution)/shard_map/pallas_call | solution.py:35
  (29 shorter events, 2.2 us)
Async XLA Ops:
  0.1 1.4 %copy-start = (f32[2,36,5184]{2,0,1:T(2,128)S(1)}, f32[2,36,5184]{2,0,1:T(2,128)}, u32[]{:S(2)}) copy-start(f32[2,36,5184]{2,0,1:T(2,128)} %param.1) | copy-start | bytes 4478980
  1.5 7.0 %copy-start.1 = (f32[2,36,5184]{2,0,1:T(2,128)S(1)}, f32[2,36,5184]{2,0,1:T(2,128)}, u32[]{:S(2)}) copy-start(f32[2,36,5184]{2,0,1:T(2,128)} %param.1) | copy-start | bytes 4478980
  4.0 28.1 %collective-permute-start.4 = (f32[22,2,2048]{2,1,0:T(2,128)S(1)}, f32[22,2,2048]{2,1,0:T(2,128)S(1)}, u32[]{:S(2)}, u32[]{:S(2)}) collective-permute-start(f32[22,2,2048]{2,1,0:T(2,128)S(1)} %get-tuple-element.34), channel_id=1, source_target_pairs={{0,24},{4,28},{8,0},{12,4},{16,8},{20,12},{24,16},{28,20},{1,25},{... | collective-permute-start | bytes 1081352 | tf_op jit(solution)/shard_map/ppermute | solution.py:462
  4.5 27.6 %collective-permute-start.5 = (f32[22,2,2048]{2,1,0:T(2,128)S(1)}, f32[22,2,2048]{2,1,0:T(2,128)S(1)}, u32[]{:S(2)}, u32[]{:S(2)}) collective-permute-start(f32[22,2,2048]{2,1,0:T(2,128)S(1)} %get-tuple-element.35), channel_id=1, source_target_pairs={{0,16},{4,20},{8,24},{12,28},{16,0},{20,4},{24,8},{28,12},{1,17},{... | collective-permute-start | bytes 1081352 | tf_op jit(solution)/shard_map/ppermute | solution.py:462
  6.1 26.0 %collective-permute-start.6 = (f32[22,2,2048]{2,1,0:T(2,128)S(1)}, f32[22,2,2048]{2,1,0:T(2,128)S(1)}, u32[]{:S(2)}, u32[]{:S(2)}) collective-permute-start(f32[22,2,2048]{2,1,0:T(2,128)S(1)} %get-tuple-element.36), channel_id=1, source_target_pairs={{0,8},{4,12},{8,16},{12,20},{16,24},{20,28},{24,0},{28,4},{1,9},{5... | collective-permute-start | bytes 1081352 | tf_op jit(solution)/shard_map/ppermute | solution.py:462
  8.5 9.0 %collective-permute-start = (f32[4,2,5184]{2,1,0:T(2,128)S(1)}, f32[4,2,5184]{2,1,0:T(2,128)S(1)}, u32[]{:S(2)}, u32[]{:S(2)}) collective-permute-start(f32[4,2,5184]{2,1,0:T(2,128)S(1)} %get-tuple-element.54), channel_id=1, source_target_pairs={{0,1},{1,2},{2,3},{3,0},{4,5},{5,6},{6,7},{7,4},{8,9},{9,10},{10,1... | collective-permute-start | bytes 497672 | tf_op jit(solution)/shard_map/ppermute | solution.py:470
  8.8 9.7 %collective-permute-start.12 = (f32[4,2,5184]{2,1,0:T(2,128)S(1)}, f32[4,2,5184]{2,1,0:T(2,128)S(1)}, u32[]{:S(2)}, u32[]{:S(2)}) collective-permute-start(f32[4,2,5184]{2,1,0:T(2,128)S(1)} %get-tuple-element.53), channel_id=1, source_target_pairs={{1,0},{2,1},{3,2},{0,3},{5,4},{6,5},{7,6},{4,7},{9,8},{10,9},{11,1... | collective-permute-start | bytes 497672 | tf_op jit(solution)/shard_map/ppermute | solution.py:471
  18.4 5.9 %collective-permute-start.1 = (f32[4,2,2048]{2,1,0:T(2,128)S(1)}, f32[4,2,2048]{2,1,0:T(2,128)S(1)}, u32[]{:S(2)}, u32[]{:S(2)}) collective-permute-start(f32[4,2,2048]{2,1,0:T(2,128)S(1)} %get-tuple-element.30), channel_id=1, source_target_pairs={{0,24},{4,28},{8,0},{12,4},{16,8},{20,12},{24,16},{28,20},{1,25},{... | collective-permute-start | bytes 196616 | tf_op jit(solution)/shard_map/ppermute | solution.py:462
  18.5 13.6 %collective-permute-start.2 = (f32[4,2,2048]{2,1,0:T(2,128)S(1)}, f32[4,2,2048]{2,1,0:T(2,128)S(1)}, u32[]{:S(2)}, u32[]{:S(2)}) collective-permute-start(f32[4,2,2048]{2,1,0:T(2,128)S(1)} %get-tuple-element.31), channel_id=1, source_target_pairs={{0,16},{4,20},{8,24},{12,28},{16,0},{20,4},{24,8},{28,12},{1,17},{... | collective-permute-start | bytes 196616 | tf_op jit(solution)/shard_map/ppermute | solution.py:462
  24.4 7.7 %collective-permute-start.3 = (f32[4,2,2048]{2,1,0:T(2,128)S(1)}, f32[4,2,2048]{2,1,0:T(2,128)S(1)}, u32[]{:S(2)}, u32[]{:S(2)}) collective-permute-start(f32[4,2,2048]{2,1,0:T(2,128)S(1)} %get-tuple-element.32), channel_id=1, source_target_pairs={{0,8},{4,12},{8,16},{12,20},{16,24},{20,28},{24,0},{28,4},{1,9},{5... | collective-permute-start | bytes 196616 | tf_op jit(solution)/shard_map/ppermute | solution.py:462
  32.7 17.2 %collective-permute-start.7 = (f32[26,8,2048]{2,1,0:T(8,128)S(1)}, f32[26,8,2048]{2,1,0:T(8,128)S(1)}, u32[]{:S(2)}, u32[]{:S(2)}) collective-permute-start(f32[26,8,2048]{2,1,0:T(8,128)S(1)} %shard_map.19.planes.refs_2_), channel_id=1, source_target_pairs={{0,4},{4,0},{8,12},{12,8},{16,20},{20,16},{24,28},{28,24},{1,5},{5... | collective-permute-start | bytes 5111816 | tf_op jit(solution)/shard_map/ppermute | solution.py:465
  32.7 10.9 %collective-permute-start.13 = (f32[18,2,2048]{2,1,0:T(2,128)S(1)}, f32[18,2,2048]{2,1,0:T(2,128)S(1)}, u32[]{:S(2)}, u32[]{:S(2)}) collective-permute-start(f32[18,2,2048]{2,1,0:T(2,128)S(1)} %get-tuple-element.44), channel_id=1, source_target_pairs={{0,24},{4,28},{8,0},{12,4},{16,8},{20,12},{24,16},{28,20},{1,25},{... | collective-permute-start | bytes 884744 | tf_op jit(solution)/shard_map/ppermute | solution.py:462
  34.3 15.1 %collective-permute-start.14 = (f32[18,2,2048]{2,1,0:T(2,128)S(1)}, f32[18,2,2048]{2,1,0:T(2,128)S(1)}, u32[]{:S(2)}, u32[]{:S(2)}) collective-permute-start(f32[18,2,2048]{2,1,0:T(2,128)S(1)} %get-tuple-element.45), channel_id=1, source_target_pairs={{0,16},{4,20},{8,24},{12,28},{16,0},{20,4},{24,8},{28,12},{1,17},{... | collective-permute-start | bytes 884744 | tf_op jit(solution)/shard_map/ppermute | solution.py:462
  35.8 13.5 %collective-permute-start.15 = (f32[18,2,2048]{2,1,0:T(2,128)S(1)}, f32[18,2,2048]{2,1,0:T(2,128)S(1)}, u32[]{:S(2)}, u32[]{:S(2)}) collective-permute-start(f32[18,2,2048]{2,1,0:T(2,128)S(1)} %get-tuple-element.46), channel_id=1, source_target_pairs={{0,8},{4,12},{8,16},{12,20},{16,24},{20,28},{24,0},{28,4},{1,9},{5... | collective-permute-start | bytes 884744 | tf_op jit(solution)/shard_map/ppermute | solution.py:462
  49.8 6.4 %collective-permute-start.16 = (f32[26,8,2048]{2,1,0:T(8,128)S(1)}, f32[26,8,2048]{2,1,0:T(8,128)S(1)}, u32[]{:S(2)}, u32[]{:S(2)}) collective-permute-start(f32[26,8,2048]{2,1,0:T(8,128)S(1)} %shard_map.25.planes), channel_id=1, source_target_pairs={{0,4},{4,0},{8,12},{12,8},{16,20},{20,16},{24,28},{28,24},{1,5},{5... | collective-permute-start | bytes 5111816 | tf_op jit(solution)/shard_map/ppermute | solution.py:465
  55.6 6.3 %collective-permute-start.8 = (f32[18,8,1536]{2,1,0:T(8,128)S(1)}, f32[18,8,1536]{2,1,0:T(8,128)S(1)}, u32[]{:S(2)}, u32[]{:S(2)}) collective-permute-start(f32[18,8,1536]{2,1,0:T(8,128)S(1)} %get-tuple-element.38), channel_id=1, source_target_pairs={{0,4},{4,0},{8,12},{12,8},{16,20},{20,16},{24,28},{28,24},{1,5},{5... | collective-permute-start | bytes 2654216 | tf_op jit(solution)/shard_map/ppermute | solution.py:465
  61.8 9.2 %collective-permute-start.17 = (f32[18,8,1536]{2,1,0:T(8,128)S(1)}, f32[18,8,1536]{2,1,0:T(8,128)S(1)}, u32[]{:S(2)}, u32[]{:S(2)}) collective-permute-start(f32[18,8,1536]{2,1,0:T(8,128)S(1)} %get-tuple-element.48), channel_id=1, source_target_pairs={{0,4},{4,0},{8,12},{12,8},{16,20},{20,16},{24,28},{28,24},{1,5},{5... | collective-permute-start | bytes 2654216 | tf_op jit(solution)/shard_map/ppermute | solution.py:465
  62.6 12.8 %collective-permute-start.9 = (f32[18,2,1408]{2,1,0:T(2,128)S(1)}, f32[18,2,1408]{2,1,0:T(2,128)S(1)}, u32[]{:S(2)}, u32[]{:S(2)}) collective-permute-start(f32[18,2,1408]{2,1,0:T(2,128)S(1)} %get-tuple-element.40), channel_id=1, source_target_pairs={{0,8},{4,12},{8,16},{12,20},{16,24},{20,28},{24,0},{28,4},{1,9},{5... | collective-permute-start | bytes 608264 | tf_op jit(solution)/shard_map/ppermute | solution.py:462
  69.6 12.3 %collective-permute-start.10 = (f32[18,2,1408]{2,1,0:T(2,128)S(1)}, f32[18,2,1408]{2,1,0:T(2,128)S(1)}, u32[]{:S(2)}, u32[]{:S(2)}) collective-permute-start(f32[18,2,1408]{2,1,0:T(2,128)S(1)} %get-tuple-element.41), channel_id=1, source_target_pairs={{0,16},{4,20},{8,24},{12,28},{16,0},{20,4},{24,8},{28,12},{1,17},{... | collective-permute-start | bytes 608264 | tf_op jit(solution)/shard_map/ppermute | solution.py:462
  71.0 11.0 %collective-permute-start.11 = (f32[18,2,1408]{2,1,0:T(2,128)S(1)}, f32[18,2,1408]{2,1,0:T(2,128)S(1)}, u32[]{:S(2)}, u32[]{:S(2)}) collective-permute-start(f32[18,2,1408]{2,1,0:T(2,128)S(1)} %get-tuple-element.42), channel_id=1, source_target_pairs={{0,24},{4,28},{8,0},{12,4},{16,8},{20,12},{24,16},{28,20},{1,25},{... | collective-permute-start | bytes 608264 | tf_op jit(solution)/shard_map/ppermute | solution.py:462
  71.8 11.7 %collective-permute-start.18 = (f32[18,2,1408]{2,1,0:T(2,128)S(1)}, f32[18,2,1408]{2,1,0:T(2,128)S(1)}, u32[]{:S(2)}, u32[]{:S(2)}) collective-permute-start(f32[18,2,1408]{2,1,0:T(2,128)S(1)} %get-tuple-element.50), channel_id=1, source_target_pairs={{0,8},{4,12},{8,16},{12,20},{16,24},{20,28},{24,0},{28,4},{1,9},{5... | collective-permute-start | bytes 608264 | tf_op jit(solution)/shard_map/ppermute | solution.py:462
  74.7 15.2 %collective-permute-start.19 = (f32[18,2,1408]{2,1,0:T(2,128)S(1)}, f32[18,2,1408]{2,1,0:T(2,128)S(1)}, u32[]{:S(2)}, u32[]{:S(2)}) collective-permute-start(f32[18,2,1408]{2,1,0:T(2,128)S(1)} %get-tuple-element.51), channel_id=1, source_target_pairs={{0,16},{4,20},{8,24},{12,28},{16,0},{20,4},{24,8},{28,12},{1,17},{... | collective-permute-start | bytes 608264 | tf_op jit(solution)/shard_map/ppermute | solution.py:462
  75.4 14.4 %collective-permute-start.20 = (f32[18,2,1408]{2,1,0:T(2,128)S(1)}, f32[18,2,1408]{2,1,0:T(2,128)S(1)}, u32[]{:S(2)}, u32[]{:S(2)}) collective-permute-start(f32[18,2,1408]{2,1,0:T(2,128)S(1)} %get-tuple-element.52), channel_id=1, source_target_pairs={{0,24},{4,28},{8,0},{12,4},{16,8},{20,12},{24,16},{28,20},{1,25},{... | collective-permute-start | bytes 608264 | tf_op jit(solution)/shard_map/ppermute | solution.py:462

commit v7 on v6

--- a/solution.py
+++ b/solution.py
@@ -144,8 +144,8 @@
     )
 
 
-def gather_body(groups, kept, unread, *refs):
-    refs, out = refs[unread:], refs[-1]
+def gather_body(groups, kept, *refs):
+    out = refs[-1]
     row = 0
     if kept:
         before = refs[0]
@@ -167,13 +167,13 @@
         row += ins[0].shape[0]
 
 
-def gather(groups, before=None, kept=0, alive=()):
+def gather(groups, before=None, kept=0):
     depth = kept + sum(g[0].shape[0] for g in groups)
     _, orbs, span = groups[0][0].shape
     return call(
-        functools.partial(gather_body, len(groups), kept, len(alive)),
+        functools.partial(gather_body, len(groups), kept),
         [sds(depth, orbs * len(groups[0]), span)],
-        [*alive, *([before] if kept else []), *(p for g in groups for p in g)],
+        [*([before] if kept else []), *(p for g in groups for p in g)],
     )[0]
 
 
@@ -537,11 +537,11 @@
 
     other_a = partner_core(planes_a)
     acc_a = same(planes_a)
-    planes_b = gather([got_b], before=planes_a, kept=2 * HALO, alive=(banded, acc_a))
+    acc_a, back_a = cross(planes_a, other_a, acc_a)
+    planes_b = gather([got_b], before=planes_a, kept=2 * HALO)
     other_b = partner_core(planes_b)
-    acc_a, back_a = cross(planes_a, other_a, acc_a)
+    home = give(acc_a, back_a)
     acc_b, back_b = cross(planes_b, other_b)
-    home = give(acc_a, back_a)
     acc_b = same(planes_b, acc_b)
     home += give(acc_b, back_b)
     out = call(

time: 92.2 us -> 101 us (1.095)
  the two profiles are of different devices: /device:TPU:26 before, /device:TPU:0 now
where the time goes in v7:
time: 101 us; the launch traced here: 99 us
  Pallas kernels  36.5 us (36%)
  waiting for transfers between devices  31.5 us (31%)
  starting transfers between devices  29.4 us (29%)
  local copies, waits for them, and re-layouts  1.41 us (1%)
    pallas_call x13, Pallas kernels, call(): pl.pallas_call(body, out_shape=out, in_specs=specs, out_specs=[VMEM] * le...  36.5 us
    ppermute x15, waiting for transfers between devices, along(): return lax.ppermute(value, 'band', pairs)  23.6 us
    ppermute x15, starting transfers between devices, along(): return lax.ppermute(value, 'band', pairs)  23.3 us
    ppermute x1, waiting for transfers between devices, per_device(): below = lax.ppermute(planes[depth - HALO:], 'slab', up)  5.58 us
    ppermute x1, starting transfers between devices, per_device(): above = lax.ppermute(planes[:HALO], 'slab', down)  3.6 us
    ppermute x1, waiting for transfers between devices, per_device(): above = lax.ppermute(planes[:HALO], 'slab', down)  2.24 us
  transfers between devices with their start and end apart: 21, of which 10 were waited for; matrix products, arithmetic and copies ran while one was open for 0% of the time, Pallas kernels for 32%

profile of v7, /device:TPU:0, one launch (start us, length us, event | category | flops | bytes accessed | tf_op | source)
XLA Modules:
  0.0 99.0 jit_solution(4298803801746975715)
XLA Ops:
  0.1 1.4 %copy-done = f32[2,36,5184]{2,0,1:T(2,128)S(1)} copy-done((f32[2,36,5184]{2,0,1:T(2,128)S(1)}, f32[2,36,5184]{2,0,1:T(2,128)}, u32[]{:S(2)}) %copy-start) | copy-done | bytes 1493016
  1.5 2.5 %shard_map.18 = (f32[22,2,2048]{2,1,0:T(2,128)S(1)}, f32[22,2,2048]{2,1,0:T(2,128)S(1)}, f32[22,2,2048]{2,1,0:T(2,128)S(1)}, f32[22,2,2048]{2,1,0:T(2,128)S(1)}) custom-call(s32[2]{0:T(128)S(1)} %pad_add_fusion.chip_ref, f32[36,2,5184]{2,1,0:T(2,128)S(1)} %bitcast.4), custom_call_target="tpu_custom_call" | custom-call | bytes 2934792 | tf_op jit(solution)/shard_map/pallas_call | solution.py:35
  4.0 4.0 %collective-permute-start.4 = (f32[22,2,2048]{2,1,0:T(2,128)S(1)}, f32[22,2,2048]{2,1,0:T(2,128)S(1)}, u32[]{:S(2)}, u32[]{:S(2)}) collective-permute-start(f32[22,2,2048]{2,1,0:T(2,128)S(1)} %get-tuple-element.34), channel_id=1, source_target_pairs={{0,24},{4,28},{8,0},{12,4},{16,8},{20,12},{24,16},{28,20},{1,25},{... | collective-permute-start | bytes 1081352 | tf_op jit(solution)/shard_map/ppermute | solution.py:462
  9.1 1.6 %collective-permute-start = (f32[4,2,5184]{2,1,0:T(2,128)S(1)}, f32[4,2,5184]{2,1,0:T(2,128)S(1)}, u32[]{:S(2)}, u32[]{:S(2)}) collective-permute-start(f32[4,2,5184]{2,1,0:T(2,128)S(1)} %get-tuple-element.54), channel_id=1, source_target_pairs={{0,1},{1,2},{2,3},{3,0},{4,5},{5,6},{6,7},{7,4},{8,9},{9,10},{10,1... | collective-permute-start | bytes 497672 | tf_op jit(solution)/shard_map/ppermute | solution.py:470
  10.7 5.6 %collective-permute-done.refs_0_ = f32[4,2,5184]{2,1,0:T(2,128)S(1)} collective-permute-done((f32[4,2,5184]{2,1,0:T(2,128)S(1)}, f32[4,2,5184]{2,1,0:T(2,128)S(1)}, u32[]{:S(2)}, u32[]{:S(2)}) %collective-permute-start) | collective-permute-done | bytes 165920 | tf_op jit(solution)/shard_map/ppermute | solution.py:470
  16.3 0.9 shard_map.17
  17.3 2.4 %collective-permute-start.1 = (f32[4,2,2048]{2,1,0:T(2,128)S(1)}, f32[4,2,2048]{2,1,0:T(2,128)S(1)}, u32[]{:S(2)}, u32[]{:S(2)}) collective-permute-start(f32[4,2,2048]{2,1,0:T(2,128)S(1)} %get-tuple-element.30), channel_id=1, source_target_pairs={{0,24},{4,28},{8,0},{12,4},{16,8},{20,12},{24,16},{28,20},{1,25},{... | collective-permute-start | bytes 196616 | tf_op jit(solution)/shard_map/ppermute | solution.py:462
  19.6 1.5 %collective-permute-start.2 = (f32[4,2,2048]{2,1,0:T(2,128)S(1)}, f32[4,2,2048]{2,1,0:T(2,128)S(1)}, u32[]{:S(2)}, u32[]{:S(2)}) collective-permute-start(f32[4,2,2048]{2,1,0:T(2,128)S(1)} %get-tuple-element.31), channel_id=1, source_target_pairs={{0,16},{4,20},{8,24},{12,28},{16,0},{20,4},{24,8},{28,12},{1,17},{... | collective-permute-start | bytes 196616 | tf_op jit(solution)/shard_map/ppermute | solution.py:462
  21.1 3.7 %collective-permute-done.1.refs_1_ = f32[4,2,2048]{2,1,0:T(2,128)S(1)} collective-permute-done((f32[4,2,2048]{2,1,0:T(2,128)S(1)}, f32[4,2,2048]{2,1,0:T(2,128)S(1)}, u32[]{:S(2)}, u32[]{:S(2)}) %collective-permute-start.1) | collective-permute-done | bytes 65568 | tf_op jit(solution)/shard_map/ppermute | solution.py:462
  24.8 2.5 %collective-permute-start.3 = (f32[4,2,2048]{2,1,0:T(2,128)S(1)}, f32[4,2,2048]{2,1,0:T(2,128)S(1)}, u32[]{:S(2)}, u32[]{:S(2)}) collective-permute-start(f32[4,2,2048]{2,1,0:T(2,128)S(1)} %get-tuple-element.32), channel_id=1, source_target_pairs={{0,8},{4,12},{8,16},{12,20},{16,24},{20,28},{24,0},{28,4},{1,9},{5... | collective-permute-start | bytes 196616 | tf_op jit(solution)/shard_map/ppermute | solution.py:462
  27.3 3.6 %collective-permute-start.12 = (f32[4,2,5184]{2,1,0:T(2,128)S(1)}, f32[4,2,5184]{2,1,0:T(2,128)S(1)}, u32[]{:S(2)}, u32[]{:S(2)}) collective-permute-start(f32[4,2,5184]{2,1,0:T(2,128)S(1)} %get-tuple-element.53), channel_id=1, source_target_pairs={{1,0},{2,1},{3,2},{0,3},{5,4},{6,5},{7,6},{4,7},{9,8},{10,9},{11,1... | collective-permute-start | bytes 497672 | tf_op jit(solution)/shard_map/ppermute | solution.py:471
  31.6 2.2 %collective-permute-done.12.refs_1_ = f32[4,2,5184]{2,1,0:T(2,128)S(1)} collective-permute-done((f32[4,2,5184]{2,1,0:T(2,128)S(1)}, f32[4,2,5184]{2,1,0:T(2,128)S(1)}, u32[]{:S(2)}, u32[]{:S(2)}) %collective-permute-start.12) | collective-permute-done | bytes 165920 | tf_op jit(solution)/shard_map/ppermute | solution.py:471
  33.8 2.2 %shard_map.24 = (f32[18,2,2048]{2,1,0:T(2,128)S(1)}, f32[18,2,2048]{2,1,0:T(2,128)S(1)}, f32[18,2,2048]{2,1,0:T(2,128)S(1)}, f32[18,2,2048]{2,1,0:T(2,128)S(1)}) custom-call(s32[2]{0:T(128)S(1)} %pad_add_fusion.chip_ref, f32[36,2,5184]{2,1,0:T(2,128)S(1)} %bitcast.6, f32[4,2,5184]{2,1,0:T(2,128)S(1)} %collective-permute-done.12.refs_1_), custom_call_target="tpu_custom_call" | custom-call | bytes 2838536 | tf_op jit(solution)/shard_map/pallas_call | solution.py:35
  36.0 1.6 %collective-permute-start.13 = (f32[18,2,2048]{2,1,0:T(2,128)S(1)}, f32[18,2,2048]{2,1,0:T(2,128)S(1)}, u32[]{:S(2)}, u32[]{:S(2)}) collective-permute-start(f32[18,2,2048]{2,1,0:T(2,128)S(1)} %get-tuple-element.44), channel_id=1, source_target_pairs={{0,24},{4,28},{8,0},{12,4},{16,8},{20,12},{24,16},{28,20},{1,25},{... | collective-permute-start | bytes 884744 | tf_op jit(solution)/shard_map/ppermute | solution.py:462
  38.1 1.5 %collective-permute-start.15 = (f32[18,2,2048]{2,1,0:T(2,128)S(1)}, f32[18,2,2048]{2,1,0:T(2,128)S(1)}, u32[]{:S(2)}, u32[]{:S(2)}) collective-permute-start(f32[18,2,2048]{2,1,0:T(2,128)S(1)} %get-tuple-element.46), channel_id=1, source_target_pairs={{0,8},{4,12},{8,16},{12,20},{16,24},{20,28},{24,0},{28,4},{1,9},{5... | collective-permute-start | bytes 884744 | tf_op jit(solution)/shard_map/ppermute | solution.py:462
  39.6 6.3 %collective-permute-done.13.refs_2_ = f32[18,2,2048]{2,1,0:T(2,128)S(1)} collective-permute-done((f32[18,2,2048]{2,1,0:T(2,128)S(1)}, f32[18,2,2048]{2,1,0:T(2,128)S(1)}, u32[]{:S(2)}, u32[]{:S(2)}) %collective-permute-start.13) | collective-permute-done | bytes 294944 | tf_op jit(solution)/shard_map/ppermute | solution.py:462
  45.9 5.0 %collective-permute-done.14.refs_3_ = f32[18,2,2048]{2,1,0:T(2,128)S(1)} collective-permute-done((f32[18,2,2048]{2,1,0:T(2,128)S(1)}, f32[18,2,2048]{2,1,0:T(2,128)S(1)}, u32[]{:S(2)}, u32[]{:S(2)}) %collective-permute-start.14) | collective-permute-done | bytes 294944 | tf_op jit(solution)/shard_map/ppermute | solution.py:462
  51.4 5.0 %shard_map.20.w_ref = bf16[13,768,256]{2,1,0:T(8,128)(2,1)S(1)} custom-call(s32[2]{0:T(128)S(1)} %pad_add_fusion.chip_ref), custom_call_target="tpu_custom_call" | custom-call | bytes 10223624 | tf_op jit(solution)/shard_map/pallas_call | solution.py:35
  56.4 4.9 %shard_map.21.refs_0_ = f32[18,8,1536]{2,1,0:T(8,128)S(1)} custom-call(f32[26,8,2048]{2,1,0:T(8,128)S(1)} %shard_map.19.planes.refs_0_, bf16[13,768,256]{2,1,0:T(8,128)(2,1)S(1)} %shard_map.20.w_ref), custom_call_target="tpu_custom_call" | custom-call | flops 4253024256 | bytes 12812288 | tf_op jit(solution)/shard_map/pallas_call | solution.py:35
  61.3 5.7 %shard_map.22 = (f32[18,8,1536]{2,1,0:T(8,128)S(1)}, f32[18,8,1536]{2,1,0:T(8,128)S(1)}) custom-call(s32[2]{0:T(128)S(1)} %pad_add_fusion.chip_ref, f32[26,8,2048]{2,1,0:T(8,128)S(1)} %shard_map.19.planes.refs_0_, bf16[13,768,256]{2,1,0:T(8,128)(2,1)S(1)} %shard_map.20.w_ref, f32[26,8,2048]{2,1,0:T(8,128)S(1)} %collective-permute-done.7.other, ...), custom_call_target="tpu_custom_call" | custom-call | flops 4253024256 | bytes 16285704 | tf_op jit(solution)/shard_map/pallas_call | solution.py:35
  67.6 5.7 %shard_map.26 = (f32[18,8,1536]{2,1,0:T(8,128)S(1)}, f32[18,8,1536]{2,1,0:T(8,128)S(1)}) custom-call(s32[2]{0:T(128)S(1)} %pad_add_fusion.chip_ref, f32[26,8,2048]{2,1,0:T(8,128)S(1)} %shard_map.25.planes, bf16[13,768,256]{2,1,0:T(8,128)(2,1)S(1)} %shard_map.20.w_ref, f32[26,8,2048]{2,1,0:T(8,128)S(1)} %collective-permute-done.16.other), custom_call_target="tpu_custom_call" | custom-call | flops 4253024256 | bytes 15400968 | tf_op jit(solution)/shard_map/pallas_call | solution.py:35
  73.4 0.7 shard_map.23
  74.7 5.0 %shard_map.27.mine = f32[18,8,1536]{2,1,0:T(8,128)S(1)} custom-call(f32[26,8,2048]{2,1,0:T(8,128)S(1)} %shard_map.25.planes, bf16[13,768,256]{2,1,0:T(8,128)(2,1)S(1)} %shard_map.20.w_ref, f32[18,8,1536]{2,1,0:T(8,128)S(1)} %get-tuple-element.47.refs_0_), custom_call_target="tpu_custom_call" | custom-call | flops 4253024256 | bytes 13697024 | tf_op jit(solution)/shard_map/pallas_call | solution.py:35
  79.7 1.5 %collective-permute-start.10 = (f32[18,2,1408]{2,1,0:T(2,128)S(1)}, f32[18,2,1408]{2,1,0:T(2,128)S(1)}, u32[]{:S(2)}, u32[]{:S(2)}) collective-permute-start(f32[18,2,1408]{2,1,0:T(2,128)S(1)} %get-tuple-element.41), channel_id=1, source_target_pairs={{0,16},{4,20},{8,24},{12,28},{16,0},{20,4},{24,8},{28,12},{1,17},{... | collective-permute-start | bytes 608264 | tf_op jit(solution)/shard_map/ppermute | solution.py:462
  81.2 1.7 %collective-permute-start.11 = (f32[18,2,1408]{2,1,0:T(2,128)S(1)}, f32[18,2,1408]{2,1,0:T(2,128)S(1)}, u32[]{:S(2)}, u32[]{:S(2)}) collective-permute-start(f32[18,2,1408]{2,1,0:T(2,128)S(1)} %get-tuple-element.42), channel_id=1, source_target_pairs={{0,24},{4,28},{8,0},{12,4},{16,8},{20,12},{24,16},{28,20},{1,25},{... | collective-permute-start | bytes 608264 | tf_op jit(solution)/shard_map/ppermute | solution.py:462
  84.0 1.3 %collective-permute-start.19 = (f32[18,2,1408]{2,1,0:T(2,128)S(1)}, f32[18,2,1408]{2,1,0:T(2,128)S(1)}, u32[]{:S(2)}, u32[]{:S(2)}) collective-permute-start(f32[18,2,1408]{2,1,0:T(2,128)S(1)} %get-tuple-element.51), channel_id=1, source_target_pairs={{0,16},{4,20},{8,24},{12,28},{16,0},{20,4},{24,8},{28,12},{1,17},{... | collective-permute-start | bytes 608264 | tf_op jit(solution)/shard_map/ppermute | solution.py:462
  85.2 2.8 %collective-permute-start.20 = (f32[18,2,1408]{2,1,0:T(2,128)S(1)}, f32[18,2,1408]{2,1,0:T(2,128)S(1)}, u32[]{:S(2)}, u32[]{:S(2)}) collective-permute-start(f32[18,2,1408]{2,1,0:T(2,128)S(1)} %get-tuple-element.52), channel_id=1, source_target_pairs={{0,24},{4,28},{8,0},{12,4},{16,8},{20,12},{24,16},{28,20},{1,25},{... | collective-permute-start | bytes 608264 | tf_op jit(solution)/shard_map/ppermute | solution.py:462
  88.3 0.8 collective-permute-done.11.refs_3_
  89.1 4.4 %collective-permute-done.18.refs_5_ = f32[18,2,1408]{2,1,0:T(2,128)S(1)} collective-permute-done((f32[18,2,1408]{2,1,0:T(2,128)S(1)}, f32[18,2,1408]{2,1,0:T(2,128)S(1)}, u32[]{:S(2)}, u32[]{:S(2)}) %collective-permute-start.18) | collective-permute-done | bytes 202784 | tf_op jit(solution)/shard_map/ppermute | solution.py:462
  93.5 2.2 %collective-permute-done.19.refs_6_ = f32[18,2,1408]{2,1,0:T(2,128)S(1)} collective-permute-done((f32[18,2,1408]{2,1,0:T(2,128)S(1)}, f32[18,2,1408]{2,1,0:T(2,128)S(1)}, u32[]{:S(2)}, u32[]{:S(2)}) %collective-permute-start.19) | collective-permute-done | bytes 202784 | tf_op jit(solution)/shard_map/ppermute | solution.py:462
  95.7 1.0 %collective-permute-done.20.refs_7_ = f32[18,2,1408]{2,1,0:T(2,128)S(1)} collective-permute-done((f32[18,2,1408]{2,1,0:T(2,128)S(1)}, f32[18,2,1408]{2,1,0:T(2,128)S(1)}, u32[]{:S(2)}, u32[]{:S(2)}) %collective-permute-start.20) | collective-permute-done | bytes 202784 | tf_op jit(solution)/shard_map/ppermute | solution.py:462
  96.8 2.2 %shard_map.29 = f32[36,2,5184]{2,1,0:T(2,128)} custom-call(s32[2]{0:T(128)S(1)} %pad_add_fusion.chip_ref, f32[18,2,1408]{2,1,0:T(2,128)S(1)} %get-tuple-element.39.refs_0_, f32[18,2,1408]{2,1,0:T(2,128)S(1)} %collective-permute-done.9.refs_1_, f32[18,2,1408]{2,1,0:T(2,128)S(1)} %collective-permute-done.10.refs_2_, ...), custom_call_target="tpu_custom_call" | custom-call | bytes 3115016 | tf_op jit(solution)/shard_map/pallas_call | solution.py:35
  (29 shorter events, 5.3 us)
Async XLA Ops:
  0.1 1.4 %copy-start = (f32[2,36,5184]{2,0,1:T(2,128)S(1)}, f32[2,36,5184]{2,0,1:T(2,128)}, u32[]{:S(2)}) copy-start(f32[2,36,5184]{2,0,1:T(2,128)} %param.1) | copy-start | bytes 4478980
  1.5 7.6 %copy-start.1 = (f32[2,36,5184]{2,0,1:T(2,128)S(1)}, f32[2,36,5184]{2,0,1:T(2,128)}, u32[]{:S(2)}) copy-start(f32[2,36,5184]{2,0,1:T(2,128)} %param.1) | copy-start | bytes 4478980
  4.0 26.9 %collective-permute-start.4 = (f32[22,2,2048]{2,1,0:T(2,128)S(1)}, f32[22,2,2048]{2,1,0:T(2,128)S(1)}, u32[]{:S(2)}, u32[]{:S(2)}) collective-permute-start(f32[22,2,2048]{2,1,0:T(2,128)S(1)} %get-tuple-element.34), channel_id=1, source_target_pairs={{0,24},{4,28},{8,0},{12,4},{16,8},{20,12},{24,16},{28,20},{1,25},{... | collective-permute-start | bytes 1081352 | tf_op jit(solution)/shard_map/ppermute | solution.py:462
  8.0 23.0 %collective-permute-start.5 = (f32[22,2,2048]{2,1,0:T(2,128)S(1)}, f32[22,2,2048]{2,1,0:T(2,128)S(1)}, u32[]{:S(2)}, u32[]{:S(2)}) collective-permute-start(f32[22,2,2048]{2,1,0:T(2,128)S(1)} %get-tuple-element.35), channel_id=1, source_target_pairs={{0,16},{4,20},{8,24},{12,28},{16,0},{20,4},{24,8},{28,12},{1,17},{... | collective-permute-start | bytes 1081352 | tf_op jit(solution)/shard_map/ppermute | solution.py:462
  8.5 22.5 %collective-permute-start.6 = (f32[22,2,2048]{2,1,0:T(2,128)S(1)}, f32[22,2,2048]{2,1,0:T(2,128)S(1)}, u32[]{:S(2)}, u32[]{:S(2)}) collective-permute-start(f32[22,2,2048]{2,1,0:T(2,128)S(1)} %get-tuple-element.36), channel_id=1, source_target_pairs={{0,8},{4,12},{8,16},{12,20},{16,24},{20,28},{24,0},{28,4},{1,9},{5... | collective-permute-start | bytes 1081352 | tf_op jit(solution)/shard_map/ppermute | solution.py:462
  9.1 7.2 %collective-permute-start = (f32[4,2,5184]{2,1,0:T(2,128)S(1)}, f32[4,2,5184]{2,1,0:T(2,128)S(1)}, u32[]{:S(2)}, u32[]{:S(2)}) collective-permute-start(f32[4,2,5184]{2,1,0:T(2,128)S(1)} %get-tuple-element.54), channel_id=1, source_target_pairs={{0,1},{1,2},{2,3},{3,0},{4,5},{5,6},{6,7},{7,4},{8,9},{9,10},{10,1... | collective-permute-start | bytes 497672 | tf_op jit(solution)/shard_map/ppermute | solution.py:470
  17.3 7.6 %collective-permute-start.1 = (f32[4,2,2048]{2,1,0:T(2,128)S(1)}, f32[4,2,2048]{2,1,0:T(2,128)S(1)}, u32[]{:S(2)}, u32[]{:S(2)}) collective-permute-start(f32[4,2,2048]{2,1,0:T(2,128)S(1)} %get-tuple-element.30), channel_id=1, source_target_pairs={{0,24},{4,28},{8,0},{12,4},{16,8},{20,12},{24,16},{28,20},{1,25},{... | collective-permute-start | bytes 196616 | tf_op jit(solution)/shard_map/ppermute | solution.py:462
  19.6 7.7 %collective-permute-start.2 = (f32[4,2,2048]{2,1,0:T(2,128)S(1)}, f32[4,2,2048]{2,1,0:T(2,128)S(1)}, u32[]{:S(2)}, u32[]{:S(2)}) collective-permute-start(f32[4,2,2048]{2,1,0:T(2,128)S(1)} %get-tuple-element.31), channel_id=1, source_target_pairs={{0,16},{4,20},{8,24},{12,28},{16,0},{20,4},{24,8},{28,12},{1,17},{... | collective-permute-start | bytes 196616 | tf_op jit(solution)/shard_map/ppermute | solution.py:462
  24.8 6.1 %collective-permute-start.3 = (f32[4,2,2048]{2,1,0:T(2,128)S(1)}, f32[4,2,2048]{2,1,0:T(2,128)S(1)}, u32[]{:S(2)}, u32[]{:S(2)}) collective-permute-start(f32[4,2,2048]{2,1,0:T(2,128)S(1)} %get-tuple-element.32), channel_id=1, source_target_pairs={{0,8},{4,12},{8,16},{12,20},{16,24},{20,28},{24,0},{28,4},{1,9},{5... | collective-permute-start | bytes 196616 | tf_op jit(solution)/shard_map/ppermute | solution.py:462
  27.3 6.5 %collective-permute-start.12 = (f32[4,2,5184]{2,1,0:T(2,128)S(1)}, f32[4,2,5184]{2,1,0:T(2,128)S(1)}, u32[]{:S(2)}, u32[]{:S(2)}) collective-permute-start(f32[4,2,5184]{2,1,0:T(2,128)S(1)} %get-tuple-element.53), channel_id=1, source_target_pairs={{1,0},{2,1},{3,2},{0,3},{5,4},{6,5},{7,6},{4,7},{9,8},{10,9},{11,1... | collective-permute-start | bytes 497672 | tf_op jit(solution)/shard_map/ppermute | solution.py:471
  31.5 29.8 %collective-permute-start.7 = (f32[26,8,2048]{2,1,0:T(8,128)S(1)}, f32[26,8,2048]{2,1,0:T(8,128)S(1)}, u32[]{:S(2)}, u32[]{:S(2)}) collective-permute-start(f32[26,8,2048]{2,1,0:T(8,128)S(1)} %shard_map.19.planes.refs_0_), channel_id=1, source_target_pairs={{0,4},{4,0},{8,12},{12,8},{16,20},{20,16},{24,28},{28,24},{1,5},{5... | collective-permute-start | bytes 5111816 | tf_op jit(solution)/shard_map/ppermute | solution.py:465
  36.0 9.9 %collective-permute-start.13 = (f32[18,2,2048]{2,1,0:T(2,128)S(1)}, f32[18,2,2048]{2,1,0:T(2,128)S(1)}, u32[]{:S(2)}, u32[]{:S(2)}) collective-permute-start(f32[18,2,2048]{2,1,0:T(2,128)S(1)} %get-tuple-element.44), channel_id=1, source_target_pairs={{0,24},{4,28},{8,0},{12,4},{16,8},{20,12},{24,16},{28,20},{1,25},{... | collective-permute-start | bytes 884744 | tf_op jit(solution)/shard_map/ppermute | solution.py:462
  37.6 13.2 %collective-permute-start.14 = (f32[18,2,2048]{2,1,0:T(2,128)S(1)}, f32[18,2,2048]{2,1,0:T(2,128)S(1)}, u32[]{:S(2)}, u32[]{:S(2)}) collective-permute-start(f32[18,2,2048]{2,1,0:T(2,128)S(1)} %get-tuple-element.45), channel_id=1, source_target_pairs={{0,16},{4,20},{8,24},{12,28},{16,0},{20,4},{24,8},{28,12},{1,17},{... | collective-permute-start | bytes 884744 | tf_op jit(solution)/shard_map/ppermute | solution.py:462
  38.1 12.8 %collective-permute-start.15 = (f32[18,2,2048]{2,1,0:T(2,128)S(1)}, f32[18,2,2048]{2,1,0:T(2,128)S(1)}, u32[]{:S(2)}, u32[]{:S(2)}) collective-permute-start(f32[18,2,2048]{2,1,0:T(2,128)S(1)} %get-tuple-element.46), channel_id=1, source_target_pairs={{0,8},{4,12},{8,16},{12,20},{16,24},{20,28},{24,0},{28,4},{1,9},{5... | collective-permute-start | bytes 884744 | tf_op jit(solution)/shard_map/ppermute | solution.py:462
  51.3 16.3 %collective-permute-start.16 = (f32[26,8,2048]{2,1,0:T(8,128)S(1)}, f32[26,8,2048]{2,1,0:T(8,128)S(1)}, u32[]{:S(2)}, u32[]{:S(2)}) collective-permute-start(f32[26,8,2048]{2,1,0:T(8,128)S(1)} %shard_map.25.planes), channel_id=1, source_target_pairs={{0,4},{4,0},{8,12},{12,8},{16,20},{20,16},{24,28},{28,24},{1,5},{5... | collective-permute-start | bytes 5111816 | tf_op jit(solution)/shard_map/ppermute | solution.py:465
  67.0 6.3 %collective-permute-start.8 = (f32[18,8,1536]{2,1,0:T(8,128)S(1)}, f32[18,8,1536]{2,1,0:T(8,128)S(1)}, u32[]{:S(2)}, u32[]{:S(2)}) collective-permute-start(f32[18,8,1536]{2,1,0:T(8,128)S(1)} %get-tuple-element.38), channel_id=1, source_target_pairs={{0,4},{4,0},{8,12},{12,8},{16,20},{20,16},{24,28},{28,24},{1,5},{5... | collective-permute-start | bytes 2654216 | tf_op jit(solution)/shard_map/ppermute | solution.py:465
  73.3 9.6 %collective-permute-start.17 = (f32[18,8,1536]{2,1,0:T(8,128)S(1)}, f32[18,8,1536]{2,1,0:T(8,128)S(1)}, u32[]{:S(2)}, u32[]{:S(2)}) collective-permute-start(f32[18,8,1536]{2,1,0:T(8,128)S(1)} %get-tuple-element.48), channel_id=1, source_target_pairs={{0,4},{4,0},{8,12},{12,8},{16,20},{20,16},{24,28},{28,24},{1,5},{5... | collective-permute-start | bytes 2654216 | tf_op jit(solution)/shard_map/ppermute | solution.py:465
  74.1 11.1 %collective-permute-start.9 = (f32[18,2,1408]{2,1,0:T(2,128)S(1)}, f32[18,2,1408]{2,1,0:T(2,128)S(1)}, u32[]{:S(2)}, u32[]{:S(2)}) collective-permute-start(f32[18,2,1408]{2,1,0:T(2,128)S(1)} %get-tuple-element.40), channel_id=1, source_target_pairs={{0,8},{4,12},{8,16},{12,20},{16,24},{20,28},{24,0},{28,4},{1,9},{5... | collective-permute-start | bytes 608264 | tf_op jit(solution)/shard_map/ppermute | solution.py:462
  79.7 8.6 %collective-permute-start.10 = (f32[18,2,1408]{2,1,0:T(2,128)S(1)}, f32[18,2,1408]{2,1,0:T(2,128)S(1)}, u32[]{:S(2)}, u32[]{:S(2)}) collective-permute-start(f32[18,2,1408]{2,1,0:T(2,128)S(1)} %get-tuple-element.41), channel_id=1, source_target_pairs={{0,16},{4,20},{8,24},{12,28},{16,0},{20,4},{24,8},{28,12},{1,17},{... | collective-permute-start | bytes 608264 | tf_op jit(solution)/shard_map/ppermute | solution.py:462
  81.2 7.9 %collective-permute-start.11 = (f32[18,2,1408]{2,1,0:T(2,128)S(1)}, f32[18,2,1408]{2,1,0:T(2,128)S(1)}, u32[]{:S(2)}, u32[]{:S(2)}) collective-permute-start(f32[18,2,1408]{2,1,0:T(2,128)S(1)} %get-tuple-element.42), channel_id=1, source_target_pairs={{0,24},{4,28},{8,0},{12,4},{16,8},{20,12},{24,16},{28,20},{1,25},{... | collective-permute-start | bytes 608264 | tf_op jit(solution)/shard_map/ppermute | solution.py:462
  83.5 9.9 %collective-permute-start.18 = (f32[18,2,1408]{2,1,0:T(2,128)S(1)}, f32[18,2,1408]{2,1,0:T(2,128)S(1)}, u32[]{:S(2)}, u32[]{:S(2)}) collective-permute-start(f32[18,2,1408]{2,1,0:T(2,128)S(1)} %get-tuple-element.50), channel_id=1, source_target_pairs={{0,8},{4,12},{8,16},{12,20},{16,24},{20,28},{24,0},{28,4},{1,9},{5... | collective-permute-start | bytes 608264 | tf_op jit(solution)/shard_map/ppermute | solution.py:462
  84.0 11.8 %collective-permute-start.19 = (f32[18,2,1408]{2,1,0:T(2,128)S(1)}, f32[18,2,1408]{2,1,0:T(2,128)S(1)}, u32[]{:S(2)}, u32[]{:S(2)}) collective-permute-start(f32[18,2,1408]{2,1,0:T(2,128)S(1)} %get-tuple-element.51), channel_id=1, source_target_pairs={{0,16},{4,20},{8,24},{12,28},{16,0},{20,4},{24,8},{28,12},{1,17},{... | collective-permute-start | bytes 608264 | tf_op jit(solution)/shard_map/ppermute | solution.py:462
  85.2 11.5 %collective-permute-start.20 = (f32[18,2,1408]{2,1,0:T(2,128)S(1)}, f32[18,2,1408]{2,1,0:T(2,128)S(1)}, u32[]{:S(2)}, u32[]{:S(2)}) collective-permute-start(f32[18,2,1408]{2,1,0:T(2,128)S(1)} %get-tuple-element.52), channel_id=1, source_target_pairs={{0,24},{4,28},{8,0},{12,4},{16,8},{20,12},{24,16},{28,20},{1,25},{... | collective-permute-start | bytes 608264 | tf_op jit(solution)/shard_map/ppermute | solution.py:462

commit v8 on v7

--- a/solution.py
+++ b/solution.py
@@ -49,6 +49,17 @@
 
 def ceil_to(value, unit):
     return -(-value // unit) * unit
+
+
+def on_each_chip(chip, chips, body):
+    for index in range(chips):
+        pl.when(chip == index)(functools.partial(body, index))
+
+
+def peer(index, turn, chips, sending):
+    if chips & (chips - 1) == 0:
+        return index ^ turn
+    return (index + (turn if sending else -turn)) % chips
 
 
 class Ranges:
@@ -105,31 +116,32 @@
 def pack_body(ranges, bounds, chip_ref, *refs):
     chips, total, length = ranges.chips, ranges.total, ranges.length
     ins, outs = refs[:-chips], refs[-chips:]
-    chip = chip_ref[0]
-    for ahead in range(chips):
-        for target in range(chips):
-
-            @pl.when(lax.rem(chip + ahead, chips) == target)
-            def _(ahead=ahead, start=ranges.starts[target]):
-                row = 0
-                for ref, (low, high) in zip(ins, bounds):
-
-                    def plane(s, _, ref=ref, row=row - low, low=low):
-                        z = low + s * STEP
-                        lo, hi = start, start + length
-                        at = pl.ds(z, STEP)
-                        pieces = []
-                        if lo < 0:
-                            pieces.append(ref[at, :, lo + total : total])
-                        pieces.append(ref[at, :, max(lo, 0) : min(hi, total)])
-                        if hi > total:
-                            pieces.append(ref[at, :, 0 : hi - total])
-                        value = pieces[0] if len(pieces) == 1 else jnp.concatenate(pieces, axis=-1)
-                        outs[ahead][pl.ds(row + z, STEP)] = value
-                        return 0
-
-                    lax.fori_loop(0, (high - low) // STEP, plane, 0)
-                    row += high - low
+
+    def cut(ref, at, lo, hi):
+        pieces = []
+        if lo < 0:
+            pieces.append(ref[at, :, lo + total : total])
+        pieces.append(ref[at, :, max(lo, 0) : min(hi, total)])
+        if hi > total:
+            pieces.append(ref[at, :, 0 : hi - total])
+        return pieces[0] if len(pieces) == 1 else jnp.concatenate(pieces, axis=-1)
+
+    def body(index):
+        row = 0
+        for ref, (low, high) in zip(ins, bounds):
+
+            def plane(s, _, ref=ref, row=row - low, low=low):
+                z = low + s * STEP
+                for turn in range(chips):
+                    start = ranges.starts[peer(index, turn, chips, True)]
+                    value = cut(ref, pl.ds(z, STEP), start, start + length)
+                    outs[turn][pl.ds(row + z, STEP)] = value
+                return 0
+
+            lax.fori_loop(0, (high - low) // STEP, plane, 0)
+            row += high - low
+
+    on_each_chip(chip_ref[0], chips, body)
 
 
 def pack(ranges, chip, pieces):
@@ -144,36 +156,42 @@
     )
 
 
-def gather_body(groups, kept, *refs):
+def gather_body(groups, kept, chips, chip_ref, *refs):
     out = refs[-1]
-    row = 0
     if kept:
         before = refs[0]
         out[0:kept] = before[before.shape[0] - kept :]
-        refs, row = refs[1:], kept
-    slots = (len(refs) - 1) // groups
-    for group in range(groups):
-        ins = refs[group * slots : (group + 1) * slots]
-        orbs = ins[0].shape[1]
-
-        def plane(s, _, ins=ins, row=row):
-            z = s * STEP
-            for slot, ref in enumerate(ins):
-                value = ref[pl.ds(z, STEP)]
-                out[pl.ds(row + z, STEP), slot * orbs : (slot + 1) * orbs, :] = value
-            return 0
-
-        lax.fori_loop(0, ins[0].shape[0] // STEP, plane, 0)
-        row += ins[0].shape[0]
-
-
-def gather(groups, before=None, kept=0):
+        refs = refs[1:]
+
+    def body(index):
+        row = kept
+        for group in range(groups):
+            ins = refs[group * chips : (group + 1) * chips]
+            orbs = ins[0].shape[1]
+
+            def plane(s, _, ins=ins, row=row):
+                z = s * STEP
+                for turn, ref in enumerate(ins):
+                    slot = (peer(index, turn, chips, False) - index) % chips
+                    value = ref[pl.ds(z, STEP)]
+                    out[pl.ds(row + z, STEP), slot * orbs : (slot + 1) * orbs, :] = value
+                return 0
+
+            lax.fori_loop(0, ins[0].shape[0] // STEP, plane, 0)
+            row += ins[0].shape[0]
+
+    on_each_chip(chip_ref[0], chips, body)
+
+
+def gather(chip, groups, before=None, kept=0):
     depth = kept + sum(g[0].shape[0] for g in groups)
     _, orbs, span = groups[0][0].shape
+    chips = len(groups[0])
     return call(
-        functools.partial(gather_body, len(groups), kept),
-        [sds(depth, orbs * len(groups[0]), span)],
-        [*([before] if kept else []), *(p for g in groups for p in g)],
+        functools.partial(gather_body, len(groups), kept, chips),
+        [sds(depth, orbs * chips, span)],
+        [chip, *([before] if kept else []), *(p for g in groups for p in g)],
+        smem=True,
     )[0]
 
 
@@ -409,44 +427,47 @@
     orbs = outs[0].shape[1]
     lanes = aligned(ranges.out_at(chip_ref[0]), ranges.out_length)
 
-    def plane(s, _):
-        at = pl.ds(s * STEP, STEP)
-        value = mine[at, :, lanes] + theirs[at, :, lanes]
-        for slot, out in enumerate(outs):
-            out[at] = value[:, slot * orbs : (slot + 1) * orbs]
-        return 0
-
-    lax.fori_loop(0, outs[0].shape[0] // STEP, plane, 0)
+    def body(index):
+        def plane(s, _):
+            at = pl.ds(s * STEP, STEP)
+            value = mine[at, :, lanes] + theirs[at, :, lanes]
+            for turn, out in enumerate(outs):
+                slot = (peer(index, turn, ranges.chips, True) - index) % ranges.chips
+                out[at] = value[:, slot * orbs : (slot + 1) * orbs]
+            return 0
+
+        lax.fori_loop(0, outs[0].shape[0] // STEP, plane, 0)
+
+    on_each_chip(chip_ref[0], ranges.chips, body)
 
 
 def place_body(ranges, chip_ref, *refs):
     chips = ranges.chips
     ins, out = refs[:-1], refs[-1]
-    chip = chip_ref[0]
-    for behind in range(chips):
-        for source in range(chips):
-
-            @pl.when(lax.rem(chip + chips - behind, chips) == source)
-            def _(parts=ins[behind::chips], source=source):
-                base = ranges.out_starts[source]
-                lo, hi = source * ranges.width, (source + 1) * ranges.width
-                row = 0
-                for ref in parts:
-
-                    def plane(s, _, ref=ref, row=row):
-                        at = pl.ds(s * STEP, STEP)
-                        into = pl.ds(row + s * STEP, STEP)
-                        lane = lo
-                        while lane < hi:
-                            stop = min(floor_to(lane, LANES) + LANES, hi)
-                            if lane % LANES == 0:
-                                stop = max(floor_to(hi, LANES), stop)
-                            out[into, :, lane:stop] = ref[at, :, lane - base : stop - base]
-                            lane = stop
-                        return 0
-
-                    lax.fori_loop(0, ref.shape[0] // STEP, plane, 0)
-                    row += ref.shape[0]
+
+    def body(index):
+        row = 0
+        for first in range(0, len(ins), chips):
+
+            def plane(s, _, row=row, first=first):
+                at = pl.ds(s * STEP, STEP)
+                into = pl.ds(row + s * STEP, STEP)
+                for turn in range(chips):
+                    source = peer(index, turn, chips, False)
+                    base = ranges.out_starts[source]
+                    lane, hi = source * ranges.width, (source + 1) * ranges.width
+                    while lane < hi:
+                        stop = min(floor_to(lane, LANES) + LANES, hi)
+                        if lane % LANES == 0:
+                            stop = max(floor_to(hi, LANES), stop)
+                        out[into, :, lane:stop] = ins[first + turn][at, :, lane - base : stop - base]
+                        lane = stop
+                return 0
+
+            lax.fori_loop(0, ins[first].shape[0] // STEP, plane, 0)
+            row += ins[first].shape[0]
+
+    on_each_chip(chip_ref[0], chips, body)
 
 
 def per_device(n_band, orbitals):
@@ -457,8 +478,8 @@
     chip = jnp.stack([index // 2, index % 2]).astype(jnp.int32)
     planes = jnp.transpose(orbitals, (1, 0, 2))
 
-    def along(value, steps):
-        pairs = [(i, (i + 2 * steps) % n_band) for i in range(n_band)]
+    def exchange(value, turn):
+        pairs = [(i, peer(i // 2, turn, chips, True) * 2 + i % 2) for i in range(n_band)]
         return lax.ppermute(value, "band", pairs)
 
     def partner_core(value):
@@ -470,18 +491,15 @@
     below = lax.ppermute(planes[depth - HALO :], "slab", up)
     above = lax.ppermute(planes[:HALO], "slab", down)
 
-    order = [0] + list(range(chips - 1, 0, -1))
-
     def spread(sent):
         got = [sent[0]]
-        for s in range(1, chips):
-            got.append(along(sent[s], s))
+        for turn in range(1, chips):
+            got.append(exchange(sent[turn], turn))
         return got
 
     def fetch(pieces):
         sent = pack(ranges, chip, pieces)
-        got = spread(sent)
-        return [got[s] for s in order]
+        return spread(sent)
 
     inner = depth // CHUNKS
     cut = inner + HALO
@@ -489,7 +507,7 @@
     banded = weights(ranges, chip)
     got_low = fetch([(below, 0, HALO)])
     got_b = fetch([(planes, cut, depth), (above, 0, HALO)])
-    planes_a = gather([got_low, got_a])
+    planes_a = gather(chip, [got_low, got_a])
 
     rows = orbs * chips
     full, swept = (inner + 2 * HALO) * rows, (inner + 2 * REACH) * rows
@@ -538,7 +556,7 @@
     other_a = partner_core(planes_a)
     acc_a = same(planes_a)
     acc_a, back_a = cross(planes_a, other_a, acc_a)
-    planes_b = gather([got_b], before=planes_a, kept=2 * HALO)
+    planes_b = gather(chip, [got_b], before=planes_a, kept=2 * HALO)
     other_b = partner_core(planes_b)
     home = give(acc_a, back_a)
     acc_b, back_b = cross(planes_b, other_b)

time: 101 us -> 102 us (level); the launches traced: 99 us -> 102 us
  waiting for transfers between devices: 31.5 us -> 36.4 us
  starting transfers between devices: 29.4 us -> 27.6 us
    ppermute x15, waiting for transfers between devices: 23.6 us -> 29.2 us  [exchange(): return lax.ppermute(value, 'band', pairs)]
    ppermute x15, starting transfers between devices: 23.3 us -> 21.2 us  [exchange(): return lax.ppermute(value, 'band', pairs)]
  transfers between devices with their start and end apart: 21 -> 21, of which waited for: 10 -> 8; matrix products, arithmetic and copies ran while one was open for 0% -> 0% of each run, Pallas kernels for 32% -> 32%
where the time goes in v8:
time: 102 us
  waiting for transfers between devices  36.4 us (36%)
  Pallas kernels  35.8 us (35%)
  starting transfers between devices  27.6 us (27%)
  local copies, waits for them, and re-layouts  1.41 us (1%)
    pallas_call x13, Pallas kernels, call(): pl.pallas_call(body, out_shape=out, in_specs=specs, out_specs=[VMEM] * le...  35.8 us
    ppermute x15, waiting for transfers between devices, exchange(): return lax.ppermute(value, 'band', pairs)  29.2 us
    ppermute x15, starting transfers between devices, exchange(): return lax.ppermute(value, 'band', pairs)  21.2 us
    ppermute x1, waiting for transfers between devices, per_device(): below = lax.ppermute(planes[depth - HALO:], 'slab', up)  5.47 us
    ppermute x1, starting transfers between devices, per_device(): above = lax.ppermute(planes[:HALO], 'slab', down)  3.6 us
    ppermute x1, starting transfers between devices, per_device(): below = lax.ppermute(planes[depth - HALO:], 'slab', up)  2.09 us
  transfers between devices with their start and end apart: 21, of which 8 were waited for; matrix products, arithmetic and copies ran while one was open for 0% of the time, Pallas kernels for 32%

profile of v8, /device:TPU:0, one launch (start us, length us, event | category | flops | bytes accessed | tf_op | source)
XLA Modules:
  0.0 101.5 jit_solution(2825988886002916215)
XLA Ops:
  0.1 1.4 %copy-done = f32[2,36,5184]{2,0,1:T(2,128)S(1)} copy-done((f32[2,36,5184]{2,0,1:T(2,128)S(1)}, f32[2,36,5184]{2,0,1:T(2,128)}, u32[]{:S(2)}) %copy-start) | copy-done | bytes 1493016
  1.5 1.6 %shard_map.18 = (f32[22,2,2048]{2,1,0:T(2,128)S(1)}, f32[22,2,2048]{2,1,0:T(2,128)S(1)}, f32[22,2,2048]{2,1,0:T(2,128)S(1)}, f32[22,2,2048]{2,1,0:T(2,128)S(1)}) custom-call(s32[2]{0:T(128)S(1)} %pad_add_fusion.chip_ref, f32[36,2,5184]{2,1,0:T(2,128)S(1)} %bitcast.4), custom_call_target="tpu_custom_call" | custom-call | bytes 2934792 | tf_op jit(solution)/shard_map/pallas_call | solution.py:35
  3.0 3.0 %collective-permute-start.4 = (f32[22,2,2048]{2,1,0:T(2,128)S(1)}, f32[22,2,2048]{2,1,0:T(2,128)S(1)}, u32[]{:S(2)}, u32[]{:S(2)}) collective-permute-start(f32[22,2,2048]{2,1,0:T(2,128)S(1)} %get-tuple-element.34), channel_id=1, source_target_pairs={{0,8},{4,12},{8,0},{12,4},{16,24},{20,28},{24,16},{28,20},{1,9},{5... | collective-permute-start | bytes 1081352 | tf_op jit(solution)/shard_map/ppermute | solution.py:483
  6.1 1.5 %collective-permute-start.5 = (f32[22,2,2048]{2,1,0:T(2,128)S(1)}, f32[22,2,2048]{2,1,0:T(2,128)S(1)}, u32[]{:S(2)}, u32[]{:S(2)}) collective-permute-start(f32[22,2,2048]{2,1,0:T(2,128)S(1)} %get-tuple-element.35), channel_id=1, source_target_pairs={{0,16},{4,20},{8,24},{12,28},{16,0},{20,4},{24,8},{28,12},{1,17},{... | collective-permute-start | bytes 1081352 | tf_op jit(solution)/shard_map/ppermute | solution.py:483
  7.6 2.1 %collective-permute-start = (f32[4,2,5184]{2,1,0:T(2,128)S(1)}, f32[4,2,5184]{2,1,0:T(2,128)S(1)}, u32[]{:S(2)}, u32[]{:S(2)}) collective-permute-start(f32[4,2,5184]{2,1,0:T(2,128)S(1)} %get-tuple-element.54), channel_id=1, source_target_pairs={{0,1},{1,2},{2,3},{3,0},{4,5},{5,6},{6,7},{7,4},{8,9},{9,10},{10,1... | collective-permute-start | bytes 497672 | tf_op jit(solution)/shard_map/ppermute | solution.py:491
  9.7 5.5 %collective-permute-done.refs_0_ = f32[4,2,5184]{2,1,0:T(2,128)S(1)} collective-permute-done((f32[4,2,5184]{2,1,0:T(2,128)S(1)}, f32[4,2,5184]{2,1,0:T(2,128)S(1)}, u32[]{:S(2)}, u32[]{:S(2)}) %collective-permute-start) | collective-permute-done | bytes 165920 | tf_op jit(solution)/shard_map/ppermute | solution.py:491
  15.9 1.7 %collective-permute-start.1 = (f32[4,2,2048]{2,1,0:T(2,128)S(1)}, f32[4,2,2048]{2,1,0:T(2,128)S(1)}, u32[]{:S(2)}, u32[]{:S(2)}) collective-permute-start(f32[4,2,2048]{2,1,0:T(2,128)S(1)} %get-tuple-element.30), channel_id=1, source_target_pairs={{0,8},{4,12},{8,0},{12,4},{16,24},{20,28},{24,16},{28,20},{1,9},{5... | collective-permute-start | bytes 196616 | tf_op jit(solution)/shard_map/ppermute | solution.py:483
  17.6 1.5 %collective-permute-start.2 = (f32[4,2,2048]{2,1,0:T(2,128)S(1)}, f32[4,2,2048]{2,1,0:T(2,128)S(1)}, u32[]{:S(2)}, u32[]{:S(2)}) collective-permute-start(f32[4,2,2048]{2,1,0:T(2,128)S(1)} %get-tuple-element.31), channel_id=1, source_target_pairs={{0,16},{4,20},{8,24},{12,28},{16,0},{20,4},{24,8},{28,12},{1,17},{... | collective-permute-start | bytes 196616 | tf_op jit(solution)/shard_map/ppermute | solution.py:483
  19.1 4.5 %collective-permute-done.1.refs_1_ = f32[4,2,2048]{2,1,0:T(2,128)S(1)} collective-permute-done((f32[4,2,2048]{2,1,0:T(2,128)S(1)}, f32[4,2,2048]{2,1,0:T(2,128)S(1)}, u32[]{:S(2)}, u32[]{:S(2)}) %collective-permute-start.1) | collective-permute-done | bytes 65568 | tf_op jit(solution)/shard_map/ppermute | solution.py:483
  23.6 2.7 %collective-permute-start.3 = (f32[4,2,2048]{2,1,0:T(2,128)S(1)}, f32[4,2,2048]{2,1,0:T(2,128)S(1)}, u32[]{:S(2)}, u32[]{:S(2)}) collective-permute-start(f32[4,2,2048]{2,1,0:T(2,128)S(1)} %get-tuple-element.32), channel_id=1, source_target_pairs={{0,24},{4,28},{8,16},{12,20},{16,8},{20,12},{24,0},{28,4},{1,25},{... | collective-permute-start | bytes 196616 | tf_op jit(solution)/shard_map/ppermute | solution.py:483
  26.3 3.6 %collective-permute-start.12 = (f32[4,2,5184]{2,1,0:T(2,128)S(1)}, f32[4,2,5184]{2,1,0:T(2,128)S(1)}, u32[]{:S(2)}, u32[]{:S(2)}) collective-permute-start(f32[4,2,5184]{2,1,0:T(2,128)S(1)} %get-tuple-element.53), channel_id=1, source_target_pairs={{1,0},{2,1},{3,2},{0,3},{5,4},{6,5},{7,6},{4,7},{9,8},{10,9},{11,1... | collective-permute-start | bytes 497672 | tf_op jit(solution)/shard_map/ppermute | solution.py:492
  30.0 1.1 %shard_map.19.planes.refs_0_ = f32[26,8,2048]{2,1,0:T(8,128)S(1)} custom-call(s32[2]{0:T(128)S(1)} %pad_add_fusion.chip_ref, f32[4,2,2048]{2,1,0:T(2,128)S(1)} %get-tuple-element.29.refs_0_, f32[4,2,2048]{2,1,0:T(2,128)S(1)} %collective-permute-done.1.refs_1_, f32[4,2,2048]{2,1,0:T(2,128)S(1)} %collective-permute-done.2.refs_2_, ...), custom_call_target="tpu_custom_call" | custom-call | bytes 3407880 | tf_op jit(solution)/shard_map/pallas_call | solution.py:35
  31.1 1.7 %collective-permute-done.12.refs_1_ = f32[4,2,5184]{2,1,0:T(2,128)S(1)} collective-permute-done((f32[4,2,5184]{2,1,0:T(2,128)S(1)}, f32[4,2,5184]{2,1,0:T(2,128)S(1)}, u32[]{:S(2)}, u32[]{:S(2)}) %collective-permute-start.12) | collective-permute-done | bytes 165920 | tf_op jit(solution)/shard_map/ppermute | solution.py:492
  32.8 1.4 %shard_map.24 = (f32[18,2,2048]{2,1,0:T(2,128)S(1)}, f32[18,2,2048]{2,1,0:T(2,128)S(1)}, f32[18,2,2048]{2,1,0:T(2,128)S(1)}, f32[18,2,2048]{2,1,0:T(2,128)S(1)}) custom-call(s32[2]{0:T(128)S(1)} %pad_add_fusion.chip_ref, f32[36,2,5184]{2,1,0:T(2,128)S(1)} %bitcast.6, f32[4,2,5184]{2,1,0:T(2,128)S(1)} %collective-permute-done.12.refs_1_), custom_call_target="tpu_custom_call" | custom-call | bytes 2838536 | tf_op jit(solution)/shard_map/pallas_call | solution.py:35
  35.4 2.3 %collective-permute-start.15 = (f32[18,2,2048]{2,1,0:T(2,128)S(1)}, f32[18,2,2048]{2,1,0:T(2,128)S(1)}, u32[]{:S(2)}, u32[]{:S(2)}) collective-permute-start(f32[18,2,2048]{2,1,0:T(2,128)S(1)} %get-tuple-element.46), channel_id=1, source_target_pairs={{0,24},{4,28},{8,16},{12,20},{16,8},{20,12},{24,0},{28,4},{1,25},{... | collective-permute-start | bytes 884744 | tf_op jit(solution)/shard_map/ppermute | solution.py:483
  37.8 6.4 %collective-permute-done.13.refs_2_ = f32[18,2,2048]{2,1,0:T(2,128)S(1)} collective-permute-done((f32[18,2,2048]{2,1,0:T(2,128)S(1)}, f32[18,2,2048]{2,1,0:T(2,128)S(1)}, u32[]{:S(2)}, u32[]{:S(2)}) %collective-permute-start.13) | collective-permute-done | bytes 294944 | tf_op jit(solution)/shard_map/ppermute | solution.py:483
  44.2 4.5 %collective-permute-done.14.refs_3_ = f32[18,2,2048]{2,1,0:T(2,128)S(1)} collective-permute-done((f32[18,2,2048]{2,1,0:T(2,128)S(1)}, f32[18,2,2048]{2,1,0:T(2,128)S(1)}, u32[]{:S(2)}, u32[]{:S(2)}) %collective-permute-start.14) | collective-permute-done | bytes 294944 | tf_op jit(solution)/shard_map/ppermute | solution.py:483
  48.6 1.1 %shard_map.25.planes = f32[26,8,2048]{2,1,0:T(8,128)S(1)} custom-call(s32[2]{0:T(128)S(1)} %pad_add_fusion.chip_ref, f32[26,8,2048]{2,1,0:T(8,128)S(1)} %shard_map.19.planes.refs_0_, f32[18,2,2048]{2,1,0:T(2,128)S(1)} %get-tuple-element.43.refs_1_, f32[18,2,2048]{2,1,0:T(2,128)S(1)} %collective-permute-done.13.refs_2_, ...), custom_call_target="tpu_custom_call" | custom-call | bytes 4587528 | tf_op jit(solution)/shard_map/pallas_call | solution.py:35
  49.9 5.0 %shard_map.20.w_ref = bf16[13,768,256]{2,1,0:T(8,128)(2,1)S(1)} custom-call(s32[2]{0:T(128)S(1)} %pad_add_fusion.chip_ref), custom_call_target="tpu_custom_call" | custom-call | bytes 10223624 | tf_op jit(solution)/shard_map/pallas_call | solution.py:35
  54.9 4.9 %shard_map.21.refs_0_ = f32[18,8,1536]{2,1,0:T(8,128)S(1)} custom-call(f32[26,8,2048]{2,1,0:T(8,128)S(1)} %shard_map.19.planes.refs_0_, bf16[13,768,256]{2,1,0:T(8,128)(2,1)S(1)} %shard_map.20.w_ref), custom_call_target="tpu_custom_call" | custom-call | flops 4253024256 | bytes 12812288 | tf_op jit(solution)/shard_map/pallas_call | solution.py:35
  59.8 5.7 %shard_map.22 = (f32[18,8,1536]{2,1,0:T(8,128)S(1)}, f32[18,8,1536]{2,1,0:T(8,128)S(1)}) custom-call(s32[2]{0:T(128)S(1)} %pad_add_fusion.chip_ref, f32[26,8,2048]{2,1,0:T(8,128)S(1)} %shard_map.19.planes.refs_0_, bf16[13,768,256]{2,1,0:T(8,128)(2,1)S(1)} %shard_map.20.w_ref, f32[26,8,2048]{2,1,0:T(8,128)S(1)} %collective-permute-done.7.other, ...), custom_call_target="tpu_custom_call" | custom-call | flops 4253024256 | bytes 16285704 | tf_op jit(solution)/shard_map/pallas_call | solution.py:35
  66.1 5.7 %shard_map.26 = (f32[18,8,1536]{2,1,0:T(8,128)S(1)}, f32[18,8,1536]{2,1,0:T(8,128)S(1)}) custom-call(s32[2]{0:T(128)S(1)} %pad_add_fusion.chip_ref, f32[26,8,2048]{2,1,0:T(8,128)S(1)} %shard_map.25.planes, bf16[13,768,256]{2,1,0:T(8,128)(2,1)S(1)} %shard_map.20.w_ref, f32[26,8,2048]{2,1,0:T(8,128)S(1)} %collective-permute-done.16.other), custom_call_target="tpu_custom_call" | custom-call | flops 4253024256 | bytes 15400968 | tf_op jit(solution)/shard_map/pallas_call | solution.py:35
  71.8 1.0 shard_map.23
  72.8 1.5 %collective-permute-start.9 = (f32[18,2,1408]{2,1,0:T(2,128)S(1)}, f32[18,2,1408]{2,1,0:T(2,128)S(1)}, u32[]{:S(2)}, u32[]{:S(2)}) collective-permute-start(f32[18,2,1408]{2,1,0:T(2,128)S(1)} %get-tuple-element.40), channel_id=1, source_target_pairs={{0,8},{4,12},{8,0},{12,4},{16,24},{20,28},{24,16},{28,20},{1,9},{5... | collective-permute-start | bytes 608264 | tf_op jit(solution)/shard_map/ppermute | solution.py:483
  74.3 5.0 %shard_map.27.mine = f32[18,8,1536]{2,1,0:T(8,128)S(1)} custom-call(f32[26,8,2048]{2,1,0:T(8,128)S(1)} %shard_map.25.planes, bf16[13,768,256]{2,1,0:T(8,128)(2,1)S(1)} %shard_map.20.w_ref, f32[18,8,1536]{2,1,0:T(8,128)S(1)} %get-tuple-element.47.refs_0_), custom_call_target="tpu_custom_call" | custom-call | flops 4253024256 | bytes 13697024 | tf_op jit(solution)/shard_map/pallas_call | solution.py:35
  80.0 1.4 %collective-permute-start.11 = (f32[18,2,1408]{2,1,0:T(2,128)S(1)}, f32[18,2,1408]{2,1,0:T(2,128)S(1)}, u32[]{:S(2)}, u32[]{:S(2)}) collective-permute-start(f32[18,2,1408]{2,1,0:T(2,128)S(1)} %get-tuple-element.42), channel_id=1, source_target_pairs={{0,24},{4,28},{8,16},{12,20},{16,8},{20,12},{24,0},{28,4},{1,25},{... | collective-permute-start | bytes 608264 | tf_op jit(solution)/shard_map/ppermute | solution.py:483
  82.2 1.5 %collective-permute-start.18 = (f32[18,2,1408]{2,1,0:T(2,128)S(1)}, f32[18,2,1408]{2,1,0:T(2,128)S(1)}, u32[]{:S(2)}, u32[]{:S(2)}) collective-permute-start(f32[18,2,1408]{2,1,0:T(2,128)S(1)} %get-tuple-element.50), channel_id=1, source_target_pairs={{0,8},{4,12},{8,0},{12,4},{16,24},{20,28},{24,16},{28,20},{1,9},{5... | collective-permute-start | bytes 608264 | tf_op jit(solution)/shard_map/ppermute | solution.py:483
  84.3 1.4 %collective-permute-start.20 = (f32[18,2,1408]{2,1,0:T(2,128)S(1)}, f32[18,2,1408]{2,1,0:T(2,128)S(1)}, u32[]{:S(2)}, u32[]{:S(2)}) collective-permute-start(f32[18,2,1408]{2,1,0:T(2,128)S(1)} %get-tuple-element.52), channel_id=1, source_target_pairs={{0,24},{4,28},{8,16},{12,20},{16,8},{20,12},{24,0},{28,4},{1,25},{... | collective-permute-start | bytes 608264 | tf_op jit(solution)/shard_map/ppermute | solution.py:483
  85.7 6.4 %collective-permute-done.10.refs_2_ = f32[18,2,1408]{2,1,0:T(2,128)S(1)} collective-permute-done((f32[18,2,1408]{2,1,0:T(2,128)S(1)}, f32[18,2,1408]{2,1,0:T(2,128)S(1)}, u32[]{:S(2)}, u32[]{:S(2)}) %collective-permute-start.10) | collective-permute-done | bytes 202784 | tf_op jit(solution)/shard_map/ppermute | solution.py:483
  92.1 1.0 collective-permute-done.18.refs_5_
  93.1 6.5 %collective-permute-done.19.refs_6_ = f32[18,2,1408]{2,1,0:T(2,128)S(1)} collective-permute-done((f32[18,2,1408]{2,1,0:T(2,128)S(1)}, f32[18,2,1408]{2,1,0:T(2,128)S(1)}, u32[]{:S(2)}, u32[]{:S(2)}) %collective-permute-start.19) | collective-permute-done | bytes 202784 | tf_op jit(solution)/shard_map/ppermute | solution.py:483
  99.5 2.0 %shard_map.29 = f32[36,2,5184]{2,1,0:T(2,128)} custom-call(s32[2]{0:T(128)S(1)} %pad_add_fusion.chip_ref, f32[18,2,1408]{2,1,0:T(2,128)S(1)} %get-tuple-element.39.refs_0_, f32[18,2,1408]{2,1,0:T(2,128)S(1)} %collective-permute-done.9.refs_1_, f32[18,2,1408]{2,1,0:T(2,128)S(1)} %collective-permute-done.10.refs_2_, ...), custom_call_target="tpu_custom_call" | custom-call | bytes 3115016 | tf_op jit(solution)/shard_map/pallas_call | solution.py:35
  (29 shorter events, 5.0 us)
Async XLA Ops:
  0.1 1.4 %copy-start = (f32[2,36,5184]{2,0,1:T(2,128)S(1)}, f32[2,36,5184]{2,0,1:T(2,128)}, u32[]{:S(2)}) copy-start(f32[2,36,5184]{2,0,1:T(2,128)} %param.1) | copy-start | bytes 4478980
  1.5 6.1 %copy-start.1 = (f32[2,36,5184]{2,0,1:T(2,128)S(1)}, f32[2,36,5184]{2,0,1:T(2,128)}, u32[]{:S(2)}) copy-start(f32[2,36,5184]{2,0,1:T(2,128)} %param.1) | copy-start | bytes 4478980
  3.0 26.9 %collective-permute-start.4 = (f32[22,2,2048]{2,1,0:T(2,128)S(1)}, f32[22,2,2048]{2,1,0:T(2,128)S(1)}, u32[]{:S(2)}, u32[]{:S(2)}) collective-permute-start(f32[22,2,2048]{2,1,0:T(2,128)S(1)} %get-tuple-element.34), channel_id=1, source_target_pairs={{0,8},{4,12},{8,0},{12,4},{16,24},{20,28},{24,16},{28,20},{1,9},{5... | collective-permute-start | bytes 1081352 | tf_op jit(solution)/shard_map/ppermute | solution.py:483
  6.1 23.9 %collective-permute-start.5 = (f32[22,2,2048]{2,1,0:T(2,128)S(1)}, f32[22,2,2048]{2,1,0:T(2,128)S(1)}, u32[]{:S(2)}, u32[]{:S(2)}) collective-permute-start(f32[22,2,2048]{2,1,0:T(2,128)S(1)} %get-tuple-element.35), channel_id=1, source_target_pairs={{0,16},{4,20},{8,24},{12,28},{16,0},{20,4},{24,8},{28,12},{1,17},{... | collective-permute-start | bytes 1081352 | tf_op jit(solution)/shard_map/ppermute | solution.py:483
  7.6 22.4 %collective-permute-start.6 = (f32[22,2,2048]{2,1,0:T(2,128)S(1)}, f32[22,2,2048]{2,1,0:T(2,128)S(1)}, u32[]{:S(2)}, u32[]{:S(2)}) collective-permute-start(f32[22,2,2048]{2,1,0:T(2,128)S(1)} %get-tuple-element.36), channel_id=1, source_target_pairs={{0,24},{4,28},{8,16},{12,20},{16,8},{20,12},{24,0},{28,4},{1,25},{... | collective-permute-start | bytes 1081352 | tf_op jit(solution)/shard_map/ppermute | solution.py:483
  7.6 7.6 %collective-permute-start = (f32[4,2,5184]{2,1,0:T(2,128)S(1)}, f32[4,2,5184]{2,1,0:T(2,128)S(1)}, u32[]{:S(2)}, u32[]{:S(2)}) collective-permute-start(f32[4,2,5184]{2,1,0:T(2,128)S(1)} %get-tuple-element.54), channel_id=1, source_target_pairs={{0,1},{1,2},{2,3},{3,0},{4,5},{5,6},{6,7},{7,4},{8,9},{9,10},{10,1... | collective-permute-start | bytes 497672 | tf_op jit(solution)/shard_map/ppermute | solution.py:491
  15.9 7.7 %collective-permute-start.1 = (f32[4,2,2048]{2,1,0:T(2,128)S(1)}, f32[4,2,2048]{2,1,0:T(2,128)S(1)}, u32[]{:S(2)}, u32[]{:S(2)}) collective-permute-start(f32[4,2,2048]{2,1,0:T(2,128)S(1)} %get-tuple-element.30), channel_id=1, source_target_pairs={{0,8},{4,12},{8,0},{12,4},{16,24},{20,28},{24,16},{28,20},{1,9},{5... | collective-permute-start | bytes 196616 | tf_op jit(solution)/shard_map/ppermute | solution.py:483
  17.6 8.7 %collective-permute-start.2 = (f32[4,2,2048]{2,1,0:T(2,128)S(1)}, f32[4,2,2048]{2,1,0:T(2,128)S(1)}, u32[]{:S(2)}, u32[]{:S(2)}) collective-permute-start(f32[4,2,2048]{2,1,0:T(2,128)S(1)} %get-tuple-element.31), channel_id=1, source_target_pairs={{0,16},{4,20},{8,24},{12,28},{16,0},{20,4},{24,8},{28,12},{1,17},{... | collective-permute-start | bytes 196616 | tf_op jit(solution)/shard_map/ppermute | solution.py:483
  23.6 6.3 %collective-permute-start.3 = (f32[4,2,2048]{2,1,0:T(2,128)S(1)}, f32[4,2,2048]{2,1,0:T(2,128)S(1)}, u32[]{:S(2)}, u32[]{:S(2)}) collective-permute-start(f32[4,2,2048]{2,1,0:T(2,128)S(1)} %get-tuple-element.32), channel_id=1, source_target_pairs={{0,24},{4,28},{8,16},{12,20},{16,8},{20,12},{24,0},{28,4},{1,25},{... | collective-permute-start | bytes 196616 | tf_op jit(solution)/shard_map/ppermute | solution.py:483
  26.3 6.5 %collective-permute-start.12 = (f32[4,2,5184]{2,1,0:T(2,128)S(1)}, f32[4,2,5184]{2,1,0:T(2,128)S(1)}, u32[]{:S(2)}, u32[]{:S(2)}) collective-permute-start(f32[4,2,5184]{2,1,0:T(2,128)S(1)} %get-tuple-element.53), channel_id=1, source_target_pairs={{1,0},{2,1},{3,2},{0,3},{5,4},{6,5},{7,6},{4,7},{9,8},{10,9},{11,1... | collective-permute-start | bytes 497672 | tf_op jit(solution)/shard_map/ppermute | solution.py:492
  31.1 28.7 %collective-permute-start.7 = (f32[26,8,2048]{2,1,0:T(8,128)S(1)}, f32[26,8,2048]{2,1,0:T(8,128)S(1)}, u32[]{:S(2)}, u32[]{:S(2)}) collective-permute-start(f32[26,8,2048]{2,1,0:T(8,128)S(1)} %shard_map.19.planes.refs_0_), channel_id=1, source_target_pairs={{0,4},{4,0},{8,12},{12,8},{16,20},{20,16},{24,28},{28,24},{1,5},{5... | collective-permute-start | bytes 5111816 | tf_op jit(solution)/shard_map/ppermute | solution.py:486
  34.2 9.9 %collective-permute-start.13 = (f32[18,2,2048]{2,1,0:T(2,128)S(1)}, f32[18,2,2048]{2,1,0:T(2,128)S(1)}, u32[]{:S(2)}, u32[]{:S(2)}) collective-permute-start(f32[18,2,2048]{2,1,0:T(2,128)S(1)} %get-tuple-element.44), channel_id=1, source_target_pairs={{0,8},{4,12},{8,0},{12,4},{16,24},{20,28},{24,16},{28,20},{1,9},{5... | collective-permute-start | bytes 884744 | tf_op jit(solution)/shard_map/ppermute | solution.py:483
  34.8 13.8 %collective-permute-start.14 = (f32[18,2,2048]{2,1,0:T(2,128)S(1)}, f32[18,2,2048]{2,1,0:T(2,128)S(1)}, u32[]{:S(2)}, u32[]{:S(2)}) collective-permute-start(f32[18,2,2048]{2,1,0:T(2,128)S(1)} %get-tuple-element.45), channel_id=1, source_target_pairs={{0,16},{4,20},{8,24},{12,28},{16,0},{20,4},{24,8},{28,12},{1,17},{... | collective-permute-start | bytes 884744 | tf_op jit(solution)/shard_map/ppermute | solution.py:483
  35.4 13.2 %collective-permute-start.15 = (f32[18,2,2048]{2,1,0:T(2,128)S(1)}, f32[18,2,2048]{2,1,0:T(2,128)S(1)}, u32[]{:S(2)}, u32[]{:S(2)}) collective-permute-start(f32[18,2,2048]{2,1,0:T(2,128)S(1)} %get-tuple-element.46), channel_id=1, source_target_pairs={{0,24},{4,28},{8,16},{12,20},{16,8},{20,12},{24,0},{28,4},{1,25},{... | collective-permute-start | bytes 884744 | tf_op jit(solution)/shard_map/ppermute | solution.py:483
  49.8 16.3 %collective-permute-start.16 = (f32[26,8,2048]{2,1,0:T(8,128)S(1)}, f32[26,8,2048]{2,1,0:T(8,128)S(1)}, u32[]{:S(2)}, u32[]{:S(2)}) collective-permute-start(f32[26,8,2048]{2,1,0:T(8,128)S(1)} %shard_map.25.planes), channel_id=1, source_target_pairs={{0,4},{4,0},{8,12},{12,8},{16,20},{20,16},{24,28},{28,24},{1,5},{5... | collective-permute-start | bytes 5111816 | tf_op jit(solution)/shard_map/ppermute | solution.py:486
  65.5 6.3 %collective-permute-start.8 = (f32[18,8,1536]{2,1,0:T(8,128)S(1)}, f32[18,8,1536]{2,1,0:T(8,128)S(1)}, u32[]{:S(2)}, u32[]{:S(2)}) collective-permute-start(f32[18,8,1536]{2,1,0:T(8,128)S(1)} %get-tuple-element.38), channel_id=1, source_target_pairs={{0,4},{4,0},{8,12},{12,8},{16,20},{20,16},{24,28},{28,24},{1,5},{5... | collective-permute-start | bytes 2654216 | tf_op jit(solution)/shard_map/ppermute | solution.py:486
  71.8 9.7 %collective-permute-start.17 = (f32[18,8,1536]{2,1,0:T(8,128)S(1)}, f32[18,8,1536]{2,1,0:T(8,128)S(1)}, u32[]{:S(2)}, u32[]{:S(2)}) collective-permute-start(f32[18,8,1536]{2,1,0:T(8,128)S(1)} %get-tuple-element.48), channel_id=1, source_target_pairs={{0,4},{4,0},{8,12},{12,8},{16,20},{20,16},{24,28},{28,24},{1,5},{5... | collective-permute-start | bytes 2654216 | tf_op jit(solution)/shard_map/ppermute | solution.py:486
  72.8 11.5 %collective-permute-start.9 = (f32[18,2,1408]{2,1,0:T(2,128)S(1)}, f32[18,2,1408]{2,1,0:T(2,128)S(1)}, u32[]{:S(2)}, u32[]{:S(2)}) collective-permute-start(f32[18,2,1408]{2,1,0:T(2,128)S(1)} %get-tuple-element.40), channel_id=1, source_target_pairs={{0,8},{4,12},{8,0},{12,4},{16,24},{20,28},{24,16},{28,20},{1,9},{5... | collective-permute-start | bytes 608264 | tf_op jit(solution)/shard_map/ppermute | solution.py:483
  79.3 12.8 %collective-permute-start.10 = (f32[18,2,1408]{2,1,0:T(2,128)S(1)}, f32[18,2,1408]{2,1,0:T(2,128)S(1)}, u32[]{:S(2)}, u32[]{:S(2)}) collective-permute-start(f32[18,2,1408]{2,1,0:T(2,128)S(1)} %get-tuple-element.41), channel_id=1, source_target_pairs={{0,16},{4,20},{8,24},{12,28},{16,0},{20,4},{24,8},{28,12},{1,17},{... | collective-permute-start | bytes 608264 | tf_op jit(solution)/shard_map/ppermute | solution.py:483
  80.0 12.1 %collective-permute-start.11 = (f32[18,2,1408]{2,1,0:T(2,128)S(1)}, f32[18,2,1408]{2,1,0:T(2,128)S(1)}, u32[]{:S(2)}, u32[]{:S(2)}) collective-permute-start(f32[18,2,1408]{2,1,0:T(2,128)S(1)} %get-tuple-element.42), channel_id=1, source_target_pairs={{0,24},{4,28},{8,16},{12,20},{16,8},{20,12},{24,0},{28,4},{1,25},{... | collective-permute-start | bytes 608264 | tf_op jit(solution)/shard_map/ppermute | solution.py:483
  82.2 10.9 %collective-permute-start.18 = (f32[18,2,1408]{2,1,0:T(2,128)S(1)}, f32[18,2,1408]{2,1,0:T(2,128)S(1)}, u32[]{:S(2)}, u32[]{:S(2)}) collective-permute-start(f32[18,2,1408]{2,1,0:T(2,128)S(1)} %get-tuple-element.50), channel_id=1, source_target_pairs={{0,8},{4,12},{8,0},{12,4},{16,24},{20,28},{24,16},{28,20},{1,9},{5... | collective-permute-start | bytes 608264 | tf_op jit(solution)/shard_map/ppermute | solution.py:483
  83.7 15.9 %collective-permute-start.19 = (f32[18,2,1408]{2,1,0:T(2,128)S(1)}, f32[18,2,1408]{2,1,0:T(2,128)S(1)}, u32[]{:S(2)}, u32[]{:S(2)}) collective-permute-start(f32[18,2,1408]{2,1,0:T(2,128)S(1)} %get-tuple-element.51), channel_id=1, source_target_pairs={{0,16},{4,20},{8,24},{12,28},{16,0},{20,4},{24,8},{28,12},{1,17},{... | collective-permute-start | bytes 608264 | tf_op jit(solution)/shard_map/ppermute | solution.py:483
  84.3 15.2 %collective-permute-start.20 = (f32[18,2,1408]{2,1,0:T(2,128)S(1)}, f32[18,2,1408]{2,1,0:T(2,128)S(1)}, u32[]{:S(2)}, u32[]{:S(2)}) collective-permute-start(f32[18,2,1408]{2,1,0:T(2,128)S(1)} %get-tuple-element.52), channel_id=1, source_target_pairs={{0,24},{4,28},{8,16},{12,20},{16,8},{20,12},{24,0},{28,4},{1,25},{... | collective-permute-start | bytes 608264 | tf_op jit(solution)/shard_map/ppermute | solution.py:483

commit v9 on v8

--- a/solution.py
+++ b/solution.py
@@ -11,7 +11,7 @@
 NY = 72
 LANES = 128
 TILE = 256
-WINDOW = 3 * TILE
+WINDOW = 2 * TILE
 REACH = 2
 HALO = 4
 CHUNKS = 2
@@ -79,6 +79,7 @@
         self.n_first = ceil_to(high + used - reach - self.first, TILE) // TILE
         self.second = floor_to(low + 2 * reach, LANES)
         self.n_second = ceil_to(high + used - 2 * reach - self.second, TILE) // TILE
+        self.needed = [(low + n * reach, high + used - n * reach) for n in (1, 2)]
         self.out_starts = [floor_to(j * self.width, LANES) for j in range(chips)]
         self.out_length = max(
             ceil_to((j + 1) * self.width, LANES) - s for j, s in enumerate(self.out_starts)
@@ -94,13 +95,13 @@
 
     @property
     def pad(self):
-        return max(0, TILE - self.first)
+        return max(0, LANES - self.first)
 
     @property
     def split_length(self):
         ends = (
-            self.pad + self.first - TILE + self.n_first * TILE + WINDOW - TILE,
-            self.pad + self.second - TILE + self.n_second * TILE + WINDOW - TILE,
+            self.pad + self.first - LANES + (self.n_first - 1) * TILE + WINDOW,
+            self.pad + self.second - LANES + (self.n_second - 1) * TILE + WINDOW,
             self.pad + self.first + self.n_first * TILE,
             self.pad + self.length,
         )
@@ -229,7 +230,7 @@
     i = lax.broadcasted_iota(jnp.int32, (WINDOW, TILE), 0)
     lane = lax.broadcasted_iota(jnp.int32, (1, TILE), 1)
     shift = ranges.shift(chip_ref[0])
-    at = lane + TILE
+    at = lane + LANES
 
     def tile(t, start, diagonal):
         y = lax.rem(lane + (start + 2 * NY) - shift, NY)
@@ -300,13 +301,29 @@
     lax.fori_loop(0, depth // STEP, density, 0)
 
     def in_plane(source, planes, start, weight, product):
-        lanes = aligned(start - TILE + pad, WINDOW)
+        lanes = aligned(start - LANES + pad, WINDOW)
         rows = planes * n_rows
         value = source[:, :, REACH * n_rows : REACH * n_rows + rows, lanes]
         value = value.reshape(2 * kinds * rows, WINDOW)
         product[0 : 2 * kinds * rows] = jnp.dot(value, weight, preferred_element_type=jnp.float32)
 
-    def off(source, k, planes, start, product):
+    def edges(source, k, rows, start, needed):
+        reach = 2 * NY - LANES
+        lane = lax.broadcasted_iota(jnp.int32, (rows, LANES), 1)
+
+        def taken(at, shift, keep):
+            row = REACH * n_rows
+            value = source[k, row : row + rows, aligned(at, LANES)]
+            return jnp.where(keep, pltpu.roll(value, shift, 1), 0.0)
+
+        sides = [None, None]
+        if start + reach > needed[0]:
+            sides[0] = taken(start - 2 * LANES, reach, lane < reach)
+        if start + TILE - reach < needed[1]:
+            sides[1] = taken(start + TILE + LANES, LANES - reach, lane >= LANES - reach)
+        return sides
+
+    def off(source, k, planes, start, product, needed):
         rows = planes * n_rows
 
         def shifted(z):
@@ -314,6 +331,11 @@
 
         near = shifted(1) + shifted(3)
         far = shifted(0) + shifted(4)
+        halves = [far[:, :LANES], far[:, LANES:]]
+        for side, extra in enumerate(edges(source, k, rows, start, needed)):
+            if extra is not None:
+                halves[side] = halves[side] + extra
+        far = jnp.concatenate(halves, axis=1)
         row = 2 * k * rows
         inside = product[row : row + rows] + product[row + rows : row + 2 * rows]
         return inside + (16.0 * near - far)
@@ -331,7 +353,7 @@
     def use_1(t, product):
         start = ranges.first + t * TILE
         for k in range(kinds):
-            value = off(rho, k, swept, start, product)
+            value = off(rho, k, swept, start, product, ranges.needed[0])
             mid[k, :, aligned(start, TILE)] = value
             store_halves(mid_split.at[k], slice(None), aligned(start + pad, TILE), value)
 
@@ -346,7 +368,7 @@
         here = aligned(start, TILE)
         values = []
         for k in range(kinds):
-            value = off(mid, k, inner, start, product)
+            value = off(mid, k, inner, start, product, ranges.needed[1])
             source = rho[k, HALO * n_rows : (HALO + inner) * n_rows, here]
             value = value + (DIAGONAL * DIAGONAL) * source
             values.append(value.reshape(inner, n_rows, TILE))

time: 102 us -> 92.9 us (0.911)
  waiting for transfers between devices: 36.4 us -> 31 us
  Pallas kernels: 35.8 us -> 32.9 us
    ppermute x15, waiting for transfers between devices: 29.2 us -> 25.9 us  [exchange(): return lax.ppermute(value, 'band', pairs)]
    pallas_call x13, Pallas kernels: 35.8 us -> 32.9 us  [call(): pl.pallas_call(body, out_shape=out, in_specs=specs, out_specs=[VMEM] * le...]
    ppermute x1, waiting for transfers between devices: 1.68 us -> 0.01 us  [per_device(): above = lax.ppermute(planes[:HALO], 'slab', down)]
    ppermute x1, starting transfers between devices: 3.6 us -> 2.09 us  [per_device(): above = lax.ppermute(planes[:HALO], 'slab', down)]
    ppermute x15, starting transfers between devices: 21.2 us -> 22.3 us  [exchange(): return lax.ppermute(value, 'band', pairs)]
where the time goes in v9:
time: 92.9 us; the launch traced here: 92.8 us
  Pallas kernels  32.9 us (35%)
  waiting for transfers between devices  31 us (33%)
  starting transfers between devices  27.3 us (29%)
  local copies, waits for them, and re-layouts  1.41 us (2%)
    pallas_call x13, Pallas kernels, call(): pl.pallas_call(body, out_shape=out, in_specs=specs, out_specs=[VMEM] * le...  32.9 us
    ppermute x15, waiting for transfers between devices, exchange(): return lax.ppermute(value, 'band', pairs)  25.9 us
    ppermute x15, starting transfers between devices, exchange(): return lax.ppermute(value, 'band', pairs)  22.3 us
    ppermute x1, waiting for transfers between devices, per_device(): below = lax.ppermute(planes[depth - HALO:], 'slab', up)  5.08 us
    ppermute x1, starting transfers between devices, per_device(): above = lax.ppermute(planes[:HALO], 'slab', down)  2.09 us
    ppermute x1, starting transfers between devices, per_device(): below = lax.ppermute(planes[depth - HALO:], 'slab', up)  2.09 us
  transfers between devices with their start and end apart: 21, of which 8 were waited for; matrix products, arithmetic and copies ran while one was open for 0% of the time, Pallas kernels for 32%

profile of v9, /device:TPU:0, one launch (start us, length us, event | category | flops | bytes accessed | tf_op | source)
XLA Modules:
  0.0 92.8 jit_solution(4149594705796241682)
XLA Ops:
  0.1 1.4 %copy-done = f32[2,36,5184]{2,0,1:T(2,128)S(1)} copy-done((f32[2,36,5184]{2,0,1:T(2,128)S(1)}, f32[2,36,5184]{2,0,1:T(2,128)}, u32[]{:S(2)}) %copy-start) | copy-done | bytes 1493016
  1.5 1.6 %shard_map.18 = (f32[22,2,2048]{2,1,0:T(2,128)S(1)}, f32[22,2,2048]{2,1,0:T(2,128)S(1)}, f32[22,2,2048]{2,1,0:T(2,128)S(1)}, f32[22,2,2048]{2,1,0:T(2,128)S(1)}) custom-call(s32[2]{0:T(128)S(1)} %pad_add_fusion.chip_ref, f32[36,2,5184]{2,1,0:T(2,128)S(1)} %bitcast.4), custom_call_target="tpu_custom_call" | custom-call | bytes 2934792 | tf_op jit(solution)/shard_map/pallas_call | solution.py:35
  3.0 3.0 %collective-permute-start.4 = (f32[22,2,2048]{2,1,0:T(2,128)S(1)}, f32[22,2,2048]{2,1,0:T(2,128)S(1)}, u32[]{:S(2)}, u32[]{:S(2)}) collective-permute-start(f32[22,2,2048]{2,1,0:T(2,128)S(1)} %get-tuple-element.34), channel_id=1, source_target_pairs={{0,8},{4,12},{8,0},{12,4},{16,24},{20,28},{24,16},{28,20},{1,9},{5... | collective-permute-start | bytes 1081352 | tf_op jit(solution)/shard_map/ppermute | solution.py:505
  6.1 1.5 %collective-permute-start.5 = (f32[22,2,2048]{2,1,0:T(2,128)S(1)}, f32[22,2,2048]{2,1,0:T(2,128)S(1)}, u32[]{:S(2)}, u32[]{:S(2)}) collective-permute-start(f32[22,2,2048]{2,1,0:T(2,128)S(1)} %get-tuple-element.35), channel_id=1, source_target_pairs={{0,16},{4,20},{8,24},{12,28},{16,0},{20,4},{24,8},{28,12},{1,17},{... | collective-permute-start | bytes 1081352 | tf_op jit(solution)/shard_map/ppermute | solution.py:505
  7.6 2.1 %collective-permute-start = (f32[4,2,5184]{2,1,0:T(2,128)S(1)}, f32[4,2,5184]{2,1,0:T(2,128)S(1)}, u32[]{:S(2)}, u32[]{:S(2)}) collective-permute-start(f32[4,2,5184]{2,1,0:T(2,128)S(1)} %get-tuple-element.54), channel_id=1, source_target_pairs={{0,1},{1,2},{2,3},{3,0},{4,5},{5,6},{6,7},{7,4},{8,9},{9,10},{10,1... | collective-permute-start | bytes 497672 | tf_op jit(solution)/shard_map/ppermute | solution.py:513
  9.7 2.1 %collective-permute-start.12 = (f32[4,2,5184]{2,1,0:T(2,128)S(1)}, f32[4,2,5184]{2,1,0:T(2,128)S(1)}, u32[]{:S(2)}, u32[]{:S(2)}) collective-permute-start(f32[4,2,5184]{2,1,0:T(2,128)S(1)} %get-tuple-element.53), channel_id=1, source_target_pairs={{1,0},{2,1},{3,2},{0,3},{5,4},{6,5},{7,6},{4,7},{9,8},{10,9},{11,1... | collective-permute-start | bytes 497672 | tf_op jit(solution)/shard_map/ppermute | solution.py:514
  11.8 5.1 %collective-permute-done.refs_0_ = f32[4,2,5184]{2,1,0:T(2,128)S(1)} collective-permute-done((f32[4,2,5184]{2,1,0:T(2,128)S(1)}, f32[4,2,5184]{2,1,0:T(2,128)S(1)}, u32[]{:S(2)}, u32[]{:S(2)}) %collective-permute-start) | collective-permute-done | bytes 165920 | tf_op jit(solution)/shard_map/ppermute | solution.py:513
  17.6 1.7 %collective-permute-start.1 = (f32[4,2,2048]{2,1,0:T(2,128)S(1)}, f32[4,2,2048]{2,1,0:T(2,128)S(1)}, u32[]{:S(2)}, u32[]{:S(2)}) collective-permute-start(f32[4,2,2048]{2,1,0:T(2,128)S(1)} %get-tuple-element.30), channel_id=1, source_target_pairs={{0,8},{4,12},{8,0},{12,4},{16,24},{20,28},{24,16},{28,20},{1,9},{5... | collective-permute-start | bytes 196616 | tf_op jit(solution)/shard_map/ppermute | solution.py:505
  19.3 1.5 %collective-permute-start.2 = (f32[4,2,2048]{2,1,0:T(2,128)S(1)}, f32[4,2,2048]{2,1,0:T(2,128)S(1)}, u32[]{:S(2)}, u32[]{:S(2)}) collective-permute-start(f32[4,2,2048]{2,1,0:T(2,128)S(1)} %get-tuple-element.31), channel_id=1, source_target_pairs={{0,16},{4,20},{8,24},{12,28},{16,0},{20,4},{24,8},{28,12},{1,17},{... | collective-permute-start | bytes 196616 | tf_op jit(solution)/shard_map/ppermute | solution.py:505
  20.8 2.8 %collective-permute-done.1.refs_1_ = f32[4,2,2048]{2,1,0:T(2,128)S(1)} collective-permute-done((f32[4,2,2048]{2,1,0:T(2,128)S(1)}, f32[4,2,2048]{2,1,0:T(2,128)S(1)}, u32[]{:S(2)}, u32[]{:S(2)}) %collective-permute-start.1) | collective-permute-done | bytes 65568 | tf_op jit(solution)/shard_map/ppermute | solution.py:505
  23.6 2.7 %collective-permute-start.3 = (f32[4,2,2048]{2,1,0:T(2,128)S(1)}, f32[4,2,2048]{2,1,0:T(2,128)S(1)}, u32[]{:S(2)}, u32[]{:S(2)}) collective-permute-start(f32[4,2,2048]{2,1,0:T(2,128)S(1)} %get-tuple-element.32), channel_id=1, source_target_pairs={{0,24},{4,28},{8,16},{12,20},{16,8},{20,12},{24,0},{28,4},{1,25},{... | collective-permute-start | bytes 196616 | tf_op jit(solution)/shard_map/ppermute | solution.py:505
  26.3 1.4 %shard_map.24 = (f32[18,2,2048]{2,1,0:T(2,128)S(1)}, f32[18,2,2048]{2,1,0:T(2,128)S(1)}, f32[18,2,2048]{2,1,0:T(2,128)S(1)}, f32[18,2,2048]{2,1,0:T(2,128)S(1)}) custom-call(s32[2]{0:T(128)S(1)} %pad_add_fusion.chip_ref, f32[36,2,5184]{2,1,0:T(2,128)S(1)} %bitcast.6, f32[4,2,5184]{2,1,0:T(2,128)S(1)} %collective-permute-done.12.refs_1_), custom_call_target="tpu_custom_call" | custom-call | bytes 2838536 | tf_op jit(solution)/shard_map/pallas_call | solution.py:35
  28.8 1.8 %collective-permute-start.14 = (f32[18,2,2048]{2,1,0:T(2,128)S(1)}, f32[18,2,2048]{2,1,0:T(2,128)S(1)}, u32[]{:S(2)}, u32[]{:S(2)}) collective-permute-start(f32[18,2,2048]{2,1,0:T(2,128)S(1)} %get-tuple-element.45), channel_id=1, source_target_pairs={{0,16},{4,20},{8,24},{12,28},{16,0},{20,4},{24,8},{28,12},{1,17},{... | collective-permute-start | bytes 884744 | tf_op jit(solution)/shard_map/ppermute | solution.py:505
  30.6 2.1 %collective-permute-start.15 = (f32[18,2,2048]{2,1,0:T(2,128)S(1)}, f32[18,2,2048]{2,1,0:T(2,128)S(1)}, u32[]{:S(2)}, u32[]{:S(2)}) collective-permute-start(f32[18,2,2048]{2,1,0:T(2,128)S(1)} %get-tuple-element.46), channel_id=1, source_target_pairs={{0,24},{4,28},{8,16},{12,20},{16,8},{20,12},{24,0},{28,4},{1,25},{... | collective-permute-start | bytes 884744 | tf_op jit(solution)/shard_map/ppermute | solution.py:505
  32.7 1.1 %shard_map.19.planes.refs_0_ = f32[26,8,2048]{2,1,0:T(8,128)S(1)} custom-call(s32[2]{0:T(128)S(1)} %pad_add_fusion.chip_ref, f32[4,2,2048]{2,1,0:T(2,128)S(1)} %get-tuple-element.29.refs_0_, f32[4,2,2048]{2,1,0:T(2,128)S(1)} %collective-permute-done.1.refs_1_, f32[4,2,2048]{2,1,0:T(2,128)S(1)} %collective-permute-done.2.refs_2_, ...), custom_call_target="tpu_custom_call" | custom-call | bytes 3407880 | tf_op jit(solution)/shard_map/pallas_call | solution.py:35
  33.9 3.8 %collective-permute-done.13.refs_2_ = f32[18,2,2048]{2,1,0:T(2,128)S(1)} collective-permute-done((f32[18,2,2048]{2,1,0:T(2,128)S(1)}, f32[18,2,2048]{2,1,0:T(2,128)S(1)}, u32[]{:S(2)}, u32[]{:S(2)}) %collective-permute-start.13) | collective-permute-done | bytes 294944 | tf_op jit(solution)/shard_map/ppermute | solution.py:505
  37.7 4.5 %collective-permute-done.14.refs_3_ = f32[18,2,2048]{2,1,0:T(2,128)S(1)} collective-permute-done((f32[18,2,2048]{2,1,0:T(2,128)S(1)}, f32[18,2,2048]{2,1,0:T(2,128)S(1)}, u32[]{:S(2)}, u32[]{:S(2)}) %collective-permute-start.14) | collective-permute-done | bytes 294944 | tf_op jit(solution)/shard_map/ppermute | solution.py:505
  42.2 1.1 %shard_map.25.planes = f32[26,8,2048]{2,1,0:T(8,128)S(1)} custom-call(s32[2]{0:T(128)S(1)} %pad_add_fusion.chip_ref, f32[26,8,2048]{2,1,0:T(8,128)S(1)} %shard_map.19.planes.refs_0_, f32[18,2,2048]{2,1,0:T(2,128)S(1)} %get-tuple-element.43.refs_1_, f32[18,2,2048]{2,1,0:T(2,128)S(1)} %collective-permute-done.13.refs_2_, ...), custom_call_target="tpu_custom_call" | custom-call | bytes 4587528 | tf_op jit(solution)/shard_map/pallas_call | solution.py:35
  43.4 3.9 %shard_map.20.w_ref = bf16[13,512,256]{2,1,0:T(8,128)(2,1)S(1)} custom-call(s32[2]{0:T(128)S(1)} %pad_add_fusion.chip_ref), custom_call_target="tpu_custom_call" | custom-call | bytes 6815752 | tf_op jit(solution)/shard_map/pallas_call | solution.py:35
  47.3 4.4 %shard_map.21.refs_0_ = f32[18,8,1536]{2,1,0:T(8,128)S(1)} custom-call(f32[26,8,2048]{2,1,0:T(8,128)S(1)} %shard_map.19.planes.refs_0_, bf16[13,512,256]{2,1,0:T(8,128)(2,1)S(1)} %shard_map.20.w_ref), custom_call_target="tpu_custom_call" | custom-call | flops 2835349504 | bytes 9404416 | tf_op jit(solution)/shard_map/pallas_call | solution.py:35
  51.8 5.3 %shard_map.22 = (f32[18,8,1536]{2,1,0:T(8,128)S(1)}, f32[18,8,1536]{2,1,0:T(8,128)S(1)}) custom-call(s32[2]{0:T(128)S(1)} %pad_add_fusion.chip_ref, f32[26,8,2048]{2,1,0:T(8,128)S(1)} %shard_map.19.planes.refs_0_, bf16[13,512,256]{2,1,0:T(8,128)(2,1)S(1)} %shard_map.20.w_ref, f32[26,8,2048]{2,1,0:T(8,128)S(1)} %collective-permute-done.7.other, ...), custom_call_target="tpu_custom_call" | custom-call | flops 2835349504 | bytes 12877832 | tf_op jit(solution)/shard_map/pallas_call | solution.py:35
  57.6 5.2 %shard_map.26 = (f32[18,8,1536]{2,1,0:T(8,128)S(1)}, f32[18,8,1536]{2,1,0:T(8,128)S(1)}) custom-call(s32[2]{0:T(128)S(1)} %pad_add_fusion.chip_ref, f32[26,8,2048]{2,1,0:T(8,128)S(1)} %shard_map.25.planes, bf16[13,512,256]{2,1,0:T(8,128)(2,1)S(1)} %shard_map.20.w_ref, f32[26,8,2048]{2,1,0:T(8,128)S(1)} %collective-permute-done.16.other), custom_call_target="tpu_custom_call" | custom-call | flops 2835349504 | bytes 11993096 | tf_op jit(solution)/shard_map/pallas_call | solution.py:35
  62.9 1.0 %shard_map.23 = (f32[18,2,1408]{2,1,0:T(2,128)S(1)}, f32[18,2,1408]{2,1,0:T(2,128)S(1)}, f32[18,2,1408]{2,1,0:T(2,128)S(1)}, f32[18,2,1408]{2,1,0:T(2,128)S(1)}) custom-call(s32[2]{0:T(128)S(1)} %pad_add_fusion.chip_ref, f32[18,8,1536]{2,1,0:T(8,128)S(1)} %get-tuple-element.37.mine, f32[18,8,1536]{2,1,0:T(8,128)S(1)} %collective-permute-done.8.theirs), custom_call_target="tpu_custom_call" | custom-call | bytes 2580488 | tf_op jit(solution)/shard_map/pallas_call | solution.py:35
  63.9 2.2 %collective-permute-start.9 = (f32[18,2,1408]{2,1,0:T(2,128)S(1)}, f32[18,2,1408]{2,1,0:T(2,128)S(1)}, u32[]{:S(2)}, u32[]{:S(2)}) collective-permute-start(f32[18,2,1408]{2,1,0:T(2,128)S(1)} %get-tuple-element.40), channel_id=1, source_target_pairs={{0,8},{4,12},{8,0},{12,4},{16,24},{20,28},{24,16},{28,20},{1,9},{5... | collective-permute-start | bytes 608264 | tf_op jit(solution)/shard_map/ppermute | solution.py:505
  66.1 4.5 %shard_map.27.mine = f32[18,8,1536]{2,1,0:T(8,128)S(1)} custom-call(f32[26,8,2048]{2,1,0:T(8,128)S(1)} %shard_map.25.planes, bf16[13,512,256]{2,1,0:T(8,128)(2,1)S(1)} %shard_map.20.w_ref, f32[18,8,1536]{2,1,0:T(8,128)S(1)} %get-tuple-element.47.refs_0_), custom_call_target="tpu_custom_call" | custom-call | flops 2835349504 | bytes 10289152 | tf_op jit(solution)/shard_map/pallas_call | solution.py:35
  70.6 1.6 %collective-permute-start.10 = (f32[18,2,1408]{2,1,0:T(2,128)S(1)}, f32[18,2,1408]{2,1,0:T(2,128)S(1)}, u32[]{:S(2)}, u32[]{:S(2)}) collective-permute-start(f32[18,2,1408]{2,1,0:T(2,128)S(1)} %get-tuple-element.41), channel_id=1, source_target_pairs={{0,16},{4,20},{8,24},{12,28},{16,0},{20,4},{24,8},{28,12},{1,17},{... | collective-permute-start | bytes 608264 | tf_op jit(solution)/shard_map/ppermute | solution.py:505
  72.9 2.0 %collective-permute-start.18 = (f32[18,2,1408]{2,1,0:T(2,128)S(1)}, f32[18,2,1408]{2,1,0:T(2,128)S(1)}, u32[]{:S(2)}, u32[]{:S(2)}) collective-permute-start(f32[18,2,1408]{2,1,0:T(2,128)S(1)} %get-tuple-element.50), channel_id=1, source_target_pairs={{0,8},{4,12},{8,0},{12,4},{16,24},{20,28},{24,16},{28,20},{1,9},{5... | collective-permute-start | bytes 608264 | tf_op jit(solution)/shard_map/ppermute | solution.py:505
  75.0 1.5 %collective-permute-start.19 = (f32[18,2,1408]{2,1,0:T(2,128)S(1)}, f32[18,2,1408]{2,1,0:T(2,128)S(1)}, u32[]{:S(2)}, u32[]{:S(2)}) collective-permute-start(f32[18,2,1408]{2,1,0:T(2,128)S(1)} %get-tuple-element.51), channel_id=1, source_target_pairs={{0,16},{4,20},{8,24},{12,28},{16,0},{20,4},{24,8},{28,12},{1,17},{... | collective-permute-start | bytes 608264 | tf_op jit(solution)/shard_map/ppermute | solution.py:505
  76.5 6.4 %collective-permute-done.10.refs_2_ = f32[18,2,1408]{2,1,0:T(2,128)S(1)} collective-permute-done((f32[18,2,1408]{2,1,0:T(2,128)S(1)}, f32[18,2,1408]{2,1,0:T(2,128)S(1)}, u32[]{:S(2)}, u32[]{:S(2)}) %collective-permute-start.10) | collective-permute-done | bytes 202784 | tf_op jit(solution)/shard_map/ppermute | solution.py:505
  82.9 1.5 %collective-permute-done.18.refs_5_ = f32[18,2,1408]{2,1,0:T(2,128)S(1)} collective-permute-done((f32[18,2,1408]{2,1,0:T(2,128)S(1)}, f32[18,2,1408]{2,1,0:T(2,128)S(1)}, u32[]{:S(2)}, u32[]{:S(2)}) %collective-permute-start.18) | collective-permute-done | bytes 202784 | tf_op jit(solution)/shard_map/ppermute | solution.py:505
  84.4 6.5 %collective-permute-done.19.refs_6_ = f32[18,2,1408]{2,1,0:T(2,128)S(1)} collective-permute-done((f32[18,2,1408]{2,1,0:T(2,128)S(1)}, f32[18,2,1408]{2,1,0:T(2,128)S(1)}, u32[]{:S(2)}, u32[]{:S(2)}) %collective-permute-start.19) | collective-permute-done | bytes 202784 | tf_op jit(solution)/shard_map/ppermute | solution.py:505
  90.8 2.0 %shard_map.29 = f32[36,2,5184]{2,1,0:T(2,128)} custom-call(s32[2]{0:T(128)S(1)} %pad_add_fusion.chip_ref, f32[18,2,1408]{2,1,0:T(2,128)S(1)} %get-tuple-element.39.refs_0_, f32[18,2,1408]{2,1,0:T(2,128)S(1)} %collective-permute-done.9.refs_1_, f32[18,2,1408]{2,1,0:T(2,128)S(1)} %collective-permute-done.10.refs_2_, ...), custom_call_target="tpu_custom_call" | custom-call | bytes 3115016 | tf_op jit(solution)/shard_map/pallas_call | solution.py:35
  (29 shorter events, 3.5 us)
Async XLA Ops:
  0.1 1.4 %copy-start = (f32[2,36,5184]{2,0,1:T(2,128)S(1)}, f32[2,36,5184]{2,0,1:T(2,128)}, u32[]{:S(2)}) copy-start(f32[2,36,5184]{2,0,1:T(2,128)} %param.1) | copy-start | bytes 4478980
  1.5 6.1 %copy-start.1 = (f32[2,36,5184]{2,0,1:T(2,128)S(1)}, f32[2,36,5184]{2,0,1:T(2,128)}, u32[]{:S(2)}) copy-start(f32[2,36,5184]{2,0,1:T(2,128)} %param.1) | copy-start | bytes 4478980
  3.0 27.6 %collective-permute-start.4 = (f32[22,2,2048]{2,1,0:T(2,128)S(1)}, f32[22,2,2048]{2,1,0:T(2,128)S(1)}, u32[]{:S(2)}, u32[]{:S(2)}) collective-permute-start(f32[22,2,2048]{2,1,0:T(2,128)S(1)} %get-tuple-element.34), channel_id=1, source_target_pairs={{0,8},{4,12},{8,0},{12,4},{16,24},{20,28},{24,16},{28,20},{1,9},{5... | collective-permute-start | bytes 1081352 | tf_op jit(solution)/shard_map/ppermute | solution.py:505
  6.1 26.7 %collective-permute-start.5 = (f32[22,2,2048]{2,1,0:T(2,128)S(1)}, f32[22,2,2048]{2,1,0:T(2,128)S(1)}, u32[]{:S(2)}, u32[]{:S(2)}) collective-permute-start(f32[22,2,2048]{2,1,0:T(2,128)S(1)} %get-tuple-element.35), channel_id=1, source_target_pairs={{0,16},{4,20},{8,24},{12,28},{16,0},{20,4},{24,8},{28,12},{1,17},{... | collective-permute-start | bytes 1081352 | tf_op jit(solution)/shard_map/ppermute | solution.py:505
  7.6 25.1 %collective-permute-start.6 = (f32[22,2,2048]{2,1,0:T(2,128)S(1)}, f32[22,2,2048]{2,1,0:T(2,128)S(1)}, u32[]{:S(2)}, u32[]{:S(2)}) collective-permute-start(f32[22,2,2048]{2,1,0:T(2,128)S(1)} %get-tuple-element.36), channel_id=1, source_target_pairs={{0,24},{4,28},{8,16},{12,20},{16,8},{20,12},{24,0},{28,4},{1,25},{... | collective-permute-start | bytes 1081352 | tf_op jit(solution)/shard_map/ppermute | solution.py:505
  7.6 9.3 %collective-permute-start = (f32[4,2,5184]{2,1,0:T(2,128)S(1)}, f32[4,2,5184]{2,1,0:T(2,128)S(1)}, u32[]{:S(2)}, u32[]{:S(2)}) collective-permute-start(f32[4,2,5184]{2,1,0:T(2,128)S(1)} %get-tuple-element.54), channel_id=1, source_target_pairs={{0,1},{1,2},{2,3},{3,0},{4,5},{5,6},{6,7},{7,4},{8,9},{9,10},{10,1... | collective-permute-start | bytes 497672 | tf_op jit(solution)/shard_map/ppermute | solution.py:513
  9.7 9.6 %collective-permute-start.12 = (f32[4,2,5184]{2,1,0:T(2,128)S(1)}, f32[4,2,5184]{2,1,0:T(2,128)S(1)}, u32[]{:S(2)}, u32[]{:S(2)}) collective-permute-start(f32[4,2,5184]{2,1,0:T(2,128)S(1)} %get-tuple-element.53), channel_id=1, source_target_pairs={{1,0},{2,1},{3,2},{0,3},{5,4},{6,5},{7,6},{4,7},{9,8},{10,9},{11,1... | collective-permute-start | bytes 497672 | tf_op jit(solution)/shard_map/ppermute | solution.py:514
  17.6 6.0 %collective-permute-start.1 = (f32[4,2,2048]{2,1,0:T(2,128)S(1)}, f32[4,2,2048]{2,1,0:T(2,128)S(1)}, u32[]{:S(2)}, u32[]{:S(2)}) collective-permute-start(f32[4,2,2048]{2,1,0:T(2,128)S(1)} %get-tuple-element.30), channel_id=1, source_target_pairs={{0,8},{4,12},{8,0},{12,4},{16,24},{20,28},{24,16},{28,20},{1,9},{5... | collective-permute-start | bytes 196616 | tf_op jit(solution)/shard_map/ppermute | solution.py:505
  19.3 8.4 %collective-permute-start.2 = (f32[4,2,2048]{2,1,0:T(2,128)S(1)}, f32[4,2,2048]{2,1,0:T(2,128)S(1)}, u32[]{:S(2)}, u32[]{:S(2)}) collective-permute-start(f32[4,2,2048]{2,1,0:T(2,128)S(1)} %get-tuple-element.31), channel_id=1, source_target_pairs={{0,16},{4,20},{8,24},{12,28},{16,0},{20,4},{24,8},{28,12},{1,17},{... | collective-permute-start | bytes 196616 | tf_op jit(solution)/shard_map/ppermute | solution.py:505
  23.6 5.2 %collective-permute-start.3 = (f32[4,2,2048]{2,1,0:T(2,128)S(1)}, f32[4,2,2048]{2,1,0:T(2,128)S(1)}, u32[]{:S(2)}, u32[]{:S(2)}) collective-permute-start(f32[4,2,2048]{2,1,0:T(2,128)S(1)} %get-tuple-element.32), channel_id=1, source_target_pairs={{0,24},{4,28},{8,16},{12,20},{16,8},{20,12},{24,0},{28,4},{1,25},{... | collective-permute-start | bytes 196616 | tf_op jit(solution)/shard_map/ppermute | solution.py:505
  27.7 9.9 %collective-permute-start.13 = (f32[18,2,2048]{2,1,0:T(2,128)S(1)}, f32[18,2,2048]{2,1,0:T(2,128)S(1)}, u32[]{:S(2)}, u32[]{:S(2)}) collective-permute-start(f32[18,2,2048]{2,1,0:T(2,128)S(1)} %get-tuple-element.44), channel_id=1, source_target_pairs={{0,8},{4,12},{8,0},{12,4},{16,24},{20,28},{24,16},{28,20},{1,9},{5... | collective-permute-start | bytes 884744 | tf_op jit(solution)/shard_map/ppermute | solution.py:505
  28.8 13.3 %collective-permute-start.14 = (f32[18,2,2048]{2,1,0:T(2,128)S(1)}, f32[18,2,2048]{2,1,0:T(2,128)S(1)}, u32[]{:S(2)}, u32[]{:S(2)}) collective-permute-start(f32[18,2,2048]{2,1,0:T(2,128)S(1)} %get-tuple-element.45), channel_id=1, source_target_pairs={{0,16},{4,20},{8,24},{12,28},{16,0},{20,4},{24,8},{28,12},{1,17},{... | collective-permute-start | bytes 884744 | tf_op jit(solution)/shard_map/ppermute | solution.py:505
  30.6 11.5 %collective-permute-start.15 = (f32[18,2,2048]{2,1,0:T(2,128)S(1)}, f32[18,2,2048]{2,1,0:T(2,128)S(1)}, u32[]{:S(2)}, u32[]{:S(2)}) collective-permute-start(f32[18,2,2048]{2,1,0:T(2,128)S(1)} %get-tuple-element.46), channel_id=1, source_target_pairs={{0,24},{4,28},{8,16},{12,20},{16,8},{20,12},{24,0},{28,4},{1,25},{... | collective-permute-start | bytes 884744 | tf_op jit(solution)/shard_map/ppermute | solution.py:505
  33.8 17.9 %collective-permute-start.7 = (f32[26,8,2048]{2,1,0:T(8,128)S(1)}, f32[26,8,2048]{2,1,0:T(8,128)S(1)}, u32[]{:S(2)}, u32[]{:S(2)}) collective-permute-start(f32[26,8,2048]{2,1,0:T(8,128)S(1)} %shard_map.19.planes.refs_0_), channel_id=1, source_target_pairs={{0,4},{4,0},{8,12},{12,8},{16,20},{20,16},{24,28},{28,24},{1,5},{5... | collective-permute-start | bytes 5111816 | tf_op jit(solution)/shard_map/ppermute | solution.py:508
  43.3 14.3 %collective-permute-start.16 = (f32[26,8,2048]{2,1,0:T(8,128)S(1)}, f32[26,8,2048]{2,1,0:T(8,128)S(1)}, u32[]{:S(2)}, u32[]{:S(2)}) collective-permute-start(f32[26,8,2048]{2,1,0:T(8,128)S(1)} %shard_map.25.planes), channel_id=1, source_target_pairs={{0,4},{4,0},{8,12},{12,8},{16,20},{20,16},{24,28},{28,24},{1,5},{5... | collective-permute-start | bytes 5111816 | tf_op jit(solution)/shard_map/ppermute | solution.py:508
  57.0 5.8 %collective-permute-start.8 = (f32[18,8,1536]{2,1,0:T(8,128)S(1)}, f32[18,8,1536]{2,1,0:T(8,128)S(1)}, u32[]{:S(2)}, u32[]{:S(2)}) collective-permute-start(f32[18,8,1536]{2,1,0:T(8,128)S(1)} %get-tuple-element.38), channel_id=1, source_target_pairs={{0,4},{4,0},{8,12},{12,8},{16,20},{20,16},{24,28},{28,24},{1,5},{5... | collective-permute-start | bytes 2654216 | tf_op jit(solution)/shard_map/ppermute | solution.py:508
  62.8 9.4 %collective-permute-start.17 = (f32[18,8,1536]{2,1,0:T(8,128)S(1)}, f32[18,8,1536]{2,1,0:T(8,128)S(1)}, u32[]{:S(2)}, u32[]{:S(2)}) collective-permute-start(f32[18,8,1536]{2,1,0:T(8,128)S(1)} %get-tuple-element.48), channel_id=1, source_target_pairs={{0,4},{4,0},{8,12},{12,8},{16,20},{20,16},{24,28},{28,24},{1,5},{5... | collective-permute-start | bytes 2654216 | tf_op jit(solution)/shard_map/ppermute | solution.py:508
  63.9 12.6 %collective-permute-start.9 = (f32[18,2,1408]{2,1,0:T(2,128)S(1)}, f32[18,2,1408]{2,1,0:T(2,128)S(1)}, u32[]{:S(2)}, u32[]{:S(2)}) collective-permute-start(f32[18,2,1408]{2,1,0:T(2,128)S(1)} %get-tuple-element.40), channel_id=1, source_target_pairs={{0,8},{4,12},{8,0},{12,4},{16,24},{20,28},{24,16},{28,20},{1,9},{5... | collective-permute-start | bytes 608264 | tf_op jit(solution)/shard_map/ppermute | solution.py:505
  70.6 12.3 %collective-permute-start.10 = (f32[18,2,1408]{2,1,0:T(2,128)S(1)}, f32[18,2,1408]{2,1,0:T(2,128)S(1)}, u32[]{:S(2)}, u32[]{:S(2)}) collective-permute-start(f32[18,2,1408]{2,1,0:T(2,128)S(1)} %get-tuple-element.41), channel_id=1, source_target_pairs={{0,16},{4,20},{8,24},{12,28},{16,0},{20,4},{24,8},{28,12},{1,17},{... | collective-permute-start | bytes 608264 | tf_op jit(solution)/shard_map/ppermute | solution.py:505
  72.2 10.7 %collective-permute-start.11 = (f32[18,2,1408]{2,1,0:T(2,128)S(1)}, f32[18,2,1408]{2,1,0:T(2,128)S(1)}, u32[]{:S(2)}, u32[]{:S(2)}) collective-permute-start(f32[18,2,1408]{2,1,0:T(2,128)S(1)} %get-tuple-element.42), channel_id=1, source_target_pairs={{0,24},{4,28},{8,16},{12,20},{16,8},{20,12},{24,0},{28,4},{1,25},{... | collective-permute-start | bytes 608264 | tf_op jit(solution)/shard_map/ppermute | solution.py:505
  72.9 11.4 %collective-permute-start.18 = (f32[18,2,1408]{2,1,0:T(2,128)S(1)}, f32[18,2,1408]{2,1,0:T(2,128)S(1)}, u32[]{:S(2)}, u32[]{:S(2)}) collective-permute-start(f32[18,2,1408]{2,1,0:T(2,128)S(1)} %get-tuple-element.50), channel_id=1, source_target_pairs={{0,8},{4,12},{8,0},{12,4},{16,24},{20,28},{24,16},{28,20},{1,9},{5... | collective-permute-start | bytes 608264 | tf_op jit(solution)/shard_map/ppermute | solution.py:505
  75.0 15.9 %collective-permute-start.19 = (f32[18,2,1408]{2,1,0:T(2,128)S(1)}, f32[18,2,1408]{2,1,0:T(2,128)S(1)}, u32[]{:S(2)}, u32[]{:S(2)}) collective-permute-start(f32[18,2,1408]{2,1,0:T(2,128)S(1)} %get-tuple-element.51), channel_id=1, source_target_pairs={{0,16},{4,20},{8,24},{12,28},{16,0},{20,4},{24,8},{28,12},{1,17},{... | collective-permute-start | bytes 608264 | tf_op jit(solution)/shard_map/ppermute | solution.py:505
  76.5 14.4 %collective-permute-start.20 = (f32[18,2,1408]{2,1,0:T(2,128)S(1)}, f32[18,2,1408]{2,1,0:T(2,128)S(1)}, u32[]{:S(2)}, u32[]{:S(2)}) collective-permute-start(f32[18,2,1408]{2,1,0:T(2,128)S(1)} %get-tuple-element.52), channel_id=1, source_target_pairs={{0,24},{4,28},{8,16},{12,20},{16,8},{20,12},{24,0},{28,4},{1,25},{... | collective-permute-start | bytes 608264 | tf_op jit(solution)/shard_map/ppermute | solution.py:505
